TPU v7x, 32 devices: a whole 2x2x4 slice. The times are simulated.
32 devices in a mesh: expert: 4 (over x, core), fsdp: 8 (over z, y).
Axes of the slice: x: 2, y: 2, z: 4, core: 2. Of those that a mesh axis runs over, the one named last changes fastest.
Arguments:
- inputs: bfloat16 [12288, 1024], P(('expert', 'fsdp')), may hold values from -6 to 6
- w_qkv: bfloat16 [1024, 3072], P(('expert', 'fsdp')), may hold values from -0.1875 to 0.1875
- w_out: bfloat16 [1024, 1024], P(('expert', 'fsdp')), may hold values from -3 to 3
- attn_gain: bfloat16 [1024], P(('expert', 'fsdp')), may hold values from 0.5 to 1.5
- moe_gain: bfloat16 [1024], P(('expert', 'fsdp')), may hold values from 0.5 to 1.5
- w_router: bfloat16 [1024, 4], P(('expert', 'fsdp')), may hold values from -0.125 to 0.125
- bias_table: bfloat16 [512], P(('expert', 'fsdp')), may hold values from -4 to 4
- w_gate: bfloat16 [4, 1024, 2816], P('expert', None, 'fsdp'), may hold values from -0.1875 to 0.1875
- w_up: bfloat16 [4, 1024, 2816], P('expert', None, 'fsdp'), may hold values from -0.1875 to 0.1875
- w_down: bfloat16 [4, 2816, 1024], P('expert', 'fsdp'), may hold values from -0.15625 to 0.15625
- routes: int32 [12288, 2], P(('expert', 'fsdp')), may hold values from 0 to 3, as said below
- slot_order: int32 [12288, 2], P(('expert', 'fsdp')), may hold values from 0 to 240, as said below
- group_map: int32 [32], P(('expert', 'fsdp')), may hold values from 0 to 1, as said below
- buckets: int32 [1152], replicated, may hold values from 0 to 31, as said below
- grad_output: bfloat16 [12288, 1024], P(('expert', 'fsdp')), may hold values from -6 to 6
Outputs:
- output: bfloat16 [12288, 1024], P(('expert', 'fsdp'))
- router_losses: float32 [32, 2], P(('expert', 'fsdp'))
- grad_inputs: float32 [12288, 1024], P(('expert', 'fsdp'))
- grad_w_qkv: float32 [1024, 3072], P(('expert', 'fsdp'))
- grad_w_out: float32 [1024, 1024], P(('expert', 'fsdp'))
- grad_attn_gain: float32 [1024], P(('expert', 'fsdp'))
- grad_moe_gain: float32 [1024], P(('expert', 'fsdp'))
- grad_w_router: float32 [1024, 4], P(('expert', 'fsdp'))
- grad_bias_table: float32 [512], P(('expert', 'fsdp'))
- grad_w_gate: float32 [4, 1024, 2816], P('expert', None, 'fsdp')
- grad_w_up: float32 [4, 1024, 2816], P('expert', None, 'fsdp')
- grad_w_down: float32 [4, 2816, 1024], P('expert', 'fsdp')
Inputs may be any that keep to these rules, and one draw needn't show every extreme that they name: `routes`: the two experts of a token differ. `slot_order`: within one routing group the choices that name one expert hold the distinct slots 0, 1, 2 and so on up to 239, and every further choice holds 240 and is dropped; in every draw one expert is named by more than 240 choices in every routing group. `group_map`: within a line each of its 2 prompts is named by exactly 4 continuations. `buckets`: non-decreasing in the distance, 0 at distance 0, every bucket used.
All inputs are finite; a program needn't handle non-finite values.
Results may differ from a plain program's by a relative error of at most 0.015.
Values may be sent and summed in bfloat16 or wider, within the bound.
A program may use at most 320 MiB of HBM per device.

v0:
```python
import jax
import jax.numpy as jnp
from jax import lax
from jax.sharding import PartitionSpec as P

D = 1024
HEADS = 16
HDIM = 64
BUCKETS = 32
TOPK = 2
PLEN = 1024
CLEN = 128
G_LINE = 2
CONT_DEV = 1


EPSILON = 1e-06
ZLOSS_FACTOR = 0.001
BALANCE_FACTOR = 0.01
MASK_VALUE = -1e30
HIGHEST = lax.Precision.HIGHEST


def rms_scale(values, scale_row):
    inverse = lax.rsqrt(jnp.mean(values * values, axis=-1, keepdims=True) + EPSILON)
    return values * inverse * scale_row


def gated_unit(gate_pre, up_pre):
    return jax.nn.gelu(gate_pre, approximate=True) * up_pre


def activation_grads(gate_pre, up_pre, grad_hidden):
    activated, act_pull = jax.vjp(gated_unit, gate_pre, up_pre)
    grad_gate_pre, grad_up_pre = act_pull(grad_hidden)
    return (grad_gate_pre.astype(jnp.bfloat16), grad_up_pre.astype(jnp.bfloat16))


def route_local(normed, router, routes):
    logits = jnp.dot(normed, router, precision=HIGHEST)
    log_total = jax.nn.logsumexp(logits, axis=-1)
    chances = jnp.exp(logits - log_total[:, None])
    expert_ids = jnp.arange(router.shape[1], dtype=jnp.int32)
    first_hot = (routes[:, 0:1] == expert_ids[None, :]).astype(jnp.float32)
    second_hot = (routes[:, 1:2] == expert_ids[None, :]).astype(jnp.float32)
    first_chance = jnp.sum(chances * first_hot, axis=-1)
    second_chance = jnp.sum(chances * second_hot, axis=-1)
    both_chances = first_chance + second_chance
    gate_pair = jnp.stack([first_chance / both_chances, second_chance / both_chances], -1)
    z_loss = jnp.mean(log_total * log_total)
    expert_share = jnp.sum(first_hot + second_hot, axis=0) / (TOPK * routes.shape[0])
    balance = router.shape[1] * jnp.sum(expert_share * jnp.mean(chances, axis=0))
    return (gate_pair, jnp.stack([z_loss, balance]))


def head_scores(queries, key_value, bias_grid, allowed):
    length, batch_count = (key_value.shape[0], key_value.shape[1])
    shaped = key_value.reshape(length, batch_count, 2, HEADS, HDIM)
    scores = (
        jnp.einsum("qbhd,kbhd->bhqk", queries, shaped[:, :, 0], preferred_element_type=jnp.float32)
        * HDIM ** (-0.5)
        + bias_grid
    )
    return (jnp.where(allowed, scores, MASK_VALUE), shaped)


def attend_forward(queries, key_value, bias_grid, allowed):
    scores, shaped = head_scores(queries, key_value, bias_grid, allowed)
    row_peak = jnp.max(scores, axis=-1, keepdims=True)
    log_total = row_peak + jnp.log(jnp.sum(jnp.exp(scores - row_peak), axis=-1, keepdims=True))
    weights = jnp.exp(scores - log_total).astype(jnp.bfloat16)
    result = jnp.einsum(
        "bhqk,kbhd->qbhd", weights, shaped[:, :, 1], preferred_element_type=jnp.float32
    )
    return (result, log_total)


def attend_backward(queries, key_value, bias_grid, allowed, log_total, grad_result):
    scores, shaped = head_scores(queries, key_value, bias_grid, allowed)
    length, batch_count = (key_value.shape[0], key_value.shape[1])
    chances = jnp.exp(scores - log_total)
    weights = chances.astype(jnp.bfloat16)
    grad_weights = jnp.einsum(
        "qbhd,kbhd->bhqk", grad_result, shaped[:, :, 1], preferred_element_type=jnp.float32
    )
    inner = jnp.sum(chances * grad_weights, axis=-1, keepdims=True)
    grad_scores = (chances * (grad_weights - inner)).astype(jnp.bfloat16)
    grad_queries = jnp.einsum(
        "bhqk,kbhd->qbhd", grad_scores, shaped[:, :, 0], preferred_element_type=jnp.float32
    ) * HDIM ** (-0.5)
    grad_keys = jnp.einsum(
        "bhqk,qbhd->kbhd", grad_scores, queries, preferred_element_type=jnp.float32
    ) * HDIM ** (-0.5)
    grad_values = jnp.einsum(
        "bhqk,qbhd->kbhd", weights, grad_result, preferred_element_type=jnp.float32
    )
    grad_pairs = jnp.stack([grad_keys, grad_values], 2).reshape(length, batch_count, 2 * D)
    grad_bias = jnp.sum(grad_scores.astype(jnp.float32), axis=0)
    return (grad_queries, grad_pairs, grad_bias)


def local(
    inputs,
    w_qkv,
    w_out,
    attn_gain,
    moe_gain,
    w_router,
    bias_table,
    w_gate,
    w_up,
    w_down,
    routes,
    slot_order,
    group_map,
    buckets,
    grad_output,
):
    tok_count = inputs.shape[0]
    expert_count = w_router.shape[1]
    capacity = (5 * TOPK * tok_count + 4 * expert_count - 1) // (4 * expert_count)
    fsdp_count = lax.axis_size("fsdp")
    fsdp_place = lax.axis_index("fsdp")
    group_count = lax.axis_size("expert") * fsdp_count
    prompt_part = PLEN // fsdp_count
    prompt_rows = prompt_part * G_LINE
    cont_rows = CONT_DEV * CLEN
    key_span = PLEN + CLEN
    slot_total = expert_count * capacity
    qkv_full, out_full, attn_full, moe_full, router_full, table_full = (
        lax.all_gather(w_qkv, ("expert", "fsdp"), axis=0, tiled=True),
        lax.all_gather(w_out, ("expert", "fsdp"), axis=0, tiled=True),
        lax.all_gather(attn_gain, ("expert", "fsdp"), axis=0, tiled=True),
        lax.all_gather(moe_gain, ("expert", "fsdp"), axis=0, tiled=True),
        lax.all_gather(w_router, ("expert", "fsdp"), axis=0, tiled=True),
        lax.all_gather(bias_table, ("expert", "fsdp"), axis=0, tiled=True),
    )
    input_float = inputs.astype(jnp.float32)
    attn_scale = attn_full.astype(jnp.float32)
    normed, first_pull = jax.vjp(rms_scale, input_float, attn_scale)
    normed_low = normed.astype(jnp.bfloat16)
    qkv_rows = jnp.dot(normed_low, qkv_full, preferred_element_type=jnp.float32).astype(
        jnp.bfloat16
    )
    bucket_ids = jnp.arange(BUCKETS, dtype=jnp.int32)
    bucket_starts = jnp.sum((buckets[:, None] < bucket_ids[None, :]).astype(jnp.int32), axis=0)
    bucket_ends = jnp.concatenate([bucket_starts[1:], jnp.full((1,), key_span, jnp.int32)])
    head_table = table_full.astype(jnp.float32).reshape(HEADS, BUCKETS)

    def bucket_grid(distance):
        widened = distance[:, :, None]
        return (
            (widened >= bucket_starts[None, None, :]) & (widened < bucket_ends[None, None, :])
        ).astype(jnp.float32)

    prompt_pos = fsdp_place * prompt_part + jnp.arange(prompt_part, dtype=jnp.int32)
    prompt_keys_pos = jnp.arange(PLEN, dtype=jnp.int32)
    prompt_dist = prompt_pos[:, None] - prompt_keys_pos[None, :]
    cont_pos = PLEN + jnp.arange(CLEN, dtype=jnp.int32)
    cont_keys_pos = jnp.concatenate([prompt_keys_pos, cont_pos])
    cont_dist = cont_pos[:, None] - cont_keys_pos[None, :]
    prompt_hot = bucket_grid(prompt_dist)
    cont_hot = bucket_grid(cont_dist)
    prompt_bias = jnp.einsum("qkb,hb->hqk", prompt_hot, head_table, precision=HIGHEST)
    cont_bias = jnp.einsum("qkb,hb->hqk", cont_hot, head_table, precision=HIGHEST)
    prompt_mask = prompt_dist >= 0
    cont_mask = cont_dist >= 0
    group_hot = (group_map[:, None] == jnp.arange(G_LINE, dtype=jnp.int32)[None, :]).astype(
        jnp.float32
    )
    group_low = group_hot.astype(jnp.bfloat16)
    q_prompt = qkv_rows[:prompt_rows, :D].reshape(prompt_part, G_LINE, HEADS, HDIM)
    kv_local = qkv_rows[:prompt_rows, D:].reshape(prompt_part, G_LINE, 2 * D)
    kv_prompt = lax.all_gather(kv_local, "fsdp", axis=0, tiled=True)
    q_cont = qkv_rows[prompt_rows:, :D].reshape(CONT_DEV, CLEN, HEADS, HDIM).transpose(1, 0, 2, 3)
    kv_own = qkv_rows[prompt_rows:, D:].reshape(CONT_DEV, CLEN, 2 * D).transpose(1, 0, 2)
    kv_shared = jnp.einsum(
        "kgx,cg->kcx", kv_prompt, group_low, preferred_element_type=jnp.float32
    ).astype(jnp.bfloat16)
    kv_cont = jnp.concatenate([kv_shared, kv_own], 0)
    prompt_att, prompt_total = attend_forward(q_prompt, kv_prompt, prompt_bias, prompt_mask)
    cont_att, cont_total = attend_forward(q_cont, kv_cont, cont_bias, cont_mask)
    attn_low = jnp.concatenate(
        [prompt_att.reshape(prompt_rows, D), cont_att.transpose(1, 0, 2, 3).reshape(cont_rows, D)],
        0,
    ).astype(jnp.bfloat16)
    middle = input_float + jnp.dot(attn_low, out_full, preferred_element_type=jnp.float32)
    moe_scale = moe_full.astype(jnp.float32)
    router = router_full.astype(jnp.float32)
    second_normed, second_pull = jax.vjp(rms_scale, middle, moe_scale)
    (gate_pair, losses), router_pull = jax.vjp(
        lambda normed_rows, router_rows: route_local(normed_rows, router_rows, routes),
        second_normed,
        router,
    )
    kept_mask = (slot_order < capacity).astype(jnp.float32)
    gate_kept = gate_pair * kept_mask
    slot_ids = jnp.arange(slot_total, dtype=jnp.int32)
    slot_place = routes * capacity + slot_order
    slot_hot = (
        (slot_place.T[:, :, None] == slot_ids[None, None, :])
        & (slot_order.T[:, :, None] < capacity)
    ).astype(jnp.float32)
    slot_low = slot_hot.astype(jnp.bfloat16)
    outgoing = (
        jnp.einsum(
            "ktn,td->nd",
            slot_low,
            second_normed.astype(jnp.bfloat16),
            preferred_element_type=jnp.float32,
        )
        .astype(jnp.bfloat16)
        .reshape(expert_count, capacity, D)
    )
    incoming = lax.all_to_all(outgoing, "expert", split_axis=0, concat_axis=0, tiled=True)
    expert_rows = incoming.reshape(slot_total, D)
    row_count = expert_rows.shape[0]
    gate_whole, up_whole, down_whole = (
        lax.all_gather(w_gate[0], "fsdp", axis=1, tiled=True),
        lax.all_gather(w_up[0], "fsdp", axis=1, tiled=True),
        lax.all_gather(w_down[0], "fsdp", axis=0, tiled=True),
    )
    gate_pre = jnp.dot(expert_rows, gate_whole, preferred_element_type=jnp.float32)
    up_pre = jnp.dot(expert_rows, up_whole, preferred_element_type=jnp.float32)
    hidden = gated_unit(gate_pre, up_pre).astype(jnp.bfloat16)
    result_rows = jnp.dot(hidden, down_whole, preferred_element_type=jnp.float32)
    returned = lax.all_to_all(
        result_rows.astype(jnp.bfloat16).reshape(expert_count, capacity, D),
        "expert",
        split_axis=0,
        concat_axis=0,
        tiled=True,
    )
    picked = jnp.einsum(
        "ktn,nd->tkd", slot_low, returned.reshape(slot_total, D), preferred_element_type=jnp.float32
    )
    block_out = middle + jnp.sum(gate_kept[:, :, None] * picked, axis=1)
    output = block_out.astype(jnp.bfloat16)
    grad_final = grad_output.astype(jnp.float32)
    grad_pair = jnp.sum(grad_final[:, None, :] * picked, axis=-1) * kept_mask
    grad_picked = gate_kept[:, :, None] * grad_final[:, None, :]
    grad_buffer = jnp.einsum("ktn,tkd->nd", slot_hot, grad_picked, precision=HIGHEST).astype(
        jnp.bfloat16
    )
    grad_result = lax.all_to_all(
        grad_buffer.reshape(expert_count, capacity, D),
        "expert",
        split_axis=0,
        concat_axis=0,
        tiled=True,
    ).reshape(row_count, D)
    grad_hidden = jnp.dot(grad_result, down_whole.T, preferred_element_type=jnp.float32)
    down_total = jnp.dot(hidden.T, grad_result, preferred_element_type=jnp.float32)
    grad_gate_pre, grad_up_pre = activation_grads(gate_pre, up_pre, grad_hidden)
    gate_total = jnp.dot(expert_rows.T, grad_gate_pre, preferred_element_type=jnp.float32)
    up_total = jnp.dot(expert_rows.T, grad_up_pre, preferred_element_type=jnp.float32)
    grad_rows = jnp.dot(grad_gate_pre, gate_whole.T, preferred_element_type=jnp.float32) + jnp.dot(
        grad_up_pre, up_whole.T, preferred_element_type=jnp.float32
    )
    grad_gate, grad_up, grad_down = (
        lax.psum_scatter(
            gate_total.astype(jnp.bfloat16), "fsdp", scatter_dimension=1, tiled=True
        ).astype(jnp.float32),
        lax.psum_scatter(
            up_total.astype(jnp.bfloat16), "fsdp", scatter_dimension=1, tiled=True
        ).astype(jnp.float32),
        lax.psum_scatter(
            down_total.astype(jnp.bfloat16), "fsdp", scatter_dimension=0, tiled=True
        ).astype(jnp.float32),
    )
    grad_sent = lax.all_to_all(
        grad_rows.astype(jnp.bfloat16).reshape(expert_count, capacity, D),
        "expert",
        split_axis=0,
        concat_axis=0,
        tiled=True,
    )
    grad_second = jnp.sum(
        jnp.einsum(
            "ktn,nd->tkd",
            slot_low,
            grad_sent.reshape(slot_total, D),
            preferred_element_type=jnp.float32,
        ),
        axis=1,
    )
    loss_weights = jnp.array([ZLOSS_FACTOR, BALANCE_FACTOR], jnp.float32) / group_count
    router_normed, grad_router = router_pull((grad_pair, loss_weights))
    grad_middle_part, grad_moe_gain = second_pull(grad_second + router_normed)
    grad_middle = grad_final + grad_middle_part
    grad_branch = grad_middle.astype(jnp.bfloat16)
    grad_out_w = jnp.dot(attn_low.T, grad_branch, preferred_element_type=jnp.float32)
    grad_attn = jnp.dot(grad_branch, out_full.T, preferred_element_type=jnp.float32).astype(
        jnp.bfloat16
    )
    grad_prompt_att = grad_attn[:prompt_rows].reshape(prompt_part, G_LINE, HEADS, HDIM)
    grad_cont_att = (
        grad_attn[prompt_rows:].reshape(CONT_DEV, CLEN, HEADS, HDIM).transpose(1, 0, 2, 3)
    )
    prompt_grads = attend_backward(
        q_prompt, kv_prompt, prompt_bias, prompt_mask, prompt_total, grad_prompt_att
    )
    cont_grads = attend_backward(q_cont, kv_cont, cont_bias, cont_mask, cont_total, grad_cont_att)
    key_term = prompt_grads[1] + jnp.einsum(
        "kcx,cg->kgx", cont_grads[1][:PLEN], group_hot, precision=HIGHEST
    )
    grad_kv_prompt = lax.psum_scatter(
        key_term.astype(jnp.bfloat16), "fsdp", scatter_dimension=0, tiled=True
    ).astype(jnp.float32)
    grad_kv_own = cont_grads[1][PLEN:].transpose(1, 0, 2).reshape(cont_rows, 2 * D)
    prompt_block = jnp.concatenate(
        [prompt_grads[0].reshape(prompt_rows, D), grad_kv_prompt.reshape(prompt_rows, 2 * D)], 1
    )
    cont_block = jnp.concatenate(
        [cont_grads[0].transpose(1, 0, 2, 3).reshape(cont_rows, D), grad_kv_own], 1
    )
    grad_qkv = jnp.concatenate([prompt_block, cont_block], 0).astype(jnp.bfloat16)
    grad_qkv_w = jnp.dot(normed_low.T, grad_qkv, preferred_element_type=jnp.float32)
    grad_normed = jnp.dot(grad_qkv, qkv_full.T, preferred_element_type=jnp.float32)
    grad_table = (
        jnp.einsum("hqk,qkb->hb", prompt_grads[2], prompt_hot, precision=HIGHEST)
        + jnp.einsum("hqk,qkb->hb", cont_grads[2], cont_hot, precision=HIGHEST)
    ).reshape(HEADS * BUCKETS)
    grad_input_part, grad_attn_gain = first_pull(grad_normed)
    grad_inputs = grad_middle + grad_input_part
    dense_sums = (
        lax.psum_scatter(grad_qkv_w, ("expert", "fsdp"), scatter_dimension=0, tiled=True),
        lax.psum_scatter(grad_out_w, ("expert", "fsdp"), scatter_dimension=0, tiled=True),
        lax.psum_scatter(grad_attn_gain, ("expert", "fsdp"), scatter_dimension=0, tiled=True),
        lax.psum_scatter(grad_moe_gain, ("expert", "fsdp"), scatter_dimension=0, tiled=True),
        lax.psum_scatter(grad_router, ("expert", "fsdp"), scatter_dimension=0, tiled=True),
        lax.psum_scatter(grad_table, ("expert", "fsdp"), scatter_dimension=0, tiled=True),
    )
    return (
        output,
        losses[None, :],
        grad_inputs,
        dense_sums[0],
        dense_sums[1],
        dense_sums[2],
        dense_sums[3],
        dense_sums[4],
        dense_sums[5],
        grad_gate[None],
        grad_up[None],
        grad_down[None],
    )


def solution(mesh):
    in_specs = (
        P(("expert", "fsdp"), None),
        P(("expert", "fsdp"), None),
        P(("expert", "fsdp"), None),
        P(("expert", "fsdp")),
        P(("expert", "fsdp")),
        P(("expert", "fsdp"), None),
        P(("expert", "fsdp")),
        P("expert", None, "fsdp"),
        P("expert", None, "fsdp"),
        P("expert", "fsdp", None),
        P(("expert", "fsdp"), None),
        P(("expert", "fsdp"), None),
        P(("expert", "fsdp")),
        P(),
        P(("expert", "fsdp"), None),
    )
    out_specs = (
        P(("expert", "fsdp"), None),
        P(("expert", "fsdp"), None),
        P(("expert", "fsdp"), None),
        P(("expert", "fsdp"), None),
        P(("expert", "fsdp"), None),
        P(("expert", "fsdp")),
        P(("expert", "fsdp")),
        P(("expert", "fsdp"), None),
        P(("expert", "fsdp")),
        P("expert", None, "fsdp"),
        P("expert", None, "fsdp"),
        P("expert", "fsdp", None),
    )
    return jax.shard_map(local, mesh=mesh, in_specs=in_specs, out_specs=out_specs, check_vma=False)
```

profile of v0, /device:TPU:0, one launch (start us, length us, event | category | flops | bytes accessed | tf_op | source)
XLA Modules:
  0.0 1698.0 jit_solution(2465941423390389040)
XLA Ops:
  10.5 43.0 %all-reduce.7 = (bf16[512]{0:T(512)(128)(2,1)S(1)}, bf16[1024]{0:T(1024)(128)(2,1)S(1)}, bf16[1024]{0:T(1024)(128)(2,1)S(1)}) all-reduce(bf16[512]{0:T(512)(128)(2,1)S(1)} %dynamic-update-slice.1, bf16[1024]{0:T(1024)(128)(2,1)S(1)} %dynamic-update-slice, ...), channel_id=1, replica_groups=mesh['expert'=4,'fsdp'=8] {'expert','fsdp'}, use_global_device_ids=true, to_apply=%add.1 | all-reduce | flops 2560 | bytes 10240
  55.5 27.5 %all-gather.11.cloned.1.call-done = bf16[1024,3072]{1,0:T(8,128)(2,1)} async-done(((bf16[32,3072]{1,0:T(8,128)(2,1)}), bf16[1024,3072]{1,0:T(8,128)(2,1)}) %all-gather.11.cloned.1.call-update) | async-done | bytes 6291472 | tf_op jit(solution)/shard_map/all_gather | solution.py:131
  101.6 24.4 %copy.136 = pred[128,1024,32]{1,2,0:T(32,128)(4,1)} copy(pred[128,1024,32]{0,2,1:T(32,128)(4,1)S(1)} %compare_and_fusion.1) | data formatting | bytes 8388608 | tf_op jit(solution)/shard_map/and | solution.py:153
  130.3 8.1 copy.137
  139.9 7.2 compare_and_fusion
  147.1 28.9 %copy.142 = pred[128,1152,32]{1,2,0:T(32,128)(4,1)} copy(pred[128,1152,32]{0,2,1:T(32,128)(4,1)} %compare_and_fusion) | data formatting | bytes 9437184 | tf_op jit(solution)/shard_map/and | solution.py:153
  175.9 8.8 fusion.127
  184.7 71.6 %all-gather.3 = bf16[32,32,4]{1,2,0:T(4,128)(2,1)S(1)} all-gather(bf16[1,32,4]{1,2,0:T(4,128)(2,1)S(1)} %bitcast.242), channel_id=1, replica_groups=mesh['expert'=4,'fsdp'=8] {'expert','fsdp'}, dimensions={0}, use_global_device_ids=true | all-gather | bytes 8448 | tf_op jit(solution)/shard_map/all_gather | solution.py:135
  264.5 10.8 fusion.124
  275.4 7.7 exponential_reduce_fusion
  283.1 10.5 fusion.76
  302.2 8.4 fusion.123
  331.4 7.5 bitcast_convert_fusion
  338.9 14.3 all-to-all-done
  358.0 9.7 all-gather.19.cloned.1.call-done
  367.7 11.4 fusion.18
  379.1 81.2 %all-gather.21.cloned.1.call-done = bf16[1,2816,1024]{2,1,0:T(8,128)(2,1)} async-done(((bf16[1,352,1024]{2,1,0:T(8,128)(2,1)}), bf16[1,2816,1024]{2,1,0:T(8,128)(2,1)}) %all-gather.21.cloned.1.call-update) | async-done | bytes 5767184 | tf_op jit(solution)/shard_map/all_gather | solution.py:221
  460.3 11.4 fusion.12
  471.7 81.1 %all-gather.17.cloned.1.call-done = bf16[1,1024,2816]{1,2,0:T(8,128)(2,1)} async-done(((bf16[1,1024,352]{1,2,0:T(8,128)(2,1)}), bf16[1,1024,2816]{1,2,0:T(8,128)(2,1)}) %all-gather.17.cloned.1.call-update) | async-done | bytes 5767184 | tf_op jit(solution)/shard_map/all_gather | solution.py:219
  552.8 24.3 %fusion.8 = (bf16[960,2816]{1,0:T(8,128)(2,1)}, bf16[960,2816]{1,0:T(8,128)(2,1)}, bf16[960,2816]{1,0:T(8,128)(2,1)}) fusion(f32[960,2816]{1,0:T(8,128)} %fusion.12, f32[960,2816]{1,0:T(8,128)} %fusion.18, bf16[960,1024]{1,0:T(8,128)(2,1)} %bitcast.18, bf16[1,1024,2816]{1,2,0:T(8,128)(2,1)} %all-gather.17.cloned.1.call-done), kind=kOutput, calls=%fused_computation.21 | convolution fusion | flops 5606768640 | bytes 45580288 | tf_op jit(solution)/shard_map/dot_general | solution.py:223
  577.1 10.8 fusion.43
  592.3 9.4 fusion.16
  601.7 10.4 add_convert_fusion
  626.7 18.7 %all-to-all-done.3 = bf16[4,240,1024]{2,1,0:T(8,128)(2,1)} async-done(((bf16[4,240,1024]{2,1,0:T(8,128)(2,1)}), bf16[4,240,1024]{2,1,0:T(8,128)(2,1)}, u32[]{:S(2)}, u32[]{:S(2)}) %all-to-all-start.3) | async-done | bytes 1966112 | tf_op jit(solution)/shard_map/all_to_all | solution.py:271
  666.3 8.9 multiply_reduce_fusion.2
  680.4 12.3 multiply_reduce_fusion.1
  692.7 9.5 convolution_bitcast_fusion.1
  702.2 7.6 multiply_convert_fusion.3
  716.9 14.3 convert_reduce_fusion
  746.0 6.2 fusion
  752.3 11.9 copy.170
  769.2 10.9 convolution_convert_fusion.1
  780.2 11.1 convolution_convert_fusion.2
  791.3 11.5 convolution_convert_fusion
  807.8 8.5 fusion.75
  828.4 80.6 %reduce-scatter.22.cloned.1.call-done = bf16[128,4096]{1,0:T(8,128)(2,1)} async-done(((bf16[1024,4096]{1,0:T(8,128)(2,1)}), bf16[128,4096]{1,0:T(8,128)(2,1)}) %reduce-scatter.22.cloned.1.call-update) | async-done | bytes 1048592
  914.4 7.8 fusion.96
  924.1 7.1 copy.160
  931.2 9.2 copy.159
  940.4 11.9 convolution_bitcast_fusion.3
  956.8 90.1 %reduce-scatter.24.cloned.1.call-done = f32[32,4]{1,0:T(8,128)} async-done(((f32[1024,4]{1,0:T(8,128)}), f32[32,4]{1,0:T(8,128)}) %reduce-scatter.24.cloned.1.call-update) | async-done | bytes 528
  1048.3 109.3 %reduce-scatter.18.cloned.1.call-done = bf16[1024,352]{0,1:T(8,128)(2,1)} async-done(((bf16[1024,2816]{0,1:T(8,128)(2,1)}), bf16[1024,352]{0,1:T(8,128)(2,1)}) %reduce-scatter.18.cloned.1.call-update) | async-done | bytes 720912 | tf_op jit(solution)/shard_map/reduce_scatter | solution.py:264
  1160.0 111.1 %reduce-scatter.16.cloned.1.call-done = bf16[1024,352]{0,1:T(8,128)(2,1)} async-done(((bf16[1024,2816]{0,1:T(8,128)(2,1)}), bf16[1024,352]{0,1:T(8,128)(2,1)}) %reduce-scatter.16.cloned.1.call-update) | async-done | bytes 720912 | tf_op jit(solution)/shard_map/reduce_scatter | solution.py:261
  1273.4 111.3 %reduce-scatter.20.cloned.1.call-done = bf16[352,1024]{1,0:T(8,128)(2,1)} async-done(((bf16[2816,1024]{1,0:T(8,128)(2,1)}), bf16[352,1024]{1,0:T(8,128)(2,1)}) %reduce-scatter.20.cloned.1.call-update) | async-done | bytes 720912 | tf_op jit(solution)/shard_map/reduce_scatter | solution.py:267
  1387.1 7.1 fusion.54
  1394.2 42.3 %all-reduce.6 = (f32[1024]{0:T(1024)S(1)}, f32[1024]{0:T(1024)S(1)}, f32[512]{0:T(512)S(1)}) all-reduce(f32[1024]{0:T(1024)S(1)} %get-tuple-element.16, f32[1024]{0:T(1024)S(1)} %copy-done.36, f32[512]{0:T(512)S(1)} %reshape.393), channel_id=8, replica_groups=mesh['expert'=4,'fsdp'=8] {'expert','fsdp'}, use_global_device_ids=true, to_apply=%region_28.29.clone | all-reduce | flops 2560 | bytes 20480
  1441.2 91.0 %reduce-scatter.14.cloned.1.call-done = f32[32,1024]{1,0:T(8,128)} async-done(((f32[1024,1024]{1,0:T(8,128)}), f32[32,1024]{1,0:T(8,128)}) %reduce-scatter.14.cloned.1.call-update) | async-done | bytes 131088 | tf_op jit(solution)/shard_map/reduce_scatter | solution.py:328
  1532.2 159.1 %reduce-scatter.12.cloned.1.call-done = f32[32,3072]{1,0:T(8,128)} async-done(((f32[1024,3072]{1,0:T(8,128)}), f32[32,3072]{1,0:T(8,128)}) %reduce-scatter.12.cloned.1.call-update) | async-done | bytes 393232 | tf_op jit(solution)/shard_map/reduce_scatter | solution.py:327
  (269 shorter events, 183.2 us)
Async XLA Ops:
  7.2 75.8 %all-gather.11.cloned.1.call-start = ((), (), s32[]{:S(2)}) async-start(), calls=%async_computation.11 | async-start | bytes 6488064 | tf_op jit(solution)/shard_map/all_gather | solution.py:131
  7.9 256.6 %all-gather.13.cloned.1.call-start = ((), (), s32[]{:S(2)}) async-start(), calls=%async_computation.12 | async-start | bytes 9437184 | tf_op jit(solution)/shard_map/all_gather | solution.py:174
  53.5 35.2 %copy-start.25 = (f32[1024]{0:T(1024)}, f32[1024]{0:T(1024)S(1)}, u32[]{:S(2)}) copy-start(f32[1024]{0:T(1024)S(1)} %convert_element_type.129) | copy-start | bytes 12292
  55.5 33.3 %copy-start.29 = (f32[384]{0:T(512)}, f32[384]{0:T(512)S(1)}, u32[]{:S(2)}) copy-start(f32[384]{0:T(512)S(1)} %fusion.106) | copy-start | bytes 4612
  93.2 224.3 %all-gather.15.cloned.1.call-start = ((), (), s32[]{:S(2)}) async-start(), calls=%async_computation.13 | async-start | bytes 2162688 | tf_op jit(solution)/shard_map/all_gather | solution.py:132
  93.9 273.8 %all-gather.19.cloned.1.call-start = ((), (), s32[]{:S(2)}) async-start(), calls=%async_computation.20 | async-start | bytes 6488064 | tf_op jit(solution)/shard_map/all_gather | solution.py:220
  94.5 365.8 %all-gather.21.cloned.1.call-start = ((), (), s32[]{:S(2)}) async-start(), calls=%async_computation.21 | async-start | bytes 6488064 | tf_op jit(solution)/shard_map/all_gather | solution.py:221
  95.1 457.8 %all-gather.17.cloned.1.call-start = ((), (), s32[]{:S(2)}) async-start(), calls=%async_computation.19 | async-start | bytes 6488064 | tf_op jit(solution)/shard_map/all_gather | solution.py:219
  97.5 160.9 %copy-start.37 = (s32[2,384]{1,0:T(2,128)}, s32[2,384]{1,0:T(2,128)S(1)}, u32[]{:S(2)}) copy-start(s32[2,384]{1,0:T(2,128)S(1)} %add_bitcast_fusion) | copy-start | bytes 9220
  97.5 160.9 %copy-start.41 = (pred[2,384]{1,0:T(4,128)(4,1)}, pred[2,384]{1,0:T(4,128)(4,1)S(1)}, u32[]{:S(2)}) copy-start(pred[2,384]{1,0:T(4,128)(4,1)S(1)} %fusion.118) | copy-start | bytes 2308
  97.7 42.2 %copy-start.43 = (s32[32]{0:T(128)}, s32[32]{0:T(128)S(1)}, u32[]{:S(2)}) copy-start(s32[32]{0:T(128)S(1)} %convert_reduce_fusion.2) | copy-start | bytes 388
  98.0 28.1 %copy-start.22 = (s32[128,1024]{0,1:T(8,128)}, s32[128,1024]{0,1:T(8,128)S(1)}, u32[]{:S(2)}) copy-start(s32[128,1024]{0,1:T(8,128)S(1)} %copy.135) | copy-start | bytes 1572868
  98.0 41.8 %copy-start.45 = (s32[32]{0:T(128)}, s32[32]{0:T(128)S(1)}, u32[]{:S(2)}) copy-start(s32[32]{0:T(128)S(1)} %pad_add_fusion.1) | copy-start | bytes 388
  175.9 80.6 %copy-start.14 = (bf16[384,1024]{1,0:T(8,128)(2,1)S(1)}, bf16[384,1024]{1,0:T(8,128)(2,1)}, u32[]{:S(2)}) copy-start(bf16[384,1024]{1,0:T(8,128)(2,1)} %param.30) | copy-start | bytes 2359300
  175.9 84.2 %copy-start.19 = (bf16[384,3072]{1,0:T(8,128)(2,1)S(1)}, bf16[384,3072]{1,0:T(8,128)(2,1)}, u32[]{:S(2)}) copy-start(bf16[384,3072]{1,0:T(8,128)(2,1)} %copy-done.18) | copy-start | bytes 7077892
  262.8 12.6 copy-start.10
  264.3 402.0 %copy-start.8 = (bf16[128,2048]{0,1:T(8,128)(2,1)}, bf16[128,2048]{0,1:T(8,128)(2,1)S(1)}, u32[]{:S(2)}) copy-start(bf16[128,2048]{0,1:T(8,128)(2,1)S(1)} %copy.139) | copy-start | bytes 1572868
  264.5 37.7 %copy-start.16 = (bf16[128,1024]{0,1:T(8,128)(2,1)}, bf16[128,1024]{0,1:T(8,128)(2,1)S(1)}, u32[]{:S(2)}) copy-start(bf16[128,1024]{0,1:T(8,128)(2,1)S(1)} %copy.140) | copy-start | bytes 786436
  283.1 10.5 copy-start.27
  283.1 12.9 copy-start.49
  296.0 21.5 %copy-start.20 = (bf16[256,1024]{1,0:T(8,128)(2,1)}, bf16[256,1024]{1,0:T(8,128)(2,1)S(1)}, u32[]{:S(2)}) copy-start(bf16[256,1024]{1,0:T(8,128)(2,1)S(1)} %reshape.373) | copy-start | bytes 1572868
  320.2 340.3 %copy-start.3 = (f32[384,1024]{1,0:T(8,128)}, f32[384,1024]{1,0:T(8,128)S(1)}, u32[]{:S(2)}) copy-start(f32[384,1024]{1,0:T(8,128)S(1)} %get-tuple-element.54) | copy-start | bytes 4718596
  320.2 10.4 copy-start.34
  320.2 10.4 copy-start.35
  320.3 11.2 copy-start.38
  320.3 11.1 copy-start.42
  324.5 28.8 %all-to-all-start = ((bf16[4,240,1024]{2,1,0:T(8,128)(2,1)}), bf16[4,240,1024]{2,1,0:T(8,128)(2,1)}, u32[]{:S(2)}, u32[]{:S(2)}) async-start(bf16[4,240,1024]{2,1,0:T(8,128)(2,1)} %bitcast.230), calls=%async_computation | async-start | bytes 3932160 | tf_op jit(solution)/shard_map/all_to_all | solution.py:215
  353.3 107.0 %all-to-all-start.2 = ((bf16[4,240,1024]{2,1,0:T(8,128)(2,1)}), bf16[4,240,1024]{2,1,0:T(8,128)(2,1)}, u32[]{:S(2)}, u32[]{:S(2)}) async-start(bf16[4,240,1024]{2,1,0:T(8,128)(2,1)} %bitcast.238), calls=%async_computation.2 | async-start | bytes 3932160 | tf_op jit(solution)/shard_map/all_to_all | solution.py:245
  587.9 28.8 %all-to-all-start.1 = ((bf16[4,240,1024]{2,1,0:T(8,128)(2,1)}), bf16[4,240,1024]{2,1,0:T(8,128)(2,1)}, u32[]{:S(2)}, u32[]{:S(2)}) async-start(bf16[4,240,1024]{2,1,0:T(8,128)(2,1)} %bitcast.239), calls=%async_computation.1 | async-start | bytes 3932160 | tf_op jit(solution)/shard_map/all_to_all | solution.py:227
  616.7 28.7 %all-to-all-start.3 = ((bf16[4,240,1024]{2,1,0:T(8,128)(2,1)}), bf16[4,240,1024]{2,1,0:T(8,128)(2,1)}, u32[]{:S(2)}, u32[]{:S(2)}) async-start(bf16[4,240,1024]{2,1,0:T(8,128)(2,1)} %bitcast.237), calls=%async_computation.3 | async-start | bytes 3932160 | tf_op jit(solution)/shard_map/all_to_all | solution.py:271
  621.1 288.0 %reduce-scatter.22.cloned.1.call-start = ((), (), s32[]{:S(2)}) async-start(), calls=%async_computation.22 | async-start | bytes 9437184
  665.0 10.2 slice-start.4
  702.2 12.2 slice-start
  702.2 12.2 slice-start.1
  702.2 13.5 slice-start.2
  716.9 14.3 copy-start.11
  764.2 282.7 %reduce-scatter.24.cloned.1.call-start = ((), (), s32[]{:S(2)}) async-start(), calls=%async_computation.23 | async-start | bytes 540672
  769.2 388.4 %reduce-scatter.18.cloned.1.call-start = ((), (), s32[]{:S(2)}) async-start(), calls=%async_computation.17 | async-start | bytes 6488064 | tf_op jit(solution)/shard_map/reduce_scatter | solution.py:264
  780.1 491.0 %reduce-scatter.16.cloned.1.call-start = ((), (), s32[]{:S(2)}) async-start(), calls=%async_computation.16 | async-start | bytes 6488064 | tf_op jit(solution)/shard_map/reduce_scatter | solution.py:261
  791.3 593.4 %reduce-scatter.20.cloned.1.call-start = ((), (), s32[]{:S(2)}) async-start(), calls=%async_computation.18 | async-start | bytes 6488064 | tf_op jit(solution)/shard_map/reduce_scatter | solution.py:267
  802.8 729.4 %reduce-scatter.14.cloned.1.call-start = ((), (), s32[]{:S(2)}) async-start(), calls=%async_computation.15 | async-start | bytes 4325376 | tf_op jit(solution)/shard_map/reduce_scatter | solution.py:328
  807.7 12.6 copy-start.9
  807.7 883.6 %reduce-scatter.12.cloned.1.call-start = ((), (), s32[]{:S(2)}) async-start(), calls=%async_computation.14 | async-start | bytes 12976128 | tf_op jit(solution)/shard_map/reduce_scatter | solution.py:327
  827.4 87.0 %copy-start.13 = (bf16[384,1024]{1,0:T(8,128)(2,1)S(1)}, bf16[384,1024]{1,0:T(8,128)(2,1)}, u32[]{:S(2)}) copy-start(bf16[384,1024]{1,0:T(8,128)(2,1)} %param.16) | copy-start | bytes 2359300
  827.4 87.0 %copy-start.26 = (f32[1024]{0:T(1024)S(1)}, f32[1024]{0:T(1024)}, u32[]{:S(2)}) copy-start(f32[1024]{0:T(1024)} %copy-done.25) | copy-start | bytes 12292
  827.4 87.0 %copy-start.30 = (f32[384]{0:T(512)S(1)}, f32[384]{0:T(512)}, u32[]{:S(2)}) copy-start(f32[384]{0:T(512)} %copy-done.29) | copy-start | bytes 4612
  940.4 11.9 copy-start.5
  1387.1 51.2 %copy-start.33 = (f32[384]{0:T(512)S(1)}, f32[384]{0:T(512)}, u32[]{:S(2)}) copy-start(f32[384]{0:T(512)} %copy-done.32) | copy-start | bytes 4612
  (29 other events, 154.1 us)
Sparse Core Ops, SparseCore 0:
  10.9 72.0 all-gather.10
  93.3 123.5 all-gather.12
  219.9 54.5 all-gather.14
  276.5 91.1 all-gather.18
  369.7 90.5 all-gather.20
  462.3 90.4 all-gather.16
  764.3 144.7 reduce-scatter.21
  911.9 134.9 reduce-scatter.23
  1050.6 106.9 reduce-scatter.17
  1161.1 109.9 reduce-scatter.15
  1274.7 109.9 reduce-scatter.19
  1387.4 144.7 reduce-scatter.13
  1538.8 152.4 reduce-scatter.11
where the time goes:
time: 1710 us; the launch traced here: 1700 us
  waiting for transfers between devices  993 us (58%)
  matrix products  286 us (17%)
  blocking collectives  157 us (9%)
  local copies, waits for them, and re-layouts  142 us (8%)
  other arithmetic  84.8 us (5%)
  starting transfers between devices  18.5 us (1%)
    unnamed x15, waiting for transfers between devices  174 us
    reduce_scatter x1, waiting for transfers between devices, local(): lax.psum_scatter(grad_qkv_w, ('expert', 'fsdp'), scatter_dimension=0, til...  159 us
    reduce_scatter x1, waiting for transfers between devices, local(): lax.psum_scatter(down_total.astype(jnp.bfloat16), 'fsdp', scatter_dimensi...  111 us
    reduce_scatter x1, waiting for transfers between devices, local(): lax.psum_scatter(gate_total.astype(jnp.bfloat16), 'fsdp', scatter_dimensi...  111 us
    reduce_scatter x1, waiting for transfers between devices, local(): lax.psum_scatter(up_total.astype(jnp.bfloat16), 'fsdp', scatter_dimension...  109 us
    reduce_scatter x1, waiting for transfers between devices, local(): lax.psum_scatter(grad_out_w, ('expert', 'fsdp'), scatter_dimension=0, til...  91 us
    unnamed x2, blocking collectives  85.3 us
    all_gather x1, waiting for transfers between devices, local(): lax.all_gather(w_down[0], 'fsdp', axis=0, tiled=True)  81.2 us
  transfers between devices with their start and end apart: 17, of which 14 were waited for; matrix products, arithmetic and copies ran while one was open for 20% of the time, Pallas kernels for 0%

commit v1 on v0

v1 whole, which is shorter than its diff:
```python
import functools

import jax
import jax.numpy as jnp
from jax import lax
from jax.experimental import pallas as pl
from jax.experimental.pallas import tpu as pltpu
from jax.sharding import PartitionSpec as P

D = 1024
HEADS = 16
HDIM = 64
BUCKETS = 32
TOPK = 2
PLEN = 1024
CLEN = 128
G_LINE = 2

EPSILON = 1e-06
ZLOSS_FACTOR = 0.001
BALANCE_FACTOR = 0.01
MASK_VALUE = -1e30
LOG2E = 1.4426950408889634
HIGHEST = lax.Precision.HIGHEST
TILE = 256
HALF = 128
SPAN_BLOCKS = (PLEN + CLEN) // HALF
BF = jnp.bfloat16
F32 = jnp.float32
NT = (((1,), (1,)), ((), ()))
TN = (((0,), (0,)), ((), ()))


def rms_scale(values, scale_row):
    inverse = lax.rsqrt(jnp.mean(values * values, axis=-1, keepdims=True) + EPSILON)
    return values * inverse * scale_row


def gated_unit(gate_pre, up_pre):
    return jax.nn.gelu(gate_pre, approximate=True) * up_pre


def activation_grads(gate_pre, up_pre, grad_hidden):
    activated, act_pull = jax.vjp(gated_unit, gate_pre, up_pre)
    grad_gate_pre, grad_up_pre = act_pull(grad_hidden)
    return (grad_gate_pre.astype(BF), grad_up_pre.astype(BF))


def route_local(normed, router, routes):
    logits = jnp.dot(normed, router, precision=HIGHEST)
    log_total = jax.nn.logsumexp(logits, axis=-1)
    chances = jnp.exp(logits - log_total[:, None])
    expert_ids = jnp.arange(router.shape[1], dtype=jnp.int32)
    first_hot = (routes[:, 0:1] == expert_ids[None, :]).astype(F32)
    second_hot = (routes[:, 1:2] == expert_ids[None, :]).astype(F32)
    first_chance = jnp.sum(chances * first_hot, axis=-1)
    second_chance = jnp.sum(chances * second_hot, axis=-1)
    both_chances = first_chance + second_chance
    gate_pair = jnp.stack([first_chance / both_chances, second_chance / both_chances], -1)
    z_loss = jnp.mean(log_total * log_total)
    expert_share = jnp.sum(first_hot + second_hot, axis=0) / (TOPK * routes.shape[0])
    balance = router.shape[1] * jnp.sum(expert_share * jnp.mean(chances, axis=0))
    return (gate_pair, jnp.stack([z_loss, balance]))


class Shape:
    def __init__(self, fsdp_count):
        self.srcs = fsdp_count
        self.hp = HEADS // fsdp_count
        self.width = self.hp * HDIM
        self.part = PLEN // fsdp_count
        self.rows = G_LINE * self.part + CLEN
        self.spt = TILE // self.part
        self.tiles = PLEN // TILE
        self.pairs = fsdp_count // 2
        self.prompt_pairs = self.pairs // G_LINE
        self.units = G_LINE * self.tiles + self.pairs


def order_conts(sh, group_ref, perm_ref):
    counts = [jnp.int32(0), jnp.int32(sh.srcs // G_LINE)]
    for c in range(sh.srcs):
        first = group_ref[c] == 0
        perm_ref[jnp.where(first, counts[0], counts[1])] = jnp.int32(c)
        step = first.astype(jnp.int32)
        counts = [counts[0] + step, counts[1] + 1 - step]


def build_bias(sh, table_ref, bucket_ref, bias_ref):
    bucket = bucket_ref[...]
    for h in range(sh.hp):
        dist = jnp.zeros(bucket.shape, F32)
        for b in range(BUCKETS):
            dist = jnp.where(bucket == b, table_ref[h, b] * LOG2E, dist)
        bias_ref[h, 0] = jnp.full((HALF, HALF), MASK_VALUE, F32)
        before = jnp.full((1, HALF), MASK_VALUE, F32)
        for n in range(SPAN_BLOCKS):
            now = dist[n : n + 1, :]
            both = jnp.broadcast_to(jnp.concatenate([before, now], axis=1), (HALF, 2 * HALF))
            turned = pltpu.roll(both, HALF, 1, stride=1, stride_axis=0)
            bias_ref[h, 1 + n] = turned[:, :HALF]
            before = now


def head_mask(sh, h, rows):
    if sh.hp == 1:
        return None
    lane = lax.broadcasted_iota(jnp.int32, (1, sh.width), 1)
    return (lane >= h * HDIM) & (lane < (h + 1) * HDIM)


def only_head(sh, h, x):
    mask = head_mask(sh, h, x.shape[0])
    return x if mask is None else jnp.where(mask, x, jnp.zeros_like(x))


def prompt_rows_of(sh, ref, g, t, part):
    lanes = slice(part * sh.width, (part + 1) * sh.width)
    start = pl.multiple_of(g * sh.part, sh.part)
    return jnp.concatenate(
        [ref[t * sh.spt + s, pl.ds(start, sh.part), lanes] for s in range(sh.spt)], axis=0
    )


def cont_rows_of(sh, ref, c, part):
    lanes = slice(part * sh.width, (part + 1) * sh.width)
    return ref[c, G_LINE * sh.part :, lanes]


def put_prompt_rows(sh, ref, g, t, part, value):
    lanes = slice(part * sh.width, (part + 1) * sh.width)
    start = pl.multiple_of(g * sh.part, sh.part)
    for s in range(sh.spt):
        ref[t * sh.spt + s, pl.ds(start, sh.part), lanes] = value[
            s * sh.part : (s + 1) * sh.part
        ].astype(ref.dtype)


def transpose_low(x):
    return x.astype(F32).T.astype(BF)


def add_bias(scores, bias_ref, h, base, step_q):
    rows = []
    for a in range(2):
        cols = []
        for b in range(2):
            part = scores[a * HALF : (a + 1) * HALF, b * HALF : (b + 1) * HALF]
            cols.append(part * LOG2E + bias_ref[h, base + b * step_q - a])
        rows.append(jnp.concatenate(cols, axis=1))
    return jnp.concatenate(rows, axis=0)


def fold_max(x):
    return jnp.max(x.reshape(-1, 8, x.shape[-1]), axis=0)


def fold_sum(x):
    return jnp.sum(x.reshape(-1, 8, x.shape[-1]), axis=0)


def attn_forward_kernel(
    sh, group_ref, table_ref, bucket_ref, x_ref, o_ref, ot_ref, lse_ref, bias, vt, vtc, sc, perm
):
    order_conts(sh, group_ref, perm)
    build_bias(sh, table_ref, bucket_ref, bias)

    def make_vt(i, _):
        g, t = i // sh.tiles, lax.rem(i, sh.tiles)
        vt[i] = transpose_low(prompt_rows_of(sh, x_ref, g, t, 2))
        return 0

    lax.fori_loop(0, G_LINE * sh.tiles, make_vt, 0)

    def make_vtc(c, _):
        vtc[c] = transpose_low(cont_rows_of(sh, x_ref, c, 2))
        return 0

    lax.fori_loop(0, sh.srcs, make_vtc, 0)

    def scores_tile(keys, qh, base, step_q, kt, peaks):
        out = []
        for h in range(sh.hp):
            s = lax.dot_general(keys, qh[h], NT, preferred_element_type=F32)
            s = add_bias(s, bias, h, base, step_q)
            sc[h, pl.ds(pl.multiple_of(kt * TILE, TILE), TILE), :] = s
            out.append(jnp.maximum(peaks[h], fold_max(s)))
        return tuple(out)

    def value_tile(g, kt, peaks, carry):
        out = []
        for h in range(sh.hp):
            total, acc = carry[h]
            p = jnp.exp2(sc[h, pl.ds(pl.multiple_of(kt * TILE, TILE), TILE), :] - peaks[h])
            total = total + fold_sum(p)
            values = vt[g * sh.tiles + kt, h * HDIM : (h + 1) * HDIM, :]
            acc = acc + jnp.dot(values, p.astype(BF), preferred_element_type=F32)
            out.append((total, acc))
        return tuple(out)

    first_peaks = tuple(jnp.full((8, TILE), MASK_VALUE, F32) for _ in range(sh.hp))
    first_carry = tuple(
        (jnp.zeros((8, TILE), F32), jnp.zeros((HDIM, TILE), F32)) for _ in range(sh.hp)
    )

    def finish(unit, peaks, carry):
        outs = []
        for h in range(sh.hp):
            total = jnp.sum(carry[h][0], axis=0, keepdims=True)
            outs.append(carry[h][1] / total)
            lse_ref[unit, h : h + 1, :] = peaks[h] + jnp.log2(total)
        whole = jnp.concatenate(outs, axis=0) if sh.hp > 1 else outs[0]
        ot_ref[unit] = whole
        return whole.T

    def prompt_unit(i, _):
        g, qt = i // sh.tiles, lax.rem(i, sh.tiles)
        q = prompt_rows_of(sh, x_ref, g, qt, 0) * BF(HDIM**-0.5)
        qh = [only_head(sh, h, q) for h in range(sh.hp)]

        def first(kt, peaks):
            keys = prompt_rows_of(sh, x_ref, g, kt, 1)
            return scores_tile(keys, qh, 2 * (qt - kt) + 1, 1, kt, peaks)

        peaks = lax.fori_loop(0, qt + 1, first, first_peaks)
        peaks = [jnp.max(p, axis=0, keepdims=True) for p in peaks]
        carry = lax.fori_loop(0, qt + 1, lambda kt, c: value_tile(g, kt, peaks, c), first_carry)
        put_prompt_rows(sh, o_ref, g, qt, 0, finish(i, peaks, carry))
        return 0

    lax.fori_loop(0, G_LINE * sh.tiles, prompt_unit, 0)

    def cont_unit(i, _):
        conts = [perm[2 * i], perm[2 * i + 1]]
        g = i // sh.prompt_pairs
        q = jnp.concatenate([cont_rows_of(sh, x_ref, c, 0) for c in conts], axis=0)
        q = q * BF(HDIM**-0.5)
        qh = [only_head(sh, h, q) for h in range(sh.hp)]

        def first(kt, peaks):
            keys = prompt_rows_of(sh, x_ref, g, kt, 1)
            return scores_tile(keys, qh, SPAN_BLOCKS - 2 * kt, 0, kt, peaks)

        peaks = lax.fori_loop(0, sh.tiles, first, first_peaks)
        own = []
        next_peaks = []
        for h in range(sh.hp):
            parts = []
            for b in range(2):
                keys = cont_rows_of(sh, x_ref, conts[b], 1)
                s = lax.dot_general(
                    keys, qh[h][b * HALF : (b + 1) * HALF], NT, preferred_element_type=F32
                )
                parts.append(s * LOG2E + bias[h, 1])
            own.append(jnp.concatenate(parts, axis=1))
            next_peaks.append(jnp.maximum(peaks[h], fold_max(own[h])))
        peaks = [jnp.max(p, axis=0, keepdims=True) for p in next_peaks]
        start = []
        for h in range(sh.hp):
            p = jnp.exp2(own[h] - peaks[h])
            low = p.astype(BF)
            acc = jnp.concatenate(
                [
                    jnp.dot(
                        vtc[conts[b], h * HDIM : (h + 1) * HDIM, :],
                        low[:, b * HALF : (b + 1) * HALF],
                        preferred_element_type=F32,
                    )
                    for b in range(2)
                ],
                axis=1,
            )
            start.append((fold_sum(p), acc))
        carry = lax.fori_loop(
            0, sh.tiles, lambda kt, c: value_tile(g, kt, peaks, c), tuple(start)
        )
        done = finish(G_LINE * sh.tiles + i, peaks, carry)
        for b in range(2):
            o_ref[conts[b], G_LINE * sh.part :, :] = done[b * HALF : (b + 1) * HALF].astype(BF)
        return 0

    lax.fori_loop(0, sh.pairs, cont_unit, 0)


def attn_backward_kernel(
    sh,
    group_ref,
    table_ref,
    bucket_ref,
    x_ref,
    do_ref,
    ot_ref,
    lse_ref,
    dx_ref,
    dtable_ref,
    bias,
    dbias,
    ktr,
    ktc,
    dk,
    dv,
    perm,
):
    order_conts(sh, group_ref, perm)
    build_bias(sh, table_ref, bucket_ref, bias)
    dbias[...] = jnp.zeros_like(dbias)
    dk[...] = jnp.zeros_like(dk)
    dv[...] = jnp.zeros_like(dv)

    def make_kt(i, _):
        g, t = i // sh.tiles, lax.rem(i, sh.tiles)
        ktr[i] = transpose_low(prompt_rows_of(sh, x_ref, g, t, 1))
        return 0

    lax.fori_loop(0, G_LINE * sh.tiles, make_kt, 0)

    def make_ktc(c, _):
        ktc[c] = transpose_low(cont_rows_of(sh, x_ref, c, 1))
        return 0

    lax.fori_loop(0, sh.srcs, make_ktc, 0)

    def inner_terms(unit, do):
        outs = []
        turned = do.astype(F32).T
        for h in range(sh.hp):
            rows = slice(h * HDIM, (h + 1) * HDIM)
            prod = ot_ref[unit, rows, :] * turned[rows, :]
            outs.append(jnp.sum(prod, axis=0, keepdims=True))
        return outs

    def grads_tile(g, kt, qh, doh, lse, inner, base, step_q, dqs):
        keys = prompt_rows_of(sh, x_ref, g, kt, 1)
        values = prompt_rows_of(sh, x_ref, g, kt, 2)
        slot = g * sh.tiles + kt
        out = []
        dkey = dvalue = None
        for h in range(sh.hp):
            s = lax.dot_general(keys, qh[h], NT, preferred_element_type=F32)
            dp = lax.dot_general(values, doh[h], NT, preferred_element_type=F32)
            p = jnp.exp2(add_bias(s, bias, h, base, step_q) - lse[h])
            ds = p * (dp - inner[h])
            for a in range(2):
                for b in range(2):
                    dbias[h, base + b * step_q - a] += ds[
                        a * HALF : (a + 1) * HALF, b * HALF : (b + 1) * HALF
                    ]
            low = ds.astype(BF)
            more_k = jnp.dot(low, qh[h], preferred_element_type=F32)
            more_v = jnp.dot(p.astype(BF), doh[h], preferred_element_type=F32)
            dkey = more_k if dkey is None else dkey + more_k
            dvalue = more_v if dvalue is None else dvalue + more_v
            turned = ktr[slot, h * HDIM : (h + 1) * HDIM, :]
            out.append(dqs[h] + jnp.dot(turned, low, preferred_element_type=F32))
        dk[slot] += dkey
        dv[slot] += dvalue
        return tuple(out)

    def finish(dqs):
        whole = jnp.concatenate(dqs, axis=0) if sh.hp > 1 else dqs[0]
        return whole.T * (HDIM**-0.5)

    first_dq = tuple(jnp.zeros((HDIM, TILE), F32) for _ in range(sh.hp))

    def prompt_unit(i, _):
        g, qt = i // sh.tiles, lax.rem(i, sh.tiles)
        q = prompt_rows_of(sh, x_ref, g, qt, 0) * BF(HDIM**-0.5)
        do = prompt_rows_of(sh, do_ref, g, qt, 0)
        qh = [only_head(sh, h, q) for h in range(sh.hp)]
        doh = [only_head(sh, h, do) for h in range(sh.hp)]
        inner = inner_terms(i, do)
        lse = [lse_ref[i, h : h + 1, :] for h in range(sh.hp)]

        def body(kt, dqs):
            return grads_tile(g, kt, qh, doh, lse, inner, 2 * (qt - kt) + 1, 1, dqs)

        dqs = lax.fori_loop(0, qt + 1, body, first_dq)
        put_prompt_rows(sh, dx_ref, g, qt, 0, finish(dqs))
        return 0

    lax.fori_loop(0, G_LINE * sh.tiles, prompt_unit, 0)

    def cont_unit(i, _):
        conts = [perm[2 * i], perm[2 * i + 1]]
        unit = G_LINE * sh.tiles + i
        g = i // sh.prompt_pairs
        q = jnp.concatenate([cont_rows_of(sh, x_ref, c, 0) for c in conts], axis=0)
        q = q * BF(HDIM**-0.5)
        do = jnp.concatenate([cont_rows_of(sh, do_ref, c, 0) for c in conts], axis=0)
        qh = [only_head(sh, h, q) for h in range(sh.hp)]
        doh = [only_head(sh, h, do) for h in range(sh.hp)]
        inner = inner_terms(unit, do)
        lse = [lse_ref[unit, h : h + 1, :] for h in range(sh.hp)]

        def body(kt, dqs):
            return grads_tile(g, kt, qh, doh, lse, inner, SPAN_BLOCKS - 2 * kt, 0, dqs)

        dqs = lax.fori_loop(0, sh.tiles, body, first_dq)
        more = [[None] * 2 for _ in range(sh.hp)]
        for b in range(2):
            cols = slice(b * HALF, (b + 1) * HALF)
            keys = cont_rows_of(sh, x_ref, conts[b], 1)
            values = cont_rows_of(sh, x_ref, conts[b], 2)
            dkey = dvalue = None
            for h in range(sh.hp):
                s = lax.dot_general(keys, qh[h][cols], NT, preferred_element_type=F32)
                dp = lax.dot_general(values, doh[h][cols], NT, preferred_element_type=F32)
                p = jnp.exp2(s * LOG2E + bias[h, 1] - lse[h][:, cols])
                ds = p * (dp - inner[h][:, cols])
                dbias[h, 1] += ds
                low = ds.astype(BF)
                more_k = jnp.dot(low, qh[h][cols], preferred_element_type=F32)
                more_v = jnp.dot(p.astype(BF), doh[h][cols], preferred_element_type=F32)
                dkey = more_k if dkey is None else dkey + more_k
                dvalue = more_v if dvalue is None else dvalue + more_v
                turned = ktc[conts[b], h * HDIM : (h + 1) * HDIM, :]
                more[h][b] = jnp.dot(turned, low, preferred_element_type=F32)
            w = sh.width
            dx_ref[conts[b], G_LINE * sh.part :, w : 2 * w] = dkey.astype(BF)
            dx_ref[conts[b], G_LINE * sh.part :, 2 * w :] = dvalue.astype(BF)
        dqs = [dqs[h] + jnp.concatenate(more[h], axis=1) for h in range(sh.hp)]
        done = finish(dqs)
        for b in range(2):
            dx_ref[conts[b], G_LINE * sh.part :, : sh.width] = done[
                b * HALF : (b + 1) * HALF
            ].astype(BF)
        return 0

    lax.fori_loop(0, sh.pairs, cont_unit, 0)

    def put_keys(i, _):
        g, t = i // sh.tiles, lax.rem(i, sh.tiles)
        put_prompt_rows(sh, dx_ref, g, t, 1, dk[i])
        put_prompt_rows(sh, dx_ref, g, t, 2, dv[i])
        return 0

    lax.fori_loop(0, G_LINE * sh.tiles, put_keys, 0)

    bucket = bucket_ref[...]
    key_row = lax.broadcasted_iota(jnp.int32, (HALF, 2 * HALF), 0)
    for h in range(sh.hp):
        spread = []
        for n in range(SPAN_BLOCKS):
            wide = jnp.concatenate(
                [jnp.zeros((HALF, HALF), F32), dbias[h, 1 + n]], axis=1
            )
            for bit in range(7):
                moved = pltpu.roll(wide, 2 * HALF - (1 << bit), 1)
                wide = jnp.where((key_row & (1 << bit)) != 0, moved, wide)
            spread.append(jnp.sum(wide, axis=0, keepdims=True))
        rows = []
        for n in range(SPAN_BLOCKS):
            row = spread[n][:, HALF:]
            if n + 1 < SPAN_BLOCKS:
                row = row + spread[n + 1][:, :HALF]
            rows.append(row)
        by_dist = jnp.concatenate(rows, axis=0)
        sums = [
            jnp.sum(jnp.where(bucket == b, by_dist, 0.0), axis=0, keepdims=True)
            for b in range(BUCKETS)
        ]
        lanes = jnp.concatenate(sums, axis=0)
        dtable_ref[h * BUCKETS : (h + 1) * BUCKETS, :] = jnp.broadcast_to(
            jnp.sum(lanes, axis=1, keepdims=True), (BUCKETS, HALF)
        )


SMEM_SPEC = pl.BlockSpec(memory_space=pltpu.SMEM)
VMEM_SPEC = pl.BlockSpec(memory_space=pltpu.VMEM)
GRANT = 48 * 1024 * 1024


def attend_forward(sh, group, table, bucket, x):
    return pl.pallas_call(
        functools.partial(attn_forward_kernel, sh),
        out_shape=(
            jax.ShapeDtypeStruct((sh.srcs, sh.rows, sh.width), BF),
            jax.ShapeDtypeStruct((sh.units, sh.width, TILE), F32),
            jax.ShapeDtypeStruct((sh.units, 8, TILE), F32),
        ),
        in_specs=[SMEM_SPEC, SMEM_SPEC, VMEM_SPEC, VMEM_SPEC],
        out_specs=(VMEM_SPEC, VMEM_SPEC, VMEM_SPEC),
        scratch_shapes=[
            pltpu.VMEM((sh.hp, SPAN_BLOCKS + 1, HALF, HALF), F32),
            pltpu.VMEM((G_LINE * sh.tiles, sh.width, TILE), BF),
            pltpu.VMEM((sh.srcs, sh.width, HALF), BF),
            pltpu.VMEM((sh.hp, PLEN, TILE), F32),
            pltpu.SMEM((sh.srcs,), jnp.int32),
        ],
        compiler_params=pltpu.CompilerParams(vmem_limit_bytes=GRANT),
        cost_estimate=pl.CostEstimate(
            flops=10**10, bytes_accessed=8 * 10**6, transcendentals=5 * 10**6
        ),
        name="attend_forward",
    )(group, table, bucket, x)


def attend_backward(sh, group, table, bucket, x, do, ot, lse):
    return pl.pallas_call(
        functools.partial(attn_backward_kernel, sh),
        out_shape=(
            jax.ShapeDtypeStruct((sh.srcs, sh.rows, 3 * sh.width), BF),
            jax.ShapeDtypeStruct((sh.hp * BUCKETS, HALF), F32),
        ),
        in_specs=[SMEM_SPEC, SMEM_SPEC, VMEM_SPEC, VMEM_SPEC, VMEM_SPEC, VMEM_SPEC, VMEM_SPEC],
        out_specs=(VMEM_SPEC, VMEM_SPEC),
        scratch_shapes=[
            pltpu.VMEM((sh.hp, SPAN_BLOCKS + 1, HALF, HALF), F32),
            pltpu.VMEM((sh.hp, SPAN_BLOCKS + 1, HALF, HALF), F32),
            pltpu.VMEM((G_LINE * sh.tiles, sh.width, TILE), BF),
            pltpu.VMEM((sh.srcs, sh.width, HALF), BF),
            pltpu.VMEM((G_LINE * sh.tiles, TILE, sh.width), F32),
            pltpu.VMEM((G_LINE * sh.tiles, TILE, sh.width), F32),
            pltpu.SMEM((sh.srcs,), jnp.int32),
        ],
        compiler_params=pltpu.CompilerParams(vmem_limit_bytes=GRANT),
        cost_estimate=pl.CostEstimate(
            flops=2 * 10**10, bytes_accessed=12 * 10**6, transcendentals=5 * 10**6
        ),
        name="attend_backward",
    )(group, table, bucket, x, do, ot, lse)


def ring_order(count):
    deep, wide = 4, count // 4
    order = [a * wide for a in range(deep)]
    for turn, a in enumerate(reversed(range(deep))):
        row = [a * wide + b for b in range(1, wide)]
        order += row if turn % 2 == 0 else row[::-1]
    return order


def ring_hop(x, count, step):
    ring = ring_order(count)
    return lax.ppermute(x, "fsdp", [(ring[i], ring[(i + step) % count]) for i in range(count)])


def ring_gather(x, count):
    chunks = [None] * count
    chunks[0] = x
    right = left = x
    for s in range(1, count // 2 + 1):
        right = ring_hop(right, count, 1)
        chunks[count - s] = right
        if s < count // 2:
            left = ring_hop(left, count, -1)
            chunks[s] = left
    return chunks


def ring_scatter(part, count):
    right = part(count - 1, 0).astype(BF)
    left = part(1, 1).astype(BF)
    for s in range(1, count):
        right = ring_hop(right, count, 1)
        left = ring_hop(left, count, -1)
        right = right.astype(F32) + part(count - 1 - s, 0).astype(F32)
        left = left.astype(F32) + part((1 + s) % count, 1).astype(F32)
        if s < count - 1:
            right, left = right.astype(BF), left.astype(BF)
    return right, left


def local(
    inputs,
    w_qkv,
    w_out,
    attn_gain,
    moe_gain,
    w_router,
    bias_table,
    w_gate,
    w_up,
    w_down,
    routes,
    slot_order,
    group_map,
    buckets,
    grad_output,
):
    tok_count = inputs.shape[0]
    expert_count = w_router.shape[1]
    capacity = (5 * TOPK * tok_count + 4 * expert_count - 1) // (4 * expert_count)
    fsdp_count = lax.axis_size("fsdp")
    fsdp_place = lax.axis_index("fsdp")
    expert_place = lax.axis_index("expert")
    group_count = lax.axis_size("expert") * fsdp_count
    sh = Shape(fsdp_count)
    prompt_rows = sh.part * G_LINE
    slot_total = expert_count * capacity
    shard = w_qkv.shape[0]
    ff_shard = w_down.shape[1]

    def by_prompt(x):
        head = x[:prompt_rows].reshape(sh.part, G_LINE, -1).transpose(1, 0, 2)
        return jnp.concatenate([head.reshape(prompt_rows, -1), x[prompt_rows:]], 0)

    def by_token(x):
        head = x[:prompt_rows].reshape(G_LINE, sh.part, -1).transpose(1, 0, 2)
        return jnp.concatenate([head.reshape(prompt_rows, -1), x[prompt_rows:]], 0)

    small = jnp.concatenate(
        [attn_gain, moe_gain, w_router.reshape(-1), bias_table, group_map.astype(BF)]
    )
    small_rows = -(-small.shape[0] // D)
    small_rows = -(-small_rows // 16) * 16
    small = jnp.pad(small, (0, small_rows * D - small.shape[0])).reshape(small_rows, D)
    pack = jnp.concatenate([w_qkv[:, i * D : (i + 1) * D] for i in range(3)] + [w_out, small], 0)
    gathered = lax.all_gather(pack, ("expert", "fsdp"), axis=0, tiled=False)
    qkv_full = jnp.concatenate(
        [gathered[:, i * shard : (i + 1) * shard].reshape(D, D) for i in range(3)], 1
    )
    out_full = gathered[:, 3 * shard : 4 * shard].reshape(D, D)
    tail = gathered[:, 4 * shard]
    marks = [0, shard, 2 * shard, 2 * shard + shard * expert_count]
    marks += [marks[-1] + bias_table.shape[0]]
    attn_scale = tail[:, marks[0] : marks[1]].reshape(D).astype(F32)
    moe_scale = tail[:, marks[1] : marks[2]].reshape(D).astype(F32)
    router = tail[:, marks[2] : marks[3]].reshape(D, expert_count).astype(F32)
    table = tail[:, marks[3] : marks[4]].reshape(fsdp_count, sh.hp, BUCKETS)
    my_table = lax.dynamic_index_in_dim(table, fsdp_place, 0, keepdims=False).astype(F32)
    groups = tail[:, marks[4]].reshape(-1, fsdp_count)
    my_groups = lax.dynamic_index_in_dim(groups, expert_place, 0, keepdims=False)
    my_groups = my_groups.astype(jnp.int32)
    bucket = buckets.reshape(SPAN_BLOCKS, HALF)

    gate_chunks = ring_gather(w_gate[0].T, fsdp_count)
    up_chunks = ring_gather(w_up[0].T, fsdp_count)
    down_chunks = ring_gather(w_down[0], fsdp_count)

    token_input = by_prompt(inputs)
    grad_rows_low = by_prompt(grad_output)
    routes = by_prompt(routes)
    slot_order = by_prompt(slot_order)

    input_float = token_input.astype(F32)
    normed, first_pull = jax.vjp(rms_scale, input_float, attn_scale)
    normed_low = normed.astype(BF)
    qkv_rows = jnp.dot(normed_low, qkv_full, preferred_element_type=F32).astype(BF)
    by_heads = (
        qkv_rows.reshape(tok_count, 3, fsdp_count, sh.width)
        .transpose(2, 0, 1, 3)
        .reshape(fsdp_count, tok_count, 3 * sh.width)
    )
    head_qkv = lax.all_to_all(by_heads, "fsdp", split_axis=0, concat_axis=0, tiled=True)
    head_att, att_turned, att_lse = attend_forward(sh, my_groups, my_table, bucket, head_qkv)
    att_back = lax.all_to_all(head_att, "fsdp", split_axis=0, concat_axis=0, tiled=True)
    attn_low = att_back.transpose(1, 0, 2).reshape(tok_count, D)

    middle = input_float + jnp.dot(attn_low, out_full, preferred_element_type=F32)
    second_normed, second_pull = jax.vjp(rms_scale, middle, moe_scale)
    (gate_pair, losses), router_pull = jax.vjp(
        lambda normed_rows, router_rows: route_local(normed_rows, router_rows, routes),
        second_normed,
        router,
    )
    kept_mask = (slot_order < capacity).astype(F32)
    gate_kept = gate_pair * kept_mask
    slot_ids = jnp.arange(slot_total, dtype=jnp.int32)
    slot_place = jnp.where(slot_order < capacity, routes * capacity + slot_order, -1)
    hot = [slot_place[:, k : k + 1] == slot_ids[None, :] for k in range(TOPK)]
    any_low = (hot[0] | hot[1]).astype(BF)
    outgoing = lax.dot_general(
        any_low, second_normed.astype(BF), TN, preferred_element_type=F32
    ).astype(BF)

    def swap_experts(rows):
        rows = rows.reshape(expert_count, capacity, D)
        rows = lax.all_to_all(rows, "expert", split_axis=0, concat_axis=0, tiled=True)
        return rows.reshape(slot_total, D)

    expert_rows = swap_experts(outgoing)
    slot_gate = jnp.sum(
        jnp.where(hot[0], gate_kept[:, 0:1], 0.0) + jnp.where(hot[1], gate_kept[:, 1:2], 0.0),
        axis=0,
    )
    slot_grad = lax.dot_general(any_low, grad_rows_low, TN, preferred_element_type=F32)
    grad_result = swap_experts((slot_gate[:, None] * slot_grad).astype(BF))

    gate_whole = jnp.concatenate(gate_chunks, 0)
    up_whole = jnp.concatenate(up_chunks, 0)
    down_whole = jnp.concatenate(down_chunks, 0)
    gate_pre = lax.dot_general(expert_rows, gate_whole, NT, preferred_element_type=F32)
    up_pre = lax.dot_general(expert_rows, up_whole, NT, preferred_element_type=F32)
    hidden = gated_unit(gate_pre, up_pre).astype(BF)
    result_rows = jnp.dot(hidden, down_whole, preferred_element_type=F32).astype(BF)
    returned = swap_experts(result_rows)

    grad_hidden = lax.dot_general(grad_result, down_whole, NT, preferred_element_type=F32)
    grad_gate_pre, grad_up_pre = activation_grads(gate_pre, up_pre, grad_hidden)
    grad_rows = jnp.dot(grad_gate_pre, gate_whole, preferred_element_type=F32) + jnp.dot(
        grad_up_pre, up_whole, preferred_element_type=F32
    )
    grad_sent = swap_experts(grad_rows.astype(BF))
    down_total = lax.dot_general(hidden, grad_result, TN, preferred_element_type=F32).astype(BF)
    gate_total = lax.dot_general(
        grad_gate_pre, expert_rows, TN, preferred_element_type=F32
    ).astype(BF)
    up_total = lax.dot_general(grad_up_pre, expert_rows, TN, preferred_element_type=F32).astype(BF)

    half_shard = ff_shard // 2

    def shares(total):
        def part(k, half):
            start = k * ff_shard + half * half_shard
            return total[start : start + half_shard]

        return jnp.concatenate(ring_scatter(part, fsdp_count), 0)

    grad_down = shares(down_total)
    grad_gate = shares(gate_total).T
    grad_up = shares(up_total).T

    picked = [
        jnp.dot(h.astype(BF), returned, preferred_element_type=F32) for h in hot
    ]
    block_out = middle + gate_kept[:, 0:1] * picked[0] + gate_kept[:, 1:2] * picked[1]
    output = by_token(block_out.astype(BF))
    grad_final = grad_rows_low.astype(F32)
    grad_pair = (
        jnp.stack([jnp.sum(grad_final * p, axis=-1) for p in picked], -1) * kept_mask
    )
    grad_second = jnp.dot(any_low, grad_sent, preferred_element_type=F32)
    loss_weights = jnp.array([ZLOSS_FACTOR, BALANCE_FACTOR], F32) / group_count
    router_normed, grad_router = router_pull((grad_pair, loss_weights))
    grad_middle_part, grad_moe_gain = second_pull(grad_second + router_normed)
    grad_middle = grad_final + grad_middle_part
    grad_branch = grad_middle.astype(BF)
    grad_attn = lax.dot_general(grad_branch, out_full, NT, preferred_element_type=F32).astype(BF)
    head_grad = (
        grad_attn.reshape(tok_count, fsdp_count, sh.width).transpose(1, 0, 2)
    )
    head_grad = lax.all_to_all(head_grad, "fsdp", split_axis=0, concat_axis=0, tiled=True)
    head_dqkv, head_table = attend_backward(
        sh, my_groups, my_table, bucket, head_qkv, head_grad, att_turned, att_lse
    )
    back_dqkv = lax.all_to_all(head_dqkv, "fsdp", split_axis=0, concat_axis=0, tiled=True)
    grad_qkv = (
        back_dqkv.reshape(fsdp_count, tok_count, 3, sh.width)
        .transpose(1, 2, 0, 3)
        .reshape(tok_count, 3 * D)
    )
    grad_out_w = lax.dot_general(attn_low, grad_branch, TN, preferred_element_type=F32)
    grad_qkv_w = lax.dot_general(normed_low, grad_qkv, TN, preferred_element_type=F32)
    grad_normed = lax.dot_general(grad_qkv, qkv_full, NT, preferred_element_type=F32)
    grad_input_part, grad_attn_gain = first_pull(grad_normed)
    grad_inputs = by_token(grad_middle + grad_input_part)

    def rows_of(x):
        return x.astype(BF).reshape(group_count, shard, -1)

    def small_block(parts):
        flat = jnp.concatenate([p.astype(BF).reshape(group_count, -1) for p in parts], 1)
        flat = jnp.pad(flat, ((0, 0), (0, 16 * D - flat.shape[1])))
        return flat.reshape(group_count, 16, D)

    def sum_shards(parts):
        whole = jnp.concatenate(parts, 1)
        count = whole.shape[1]
        flat = whole.reshape(group_count * count, D)
        return lax.psum_scatter(
            flat, ("expert", "fsdp"), scatter_dimension=0, tiled=True
        ).astype(F32)

    early = sum_shards([rows_of(grad_out_w), small_block([grad_moe_gain, grad_router])])
    sum_out = early[:shard]
    sum_moe = early[shard, :shard]
    sum_router = early[shard, shard : shard + shard * expert_count].reshape(shard, expert_count)
    place_table = (jnp.arange(fsdp_count) == fsdp_place).astype(F32)
    whole_table = place_table[:, None] * head_table[:, 0][None, :]
    late = sum_shards(
        [rows_of(grad_qkv_w[:, i * D : (i + 1) * D]) for i in range(3)]
        + [small_block([grad_attn_gain, whole_table.reshape(-1)])]
    )
    sum_qkv = jnp.concatenate([late[i * shard : (i + 1) * shard] for i in range(3)], 1)
    sum_attn = late[3 * shard, :shard]
    sum_table = late[3 * shard, shard : shard + bias_table.shape[0]]
    return (
        output,
        losses[None, :],
        grad_inputs,
        sum_qkv,
        sum_out,
        sum_attn,
        sum_moe,
        sum_router,
        sum_table,
        grad_gate[None],
        grad_up[None],
        grad_down[None],
    )


def solution(mesh):
    rows = P(("expert", "fsdp"), None)
    flat = P(("expert", "fsdp"))
    cols = P("expert", None, "fsdp")
    deep = P("expert", "fsdp", None)
    in_specs = (
        rows, rows, rows, flat, flat, rows, flat, cols, cols, deep, rows, rows, flat, P(), rows,
    )
    out_specs = (rows, rows, rows, rows, rows, flat, flat, rows, flat, cols, cols, deep)
    return jax.shard_map(local, mesh=mesh, in_specs=in_specs, out_specs=out_specs, check_vma=False)
```

time: 1710 us -> 1070 us (0.63)
  waiting for transfers between devices: 993 us -> 504 us
  matrix products: 286 us -> 144 us
  starting transfers between devices: 18.5 us -> 159 us
  blocking collectives: 157 us -> 27.5 us
  Pallas kernels: 0 us -> 66.2 us
  other arithmetic: 84.8 us -> 38.7 us
  local copies, waits for them, and re-layouts: 142 us -> 103 us
    reduce_scatter x5 -> x2, waiting for transfers between devices: 582 us -> 0.01 us  [sum_shards(): lax.psum_scatter(flat, ('expert', 'fsdp'), scatter_dimension=0, tiled=True)]
    ppermute x0 -> x63, waiting for transfers between devices: none -> 324 us  [ring_hop(): lax.ppermute(x, 'fsdp', [(ring[i], ring[(i + step) % count]) for i in ran...]
    unnamed x15 -> x3, waiting for transfers between devices: 174 us -> 0.05 us
    dot_general x35 -> x20, matrix products: 277 us -> 141 us  [the longest x1 24.2 us: local(): lax.dot_general(expert_rows, gate_whole, NT, preferred_element_type=F32)]
    ppermute x0 -> x63, starting transfers between devices: none -> 126 us  [ring_hop(): lax.ppermute(x, 'fsdp', [(ring[i], ring[(i + step) % count]) for i in ran...]
    all_gather x6 -> x1, waiting for transfers between devices: 200 us -> 82.8 us  [local(): gathered = lax.all_gather(pack, ('expert', 'fsdp'), axis=0, tiled=False)]
    unnamed x2 -> x0, blocking collectives: 85.3 us -> none
    all_gather x1 -> x0, blocking collectives: 71.6 us -> none  [local(): lax.all_gather(w_router, ('expert', 'fsdp'), axis=0, tiled=True)]
  transfers between devices with their start and end apart: 17 -> 73, of which waited for: 14 -> 42; matrix products, arithmetic and copies ran while one was open for 20% -> 17% of each run, Pallas kernels for 0% -> 2%
where the time goes in v1:
time: 1070 us; the launch traced here: 1060 us
  waiting for transfers between devices  504 us (47%)
  starting transfers between devices  159 us (15%)
  matrix products  144 us (13%)
  local copies, waits for them, and re-layouts  103 us (10%)
  Pallas kernels  66.2 us (6%)
  other arithmetic  38.7 us (4%)
  blocking collectives  27.5 us (3%)
  between operations  17.2 us (2%)
    ppermute x63, waiting for transfers between devices, ring_hop(): lax.ppermute(x, 'fsdp', [(ring[i], ring[(i + step) % count]) for i in ran...  324 us
    ppermute x63, starting transfers between devices, ring_hop(): lax.ppermute(x, 'fsdp', [(ring[i], ring[(i + step) % count]) for i in ran...  126 us
    all_gather x1, waiting for transfers between devices, local(): gathered = lax.all_gather(pack, ('expert', 'fsdp'), axis=0, tiled=False)  82.8 us
    unnamed x119, local copies, waits for them, and re-layouts  50.7 us
    all_to_all x4, waiting for transfers between devices, swap_experts(): lax.all_to_all(rows, 'expert', split_axis=0, concat_axis=0, tiled=True)  50.4 us
    all_to_all x1, waiting for transfers between devices, local(): lax.all_to_all(head_dqkv, 'fsdp', split_axis=0, concat_axis=0, tiled=True)  46.4 us
    pallas_call x1, Pallas kernels, attend_backward(): pl.pallas_call(functools.partial(attn_backward_kernel, sh), out_shape=(ja...  43.1 us
    all_to_all x1, blocking collectives, local(): lax.all_to_all(head_grad, 'fsdp', split_axis=0, concat_axis=0, tiled=True)  27.5 us
  transfers between devices with their start and end apart: 73, of which 42 were waited for; matrix products, arithmetic and copies ran while one was open for 17% of the time, Pallas kernels for 2%

profile of v1, /device:TPU:0, one launch (start us, length us, event | category | flops | bytes accessed | tf_op | source)
XLA Modules:
  0.0 1060.0 jit_solution(14976730490608543486)
XLA Ops:
  16.7 82.8 %all-gather.3.cloned.1.call-done = bf16[4608,1024]{1,0:T(8,128)(2,1)} async-done(((bf16[144,1024]{1,0:T(8,128)(2,1)}), bf16[4608,1024]{1,0:T(8,128)(2,1)}) %all-gather.3.cloned.1.call-update) | async-done | bytes 9437200 | tf_op jit(solution)/shard_map/all_gather | solution.py:609
  100.6 5.8 fusion.69
  107.7 4.9 fusion.14
  138.7 42.0 %collective-permute-done.3 = bf16[352,1024]{1,0:T(8,128)(2,1)} collective-permute-done((bf16[352,1024]{1,0:T(8,128)(2,1)}, bf16[352,1024]{1,0:T(8,128)(2,1)}, u32[]{:S(2)}, u32[]{:S(2)}) %collective-permute-start.3) | collective-permute-done | bytes 720928 | tf_op jit(solution)/shard_map/ppermute | solution.py:535
  187.5 10.7 %collective-permute-start.4 = (bf16[352,1024]{1,0:T(8,128)(2,1)}, bf16[352,1024]{1,0:T(8,128)(2,1)}, u32[]{:S(2)}, u32[]{:S(2)}) collective-permute-start(bf16[352,1024]{1,0:T(8,128)(2,1)} %collective-permute-done.3), channel_id=1, source_target_pairs={{0,2},{2,4},{4,6},{6,7},{7,5},{5,3},{3,1},{1,0},{8,10},{10,12},{12... | collective-permute-start | bytes 2162696 | tf_op jit(solution)/shard_map/ppermute | solution.py:535
  201.7 9.8 collective-permute-start.11
  214.3 12.5 %collective-permute-start.18 = (bf16[352,1024]{1,0:T(8,128)(2,1)}, bf16[352,1024]{1,0:T(8,128)(2,1)}, u32[]{:S(2)}, u32[]{:S(2)}) collective-permute-start(bf16[352,1024]{1,0:T(8,128)(2,1)} %collective-permute-done.17), channel_id=1, source_target_pairs={{0,2},{2,4},{4,6},{6,7},{7,5},{5,3},{3,1},{1,0},{8,10},{10,12},{12... | collective-permute-start | bytes 2162696 | tf_op jit(solution)/shard_map/ppermute | solution.py:535
  232.0 10.3 collective-permute-start.5
  245.2 12.7 %collective-permute-start.12 = (bf16[352,1024]{1,0:T(8,128)(2,1)}, bf16[352,1024]{1,0:T(8,128)(2,1)}, u32[]{:S(2)}, u32[]{:S(2)}) collective-permute-start(bf16[352,1024]{1,0:T(8,128)(2,1)} %collective-permute-done.11), channel_id=1, source_target_pairs={{0,2},{2,4},{4,6},{6,7},{7,5},{5,3},{3,1},{1,0},{8,10},{10,12},{12... | collective-permute-start | bytes 2162696 | tf_op jit(solution)/shard_map/ppermute | solution.py:535
  257.9 13.3 %collective-permute-start.19 = (bf16[352,1024]{1,0:T(8,128)(2,1)}, bf16[352,1024]{1,0:T(8,128)(2,1)}, u32[]{:S(2)}, u32[]{:S(2)}) collective-permute-start(bf16[352,1024]{1,0:T(8,128)(2,1)} %collective-permute-done.18), channel_id=1, source_target_pairs={{0,2},{2,4},{4,6},{6,7},{7,5},{5,3},{3,1},{1,0},{8,10},{10,12},{12... | collective-permute-start | bytes 2162696 | tf_op jit(solution)/shard_map/ppermute | solution.py:535
  271.3 23.1 %attend_forward.1 = (bf16[8,384,128]{2,1,0:T(8,128)(2,1)}, f32[12,128,256]{2,1,0:T(8,128)S(1)}, f32[12,8,256]{2,1,0:T(8,128)S(1)}) custom-call(s32[8]{0:T(128)S(1)} %bitcast_convert_fusion.1.group_ref, f32[2,32]{1,0:T(2,128)S(1)} %bitcast_convert_fusion.table_ref, s32[9,128]{1,0:T(8,128)S(1)} %bitcast.128, bf16[8,384,384]{2,1,0:T(8,128)(2,1)S(1)} %all-to-all-done.x_ref), custom_call_target="tpu_custom_call" | custom-call | flops 10000000000 | bytes 8000000 | tf_op jit(solution)/shard_map/attend_forward/pallas_call | solution.py:474
  295.6 5.7 all-to-all-start.1
  314.5 12.0 %collective-permute-start.20 = (bf16[352,1024]{1,0:T(8,128)(2,1)}, bf16[352,1024]{1,0:T(8,128)(2,1)}, u32[]{:S(2)}, u32[]{:S(2)}) collective-permute-start(bf16[352,1024]{1,0:T(8,128)(2,1)} %collective-permute-done.19), channel_id=1, source_target_pairs={{0,2},{2,4},{4,6},{6,7},{7,5},{5,3},{3,1},{1,0},{8,10},{10,12},{12... | collective-permute-start | bytes 2162696 | tf_op jit(solution)/shard_map/ppermute | solution.py:535
  333.8 12.2 %collective-permute-done.16 = bf16[352,1024]{1,0:T(8,128)(2,1)S(1)} collective-permute-done((bf16[352,1024]{1,0:T(8,128)(2,1)}, bf16[352,1024]{1,0:T(8,128)(2,1)S(1)}, u32[]{:S(2)}, u32[]{:S(2)}) %collective-permute-start.16) | collective-permute-done | bytes 720928 | tf_op jit(solution)/shard_map/ppermute | solution.py:535
  390.2 4.6 all-to-all-start.2
  394.8 11.3 %fusion.77 = f32[960,2816]{1,0:T(8,128)} fusion(bf16[960,1024]{1,0:T(8,128)(2,1)} %bitcast.38, bf16[2816,1024]{1,0:T(8,128)(2,1)} %constant_dynamic-update-slice_fusion.18), kind=kOutput, calls=%fused_computation.244 | convolution fusion | flops 5536481280 | bytes 18546688 | tf_op jit(solution)/shard_map/dot_general | solution.py:689
  406.2 13.0 %all-to-all-done.2 = bf16[4,240,1024]{2,1,0:T(8,128)(2,1)} async-done(((bf16[4,240,1024]{2,1,0:T(8,128)(2,1)}), bf16[4,240,1024]{2,1,0:T(8,128)(2,1)}, u32[]{:S(2)}, u32[]{:S(2)}) %all-to-all-start.2) | async-done | bytes 1966112 | tf_op jit(solution)/shard_map/all_to_all | solution.py:669
  419.1 11.3 %fusion.76 = f32[960,2816]{1,0:T(8,128)} fusion(bf16[960,1024]{1,0:T(8,128)(2,1)} %bitcast.20, bf16[2816,1024]{1,0:T(8,128)(2,1)} %constant_dynamic-update-slice_fusion.10), kind=kOutput, calls=%fused_computation.243 | convolution fusion | flops 5536481280 | bytes 18546688 | tf_op jit(solution)/shard_map/dot_general | solution.py:684
  430.5 24.2 %fusion.6 = (bf16[960,2816]{1,0:T(8,128)(2,1)}, bf16[960,2816]{1,0:T(8,128)(2,1)}, bf16[960,2816]{1,0:T(8,128)(2,1)}) fusion(f32[960,2816]{1,0:T(8,128)} %fusion.77, f32[960,2816]{1,0:T(8,128)} %fusion.76, bf16[960,1024]{1,0:T(8,128)(2,1)} %bitcast.20, bf16[2816,1024]{1,0:T(8,128)(2,1)} %constant_dynamic-update-slice_fusion.2), kind=kOutput, calls=%fused_computation.8 | convolution fusion | flops 5606768640 | bytes 45580288 | tf_op jit(solution)/shard_map/dot_general | solution.py:683
  454.7 9.7 fusion.78
  464.4 8.7 add_convert_fusion
  477.6 10.4 convolution_convert_fusion.7
  487.9 14.0 %all-to-all-done.5 = bf16[4,240,1024]{2,1,0:T(8,128)(2,1)} async-done(((bf16[4,240,1024]{2,1,0:T(8,128)(2,1)}), bf16[4,240,1024]{2,1,0:T(8,128)(2,1)}, u32[]{:S(2)}, u32[]{:S(2)}) %all-to-all-start.5) | async-done | bytes 1966112 | tf_op jit(solution)/shard_map/all_to_all | solution.py:669
  510.6 20.0 %all-to-all-done.3 = bf16[4,240,1024]{2,1,0:T(8,128)(2,1)} async-done(((bf16[4,240,1024]{2,1,0:T(8,128)(2,1)}), bf16[4,240,1024]{2,1,0:T(8,128)(2,1)}, u32[]{:S(2)}, u32[]{:S(2)}) %all-to-all-start.3) | async-done | bytes 1966112 | tf_op jit(solution)/shard_map/all_to_all | solution.py:669
  545.4 27.5 %all_to_all.40.do_ref = bf16[8,384,128]{2,1,0:T(8,128)(2,1)S(1)} all-to-all(bf16[8,384,128]{2,1,0:T(8,128)(2,1)} %bitcast.158), channel_id=1, replica_groups=mesh['expert'=4,'fsdp'=8] {'fsdp'}, dimensions={0} | all-to-all | bytes 1572864 | tf_op jit(solution)/shard_map/all_to_all | solution.py:733
  572.9 43.1 %attend_backward.1 = (bf16[8,384,384]{2,1,0:T(8,128)(2,1)}, f32[64,128]{1,0:T(8,128)S(1)}) custom-call(s32[8]{0:T(128)S(1)} %bitcast_convert_fusion.1.group_ref, f32[2,32]{1,0:T(2,128)S(1)} %bitcast_convert_fusion.table_ref, s32[9,128]{1,0:T(8,128)S(1)} %bitcast.129, bf16[8,384,384]{2,1,0:T(8,128)(2,1)} %copy-done, ...), custom_call_target="tpu_custom_call" | custom-call | flops 20000000000 | bytes 12000000 | tf_op jit(solution)/shard_map/attend_backward/pallas_call | solution.py:499
  627.0 46.4 %all-to-all-done.7 = bf16[8,384,384]{2,1,0:T(8,128)(2,1)} async-done(((bf16[8,384,384]{2,1,0:T(8,128)(2,1)}), bf16[8,384,384]{2,1,0:T(8,128)(2,1)}, u32[]{:S(2)}, u32[]{:S(2)}) %all-to-all-start.7) | async-done | bytes 2359328 | tf_op jit(solution)/shard_map/all_to_all | solution.py:737
  681.0 5.2 fusion.16
  698.2 9.3 convolution_convert_fusion.1
  709.6 10.7 %convolution_convert_fusion.2 = bf16[2816,1024]{1,0:T(8,128)(2,1)S(1)} fusion(bf16[960,2816]{1,0:T(8,128)(2,1)} %get-tuple-element.92, bf16[960,1024]{1,0:T(8,128)(2,1)} %bitcast.20), kind=kOutput, calls=%fused_computation.16 | convolution fusion | flops 5539364864 | bytes 13139968 | tf_op jit(solution)/shard_map/dot_general | solution.py:696
  720.3 9.5 convolution_convert_fusion
  734.5 10.4 collective-permute-done.21
  745.0 5.6 collective-permute-done.28
  750.9 18.0 %collective-permute-done.49 = bf16[176,1024]{1,0:T(8,128)(2,1)S(1)} collective-permute-done((bf16[176,1024]{1,0:T(8,128)(2,1)S(1)}, bf16[176,1024]{1,0:T(8,128)(2,1)S(1)}, u32[]{:S(2)}, u32[]{:S(2)}) %collective-permute-start.49) | collective-permute-done | bytes 360480 | tf_op jit(solution)/shard_map/ppermute | solution.py:535
  773.7 18.1 %collective-permute-done.36 = bf16[176,1024]{1,0:T(8,128)(2,1)S(1)} collective-permute-done((bf16[176,1024]{1,0:T(8,128)(2,1)S(1)}, bf16[176,1024]{1,0:T(8,128)(2,1)S(1)}, u32[]{:S(2)}, u32[]{:S(2)}) %collective-permute-start.36) | collective-permute-done | bytes 360480 | tf_op jit(solution)/shard_map/ppermute | solution.py:535
  791.9 4.6 collective-permute-done.43
  796.8 18.3 %collective-permute-done.22 = bf16[176,1024]{1,0:T(8,128)(2,1)S(1)} collective-permute-done((bf16[176,1024]{1,0:T(8,128)(2,1)S(1)}, bf16[176,1024]{1,0:T(8,128)(2,1)S(1)}, u32[]{:S(2)}, u32[]{:S(2)}) %collective-permute-start.22) | collective-permute-done | bytes 360480 | tf_op jit(solution)/shard_map/ppermute | solution.py:535
  815.1 4.6 collective-permute-done.29
  820.1 18.4 %collective-permute-done.50 = bf16[176,1024]{1,0:T(8,128)(2,1)S(1)} collective-permute-done((bf16[176,1024]{1,0:T(8,128)(2,1)S(1)}, bf16[176,1024]{1,0:T(8,128)(2,1)S(1)}, u32[]{:S(2)}, u32[]{:S(2)}) %collective-permute-start.50) | collective-permute-done | bytes 360480 | tf_op jit(solution)/shard_map/ppermute | solution.py:535
  843.2 18.2 %collective-permute-done.37 = bf16[176,1024]{1,0:T(8,128)(2,1)S(1)} collective-permute-done((bf16[176,1024]{1,0:T(8,128)(2,1)S(1)}, bf16[176,1024]{1,0:T(8,128)(2,1)S(1)}, u32[]{:S(2)}, u32[]{:S(2)}) %collective-permute-start.37) | collective-permute-done | bytes 360480 | tf_op jit(solution)/shard_map/ppermute | solution.py:535
  861.4 4.8 collective-permute-done.44
  866.5 18.3 %collective-permute-done.23 = bf16[176,1024]{1,0:T(8,128)(2,1)S(1)} collective-permute-done((bf16[176,1024]{1,0:T(8,128)(2,1)S(1)}, bf16[176,1024]{1,0:T(8,128)(2,1)S(1)}, u32[]{:S(2)}, u32[]{:S(2)}) %collective-permute-start.23) | collective-permute-done | bytes 360480 | tf_op jit(solution)/shard_map/ppermute | solution.py:535
  889.6 18.0 %collective-permute-done.51 = bf16[176,1024]{1,0:T(8,128)(2,1)S(1)} collective-permute-done((bf16[176,1024]{1,0:T(8,128)(2,1)S(1)}, bf16[176,1024]{1,0:T(8,128)(2,1)S(1)}, u32[]{:S(2)}, u32[]{:S(2)}) %collective-permute-start.51) | collective-permute-done | bytes 360480 | tf_op jit(solution)/shard_map/ppermute | solution.py:535
  907.6 4.8 collective-permute-done.58
  912.8 18.3 %collective-permute-done.38 = bf16[176,1024]{1,0:T(8,128)(2,1)S(1)} collective-permute-done((bf16[176,1024]{1,0:T(8,128)(2,1)S(1)}, bf16[176,1024]{1,0:T(8,128)(2,1)S(1)}, u32[]{:S(2)}, u32[]{:S(2)}) %collective-permute-start.38) | collective-permute-done | bytes 360480 | tf_op jit(solution)/shard_map/ppermute | solution.py:535
  936.7 17.5 %collective-permute-done.24 = bf16[176,1024]{1,0:T(8,128)(2,1)S(1)} collective-permute-done((bf16[176,1024]{1,0:T(8,128)(2,1)S(1)}, bf16[176,1024]{1,0:T(8,128)(2,1)S(1)}, u32[]{:S(2)}, u32[]{:S(2)}) %collective-permute-start.24) | collective-permute-done | bytes 360480 | tf_op jit(solution)/shard_map/ppermute | solution.py:535
  959.8 11.1 %collective-permute-done.52 = bf16[176,1024]{1,0:T(8,128)(2,1)S(1)} collective-permute-done((bf16[176,1024]{1,0:T(8,128)(2,1)S(1)}, bf16[176,1024]{1,0:T(8,128)(2,1)S(1)}, u32[]{:S(2)}, u32[]{:S(2)}) %collective-permute-start.52) | collective-permute-done | bytes 360480 | tf_op jit(solution)/shard_map/ppermute | solution.py:535
  1026.3 6.4 collective-permute-done.27
  (384 shorter events, 290.5 us)
Async XLA Ops:
  7.2 92.3 %all-gather.3.cloned.1.call-start = ((), (), s32[]{:S(2)}) async-start(), calls=%async_computation.12 | async-start | bytes 9732096 | tf_op jit(solution)/shard_map/all_gather | solution.py:609
  120.4 150.9 %all-to-all-start = ((bf16[8,384,384]{2,1,0:T(8,128)(2,1)}), bf16[8,384,384]{2,1,0:T(8,128)(2,1)S(1)}, u32[]{:S(2)}, u32[]{:S(2)}) async-start(bf16[8,384,384]{2,1,0:T(8,128)(2,1)} %copy.77), calls=%async_computation | async-start | bytes 4718592 | tf_op jit(solution)/shard_map/all_to_all | solution.py:645
  124.6 56.1 %collective-permute-start.3 = (bf16[352,1024]{1,0:T(8,128)(2,1)}, bf16[352,1024]{1,0:T(8,128)(2,1)}, u32[]{:S(2)}, u32[]{:S(2)}) collective-permute-start(bf16[352,1024]{1,0:T(8,128)(2,1)} %bitcast.175), channel_id=1, source_target_pairs={{0,2},{2,4},{4,6},{6,7},{7,5},{5,3},{3,1},{1,0},{8,10},{10,12},{12... | collective-permute-start | bytes 2162696 | tf_op jit(solution)/shard_map/ppermute | solution.py:535
  126.7 60.8 %collective-permute-start = (bf16[352,1024]{1,0:T(8,128)(2,1)}, bf16[352,1024]{1,0:T(8,128)(2,1)}, u32[]{:S(2)}, u32[]{:S(2)}) collective-permute-start(bf16[352,1024]{1,0:T(8,128)(2,1)} %bitcast.176), channel_id=1, source_target_pairs={{0,1},{2,0},{4,2},{6,4},{7,6},{5,7},{3,5},{1,3},{8,9},{10,8},{12,1... | collective-permute-start | bytes 2162696 | tf_op jit(solution)/shard_map/ppermute | solution.py:535
  126.7 71.5 %collective-permute-start.10 = (bf16[352,1024]{1,0:T(8,128)(2,1)}, bf16[352,1024]{1,0:T(8,128)(2,1)}, u32[]{:S(2)}, u32[]{:S(2)}) collective-permute-start(bf16[352,1024]{1,0:T(8,128)(2,1)} %bitcast.177), channel_id=1, source_target_pairs={{0,2},{2,4},{4,6},{6,7},{7,5},{5,3},{3,1},{1,0},{8,10},{10,12},{12... | collective-permute-start | bytes 2162696 | tf_op jit(solution)/shard_map/ppermute | solution.py:535
  128.7 73.0 %collective-permute-start.7 = (bf16[352,1024]{1,0:T(8,128)(2,1)}, bf16[352,1024]{1,0:T(8,128)(2,1)}, u32[]{:S(2)}, u32[]{:S(2)}) collective-permute-start(bf16[352,1024]{1,0:T(8,128)(2,1)} %bitcast.178), channel_id=1, source_target_pairs={{0,1},{2,0},{4,2},{6,4},{7,6},{5,7},{3,5},{1,3},{8,9},{10,8},{12,1... | collective-permute-start | bytes 2162696 | tf_op jit(solution)/shard_map/ppermute | solution.py:535
  128.7 82.9 %collective-permute-start.17 = (bf16[352,1024]{1,0:T(8,128)(2,1)}, bf16[352,1024]{1,0:T(8,128)(2,1)}, u32[]{:S(2)}, u32[]{:S(2)}) collective-permute-start(bf16[352,1024]{1,0:T(8,128)(2,1)} %bitcast.179), channel_id=1, source_target_pairs={{0,2},{2,4},{4,6},{6,7},{7,5},{5,3},{3,1},{1,0},{8,10},{10,12},{12... | collective-permute-start | bytes 2162696 | tf_op jit(solution)/shard_map/ppermute | solution.py:535
  180.7 33.6 %collective-permute-start.14 = (bf16[352,1024]{1,0:T(8,128)(2,1)}, bf16[352,1024]{1,0:T(8,128)(2,1)S(1)}, u32[]{:S(2)}, u32[]{:S(2)}) collective-permute-start(bf16[352,1024]{1,0:T(8,128)(2,1)} %bitcast.180), channel_id=1, source_target_pairs={{0,1},{2,0},{4,2},{6,4},{7,6},{5,7},{3,5},{1,3},{8,9},{10,8},{12,1... | collective-permute-start | bytes 2162696 | tf_op jit(solution)/shard_map/ppermute | solution.py:535
  187.5 42.7 %collective-permute-start.4 = (bf16[352,1024]{1,0:T(8,128)(2,1)}, bf16[352,1024]{1,0:T(8,128)(2,1)}, u32[]{:S(2)}, u32[]{:S(2)}) collective-permute-start(bf16[352,1024]{1,0:T(8,128)(2,1)} %collective-permute-done.3), channel_id=1, source_target_pairs={{0,2},{2,4},{4,6},{6,7},{7,5},{5,3},{3,1},{1,0},{8,10},{10,12},{12... | collective-permute-start | bytes 2162696 | tf_op jit(solution)/shard_map/ppermute | solution.py:535
  198.2 33.9 %collective-permute-start.1 = (bf16[352,1024]{1,0:T(8,128)(2,1)}, bf16[352,1024]{1,0:T(8,128)(2,1)}, u32[]{:S(2)}, u32[]{:S(2)}) collective-permute-start(bf16[352,1024]{1,0:T(8,128)(2,1)} %collective-permute-done), channel_id=1, source_target_pairs={{0,1},{2,0},{4,2},{6,4},{7,6},{5,7},{3,5},{1,3},{8,9},{10,8},{12,1... | collective-permute-start | bytes 2162696 | tf_op jit(solution)/shard_map/ppermute | solution.py:535
  201.7 40.8 %collective-permute-start.11 = (bf16[352,1024]{1,0:T(8,128)(2,1)}, bf16[352,1024]{1,0:T(8,128)(2,1)}, u32[]{:S(2)}, u32[]{:S(2)}) collective-permute-start(bf16[352,1024]{1,0:T(8,128)(2,1)} %collective-permute-done.10), channel_id=1, source_target_pairs={{0,2},{2,4},{4,6},{6,7},{7,5},{5,3},{3,1},{1,0},{8,10},{10,12},{12... | collective-permute-start | bytes 2162696 | tf_op jit(solution)/shard_map/ppermute | solution.py:535
  211.6 33.6 %collective-permute-start.8 = (bf16[352,1024]{1,0:T(8,128)(2,1)}, bf16[352,1024]{1,0:T(8,128)(2,1)}, u32[]{:S(2)}, u32[]{:S(2)}) collective-permute-start(bf16[352,1024]{1,0:T(8,128)(2,1)} %collective-permute-done.7), channel_id=1, source_target_pairs={{0,1},{2,0},{4,2},{6,4},{7,6},{5,7},{3,5},{1,3},{8,9},{10,8},{12,1... | collective-permute-start | bytes 2162696 | tf_op jit(solution)/shard_map/ppermute | solution.py:535
  214.3 43.7 %collective-permute-start.18 = (bf16[352,1024]{1,0:T(8,128)(2,1)}, bf16[352,1024]{1,0:T(8,128)(2,1)}, u32[]{:S(2)}, u32[]{:S(2)}) collective-permute-start(bf16[352,1024]{1,0:T(8,128)(2,1)} %collective-permute-done.17), channel_id=1, source_target_pairs={{0,2},{2,4},{4,6},{6,7},{7,5},{5,3},{3,1},{1,0},{8,10},{10,12},{12... | collective-permute-start | bytes 2162696 | tf_op jit(solution)/shard_map/ppermute | solution.py:535
  230.2 71.1 %collective-permute-start.15 = (bf16[352,1024]{1,0:T(8,128)(2,1)}, bf16[352,1024]{1,0:T(8,128)(2,1)}, u32[]{:S(2)}, u32[]{:S(2)}) collective-permute-start(bf16[352,1024]{1,0:T(8,128)(2,1)} %copy-done.30), channel_id=1, source_target_pairs={{0,1},{2,0},{4,2},{6,4},{7,6},{5,7},{3,5},{1,3},{8,9},{10,8},{12,1... | collective-permute-start | bytes 2162696 | tf_op jit(solution)/shard_map/ppermute | solution.py:535
  232.0 73.3 %collective-permute-start.5 = (bf16[352,1024]{1,0:T(8,128)(2,1)}, bf16[352,1024]{1,0:T(8,128)(2,1)}, u32[]{:S(2)}, u32[]{:S(2)}) collective-permute-start(bf16[352,1024]{1,0:T(8,128)(2,1)} %collective-permute-done.4), channel_id=1, source_target_pairs={{0,2},{2,4},{4,6},{6,7},{7,5},{5,3},{3,1},{1,0},{8,10},{10,12},{12... | collective-permute-start | bytes 2162696 | tf_op jit(solution)/shard_map/ppermute | solution.py:535
  242.5 65.3 %collective-permute-start.2 = (bf16[352,1024]{1,0:T(8,128)(2,1)}, bf16[352,1024]{1,0:T(8,128)(2,1)}, u32[]{:S(2)}, u32[]{:S(2)}) collective-permute-start(bf16[352,1024]{1,0:T(8,128)(2,1)} %collective-permute-done.1), channel_id=1, source_target_pairs={{0,1},{2,0},{4,2},{6,4},{7,6},{5,7},{3,5},{1,3},{8,9},{10,8},{12,1... | collective-permute-start | bytes 2162696 | tf_op jit(solution)/shard_map/ppermute | solution.py:535
  245.2 69.3 %collective-permute-start.12 = (bf16[352,1024]{1,0:T(8,128)(2,1)}, bf16[352,1024]{1,0:T(8,128)(2,1)}, u32[]{:S(2)}, u32[]{:S(2)}) collective-permute-start(bf16[352,1024]{1,0:T(8,128)(2,1)} %collective-permute-done.11), channel_id=1, source_target_pairs={{0,2},{2,4},{4,6},{6,7},{7,5},{5,3},{3,1},{1,0},{8,10},{10,12},{12... | collective-permute-start | bytes 2162696 | tf_op jit(solution)/shard_map/ppermute | solution.py:535
  257.9 56.5 %collective-permute-start.19 = (bf16[352,1024]{1,0:T(8,128)(2,1)}, bf16[352,1024]{1,0:T(8,128)(2,1)}, u32[]{:S(2)}, u32[]{:S(2)}) collective-permute-start(bf16[352,1024]{1,0:T(8,128)(2,1)} %collective-permute-done.18), channel_id=1, source_target_pairs={{0,2},{2,4},{4,6},{6,7},{7,5},{5,3},{3,1},{1,0},{8,10},{10,12},{12... | collective-permute-start | bytes 2162696 | tf_op jit(solution)/shard_map/ppermute | solution.py:535
  295.6 57.6 %all-to-all-start.1 = ((bf16[8,384,128]{2,1,0:T(8,128)(2,1)}), bf16[8,384,128]{2,1,0:T(8,128)(2,1)S(1)}, u32[]{:S(2)}, u32[]{:S(2)}) async-start(bf16[8,384,128]{2,1,0:T(8,128)(2,1)} %get-tuple-element.17), calls=%async_computation.1 | async-start | bytes 1572864 | tf_op jit(solution)/shard_map/all_to_all | solution.py:647
  301.3 31.5 %collective-permute-start.9 = (bf16[352,1024]{1,0:T(8,128)(2,1)}, bf16[352,1024]{1,0:T(8,128)(2,1)S(1)}, u32[]{:S(2)}, u32[]{:S(2)}) collective-permute-start(bf16[352,1024]{1,0:T(8,128)(2,1)} %collective-permute-done.8), channel_id=1, source_target_pairs={{0,1},{2,0},{4,2},{6,4},{7,6},{5,7},{3,5},{1,3},{8,9},{10,8},{12,1... | collective-permute-start | bytes 2162696 | tf_op jit(solution)/shard_map/ppermute | solution.py:535
  305.3 40.6 %collective-permute-start.16 = (bf16[352,1024]{1,0:T(8,128)(2,1)}, bf16[352,1024]{1,0:T(8,128)(2,1)S(1)}, u32[]{:S(2)}, u32[]{:S(2)}) collective-permute-start(bf16[352,1024]{1,0:T(8,128)(2,1)} %collective-permute-done.15), channel_id=1, source_target_pairs={{0,1},{2,0},{4,2},{6,4},{7,6},{5,7},{3,5},{1,3},{8,9},{10,8},{12,1... | collective-permute-start | bytes 2162696 | tf_op jit(solution)/shard_map/ppermute | solution.py:535
  307.8 39.0 %collective-permute-start.6 = (bf16[352,1024]{1,0:T(8,128)(2,1)}, bf16[352,1024]{1,0:T(8,128)(2,1)S(1)}, u32[]{:S(2)}, u32[]{:S(2)}) collective-permute-start(bf16[352,1024]{1,0:T(8,128)(2,1)} %collective-permute-done.5), channel_id=1, source_target_pairs={{0,2},{2,4},{4,6},{6,7},{7,5},{5,3},{3,1},{1,0},{8,10},{10,12},{12... | collective-permute-start | bytes 2162696 | tf_op jit(solution)/shard_map/ppermute | solution.py:535
  314.4 53.5 %collective-permute-start.13 = (bf16[352,1024]{1,0:T(8,128)(2,1)}, bf16[352,1024]{1,0:T(8,128)(2,1)}, u32[]{:S(2)}, u32[]{:S(2)}) collective-permute-start(bf16[352,1024]{1,0:T(8,128)(2,1)} %collective-permute-done.12), channel_id=1, source_target_pairs={{0,2},{2,4},{4,6},{6,7},{7,5},{5,3},{3,1},{1,0},{8,10},{10,12},{12... | collective-permute-start | bytes 2162696 | tf_op jit(solution)/shard_map/ppermute | solution.py:535
  314.5 61.5 %collective-permute-start.20 = (bf16[352,1024]{1,0:T(8,128)(2,1)}, bf16[352,1024]{1,0:T(8,128)(2,1)}, u32[]{:S(2)}, u32[]{:S(2)}) collective-permute-start(bf16[352,1024]{1,0:T(8,128)(2,1)} %collective-permute-done.19), channel_id=1, source_target_pairs={{0,2},{2,4},{4,6},{6,7},{7,5},{5,3},{3,1},{1,0},{8,10},{10,12},{12... | collective-permute-start | bytes 2162696 | tf_op jit(solution)/shard_map/ppermute | solution.py:535
  616.0 57.5 %all-to-all-start.7 = ((bf16[8,384,384]{2,1,0:T(8,128)(2,1)}), bf16[8,384,384]{2,1,0:T(8,128)(2,1)}, u32[]{:S(2)}, u32[]{:S(2)}) async-start(bf16[8,384,384]{2,1,0:T(8,128)(2,1)} %get-tuple-element.20), calls=%async_computation.7 | async-start | bytes 4718592 | tf_op jit(solution)/shard_map/all_to_all | solution.py:737
  620.5 420.2 %reduce-scatter.5.cloned.1.call-start = ((), (), s32[]{:S(2)}) async-start(), calls=%async_computation.11 | async-start | bytes 3244032 | tf_op jit(solution)/shard_map/reduce_scatter | solution.py:761
  626.7 422.6 %reduce-scatter.3.cloned.1.call-start = ((), (), s32[]{:S(2)}) async-start(), calls=%async_computation.10 | async-start | bytes 7569408 | tf_op jit(solution)/shard_map/reduce_scatter | solution.py:761
  732.1 36.8 %collective-permute-start.49 = (bf16[176,1024]{1,0:T(8,128)(2,1)S(1)}, bf16[176,1024]{1,0:T(8,128)(2,1)S(1)}, u32[]{:S(2)}, u32[]{:S(2)}) collective-permute-start(bf16[176,1024]{1,0:T(8,128)(2,1)S(1)} %get-tuple-element.116), channel_id=1, source_target_pairs={{0,2},{2,4},{4,6},{6,7},{7,5},{5,3},{3,1},{1,0},{8,10},{10,12},{12... | collective-permute-start | bytes 1081352 | tf_op jit(solution)/shard_map/ppermute | solution.py:535
  732.2 41.2 %collective-permute-start.56 = (bf16[176,1024]{1,0:T(8,128)(2,1)S(1)}, bf16[176,1024]{1,0:T(8,128)(2,1)S(1)}, u32[]{:S(2)}, u32[]{:S(2)}) collective-permute-start(bf16[176,1024]{1,0:T(8,128)(2,1)S(1)} %get-tuple-element.117), channel_id=1, source_target_pairs={{0,1},{2,0},{4,2},{6,4},{7,6},{5,7},{3,5},{1,3},{8,9},{10,8},{12,1... | collective-permute-start | bytes 1081352 | tf_op jit(solution)/shard_map/ppermute | solution.py:535
  734.4 57.4 %collective-permute-start.36 = (bf16[176,1024]{1,0:T(8,128)(2,1)S(1)}, bf16[176,1024]{1,0:T(8,128)(2,1)S(1)}, u32[]{:S(2)}, u32[]{:S(2)}) collective-permute-start(bf16[176,1024]{1,0:T(8,128)(2,1)S(1)} %get-tuple-element.130), channel_id=1, source_target_pairs={{0,2},{2,4},{4,6},{6,7},{7,5},{5,3},{3,1},{1,0},{8,10},{10,12},{12... | collective-permute-start | bytes 1081352 | tf_op jit(solution)/shard_map/ppermute | solution.py:535
  745.0 51.5 %collective-permute-start.43 = (bf16[176,1024]{1,0:T(8,128)(2,1)S(1)}, bf16[176,1024]{1,0:T(8,128)(2,1)S(1)}, u32[]{:S(2)}, u32[]{:S(2)}) collective-permute-start(bf16[176,1024]{1,0:T(8,128)(2,1)S(1)} %get-tuple-element.131), channel_id=1, source_target_pairs={{0,1},{2,0},{4,2},{6,4},{7,6},{5,7},{3,5},{1,3},{8,9},{10,8},{12,1... | collective-permute-start | bytes 1081352 | tf_op jit(solution)/shard_map/ppermute | solution.py:535
  750.8 64.3 %collective-permute-start.22 = (bf16[176,1024]{1,0:T(8,128)(2,1)S(1)}, bf16[176,1024]{1,0:T(8,128)(2,1)S(1)}, u32[]{:S(2)}, u32[]{:S(2)}) collective-permute-start(bf16[176,1024]{1,0:T(8,128)(2,1)S(1)} %get-tuple-element.146), channel_id=1, source_target_pairs={{0,2},{2,4},{4,6},{6,7},{7,5},{5,3},{3,1},{1,0},{8,10},{10,12},{12... | collective-permute-start | bytes 1081352 | tf_op jit(solution)/shard_map/ppermute | solution.py:535
  768.9 50.9 %collective-permute-start.29 = (bf16[176,1024]{1,0:T(8,128)(2,1)S(1)}, bf16[176,1024]{1,0:T(8,128)(2,1)S(1)}, u32[]{:S(2)}, u32[]{:S(2)}) collective-permute-start(bf16[176,1024]{1,0:T(8,128)(2,1)S(1)} %get-tuple-element.147), channel_id=1, source_target_pairs={{0,1},{2,0},{4,2},{6,4},{7,6},{5,7},{3,5},{1,3},{8,9},{10,8},{12,1... | collective-permute-start | bytes 1081352 | tf_op jit(solution)/shard_map/ppermute | solution.py:535
  773.7 64.8 %collective-permute-start.50 = (bf16[176,1024]{1,0:T(8,128)(2,1)S(1)}, bf16[176,1024]{1,0:T(8,128)(2,1)S(1)}, u32[]{:S(2)}, u32[]{:S(2)}) collective-permute-start(bf16[176,1024]{1,0:T(8,128)(2,1)S(1)} %get-tuple-element.114), channel_id=1, source_target_pairs={{0,2},{2,4},{4,6},{6,7},{7,5},{5,3},{3,1},{1,0},{8,10},{10,12},{12... | collective-permute-start | bytes 1081352 | tf_op jit(solution)/shard_map/ppermute | solution.py:535
  791.9 51.0 %collective-permute-start.57 = (bf16[176,1024]{1,0:T(8,128)(2,1)S(1)}, bf16[176,1024]{1,0:T(8,128)(2,1)S(1)}, u32[]{:S(2)}, u32[]{:S(2)}) collective-permute-start(bf16[176,1024]{1,0:T(8,128)(2,1)S(1)} %get-tuple-element.115), channel_id=1, source_target_pairs={{0,1},{2,0},{4,2},{6,4},{7,6},{5,7},{3,5},{1,3},{8,9},{10,8},{12,1... | collective-permute-start | bytes 1081352 | tf_op jit(solution)/shard_map/ppermute | solution.py:535
  796.7 64.6 %collective-permute-start.37 = (bf16[176,1024]{1,0:T(8,128)(2,1)S(1)}, bf16[176,1024]{1,0:T(8,128)(2,1)S(1)}, u32[]{:S(2)}, u32[]{:S(2)}) collective-permute-start(bf16[176,1024]{1,0:T(8,128)(2,1)S(1)} %get-tuple-element.128), channel_id=1, source_target_pairs={{0,2},{2,4},{4,6},{6,7},{7,5},{5,3},{3,1},{1,0},{8,10},{10,12},{12... | collective-permute-start | bytes 1081352 | tf_op jit(solution)/shard_map/ppermute | solution.py:535
  815.1 51.0 %collective-permute-start.44 = (bf16[176,1024]{1,0:T(8,128)(2,1)S(1)}, bf16[176,1024]{1,0:T(8,128)(2,1)S(1)}, u32[]{:S(2)}, u32[]{:S(2)}) collective-permute-start(bf16[176,1024]{1,0:T(8,128)(2,1)S(1)} %get-tuple-element.129), channel_id=1, source_target_pairs={{0,1},{2,0},{4,2},{6,4},{7,6},{5,7},{3,5},{1,3},{8,9},{10,8},{12,1... | collective-permute-start | bytes 1081352 | tf_op jit(solution)/shard_map/ppermute | solution.py:535
  820.0 64.8 %collective-permute-start.23 = (bf16[176,1024]{1,0:T(8,128)(2,1)S(1)}, bf16[176,1024]{1,0:T(8,128)(2,1)S(1)}, u32[]{:S(2)}, u32[]{:S(2)}) collective-permute-start(bf16[176,1024]{1,0:T(8,128)(2,1)S(1)} %get-tuple-element.144), channel_id=1, source_target_pairs={{0,2},{2,4},{4,6},{6,7},{7,5},{5,3},{3,1},{1,0},{8,10},{10,12},{12... | collective-permute-start | bytes 1081352 | tf_op jit(solution)/shard_map/ppermute | solution.py:535
  838.5 50.8 %collective-permute-start.30 = (bf16[176,1024]{1,0:T(8,128)(2,1)S(1)}, bf16[176,1024]{1,0:T(8,128)(2,1)S(1)}, u32[]{:S(2)}, u32[]{:S(2)}) collective-permute-start(bf16[176,1024]{1,0:T(8,128)(2,1)S(1)} %get-tuple-element.145), channel_id=1, source_target_pairs={{0,1},{2,0},{4,2},{6,4},{7,6},{5,7},{3,5},{1,3},{8,9},{10,8},{12,1... | collective-permute-start | bytes 1081352 | tf_op jit(solution)/shard_map/ppermute | solution.py:535
  843.1 64.5 %collective-permute-start.51 = (bf16[176,1024]{1,0:T(8,128)(2,1)S(1)}, bf16[176,1024]{1,0:T(8,128)(2,1)S(1)}, u32[]{:S(2)}, u32[]{:S(2)}) collective-permute-start(bf16[176,1024]{1,0:T(8,128)(2,1)S(1)} %get-tuple-element.112), channel_id=1, source_target_pairs={{0,2},{2,4},{4,6},{6,7},{7,5},{5,3},{3,1},{1,0},{8,10},{10,12},{12... | collective-permute-start | bytes 1081352 | tf_op jit(solution)/shard_map/ppermute | solution.py:535
  861.4 51.0 %collective-permute-start.58 = (bf16[176,1024]{1,0:T(8,128)(2,1)S(1)}, bf16[176,1024]{1,0:T(8,128)(2,1)S(1)}, u32[]{:S(2)}, u32[]{:S(2)}) collective-permute-start(bf16[176,1024]{1,0:T(8,128)(2,1)S(1)} %get-tuple-element.113), channel_id=1, source_target_pairs={{0,1},{2,0},{4,2},{6,4},{7,6},{5,7},{3,5},{1,3},{8,9},{10,8},{12,1... | collective-permute-start | bytes 1081352 | tf_op jit(solution)/shard_map/ppermute | solution.py:535
  866.4 64.6 %collective-permute-start.38 = (bf16[176,1024]{1,0:T(8,128)(2,1)S(1)}, bf16[176,1024]{1,0:T(8,128)(2,1)S(1)}, u32[]{:S(2)}, u32[]{:S(2)}) collective-permute-start(bf16[176,1024]{1,0:T(8,128)(2,1)S(1)} %get-tuple-element.126), channel_id=1, source_target_pairs={{0,2},{2,4},{4,6},{6,7},{7,5},{5,3},{3,1},{1,0},{8,10},{10,12},{12... | collective-permute-start | bytes 1081352 | tf_op jit(solution)/shard_map/ppermute | solution.py:535
  884.8 50.7 %collective-permute-start.45 = (bf16[176,1024]{1,0:T(8,128)(2,1)S(1)}, bf16[176,1024]{1,0:T(8,128)(2,1)S(1)}, u32[]{:S(2)}, u32[]{:S(2)}) collective-permute-start(bf16[176,1024]{1,0:T(8,128)(2,1)S(1)} %get-tuple-element.127), channel_id=1, source_target_pairs={{0,1},{2,0},{4,2},{6,4},{7,6},{5,7},{3,5},{1,3},{8,9},{10,8},{12,1... | collective-permute-start | bytes 1081352 | tf_op jit(solution)/shard_map/ppermute | solution.py:535
  889.5 64.7 %collective-permute-start.24 = (bf16[176,1024]{1,0:T(8,128)(2,1)S(1)}, bf16[176,1024]{1,0:T(8,128)(2,1)S(1)}, u32[]{:S(2)}, u32[]{:S(2)}) collective-permute-start(bf16[176,1024]{1,0:T(8,128)(2,1)S(1)} %get-tuple-element.142), channel_id=1, source_target_pairs={{0,2},{2,4},{4,6},{6,7},{7,5},{5,3},{3,1},{1,0},{8,10},{10,12},{12... | collective-permute-start | bytes 1081352 | tf_op jit(solution)/shard_map/ppermute | solution.py:535
  907.6 51.0 %collective-permute-start.31 = (bf16[176,1024]{1,0:T(8,128)(2,1)S(1)}, bf16[176,1024]{1,0:T(8,128)(2,1)S(1)}, u32[]{:S(2)}, u32[]{:S(2)}) collective-permute-start(bf16[176,1024]{1,0:T(8,128)(2,1)S(1)} %get-tuple-element.143), channel_id=1, source_target_pairs={{0,1},{2,0},{4,2},{6,4},{7,6},{5,7},{3,5},{1,3},{8,9},{10,8},{12,1... | collective-permute-start | bytes 1081352 | tf_op jit(solution)/shard_map/ppermute | solution.py:535
  912.7 58.2 %collective-permute-start.52 = (bf16[176,1024]{1,0:T(8,128)(2,1)S(1)}, bf16[176,1024]{1,0:T(8,128)(2,1)S(1)}, u32[]{:S(2)}, u32[]{:S(2)}) collective-permute-start(bf16[176,1024]{1,0:T(8,128)(2,1)S(1)} %get-tuple-element.110), channel_id=1, source_target_pairs={{0,2},{2,4},{4,6},{6,7},{7,5},{5,3},{3,1},{1,0},{8,10},{10,12},{12... | collective-permute-start | bytes 1081352 | tf_op jit(solution)/shard_map/ppermute | solution.py:535
  931.1 39.8 %collective-permute-start.59 = (bf16[176,1024]{1,0:T(8,128)(2,1)S(1)}, bf16[176,1024]{1,0:T(8,128)(2,1)S(1)}, u32[]{:S(2)}, u32[]{:S(2)}) collective-permute-start(bf16[176,1024]{1,0:T(8,128)(2,1)S(1)} %get-tuple-element.111), channel_id=1, source_target_pairs={{0,1},{2,0},{4,2},{6,4},{7,6},{5,7},{3,5},{1,3},{8,9},{10,8},{12,1... | collective-permute-start | bytes 1081352 | tf_op jit(solution)/shard_map/ppermute | solution.py:535
  936.7 42.1 %collective-permute-start.39 = (bf16[176,1024]{1,0:T(8,128)(2,1)}, bf16[176,1024]{1,0:T(8,128)(2,1)}, u32[]{:S(2)}, u32[]{:S(2)}) collective-permute-start(bf16[176,1024]{1,0:T(8,128)(2,1)} %get-tuple-element.124), channel_id=1, source_target_pairs={{0,2},{2,4},{4,6},{6,7},{7,5},{5,3},{3,1},{1,0},{8,10},{10,12},{12... | collective-permute-start | bytes 1081352 | tf_op jit(solution)/shard_map/ppermute | solution.py:535
  (72 other events, 2466.2 us)
Sparse Core Ops, SparseCore 0:
  15.2 84.1 all-gather.2
  626.8 102.7 reduce-scatter.4
  731.9 236.6 reduce-scatter.2

commit v2 on v1

--- a/solution.py
+++ b/solution.py
@@ -535,30 +535,432 @@
     return lax.ppermute(x, "fsdp", [(ring[i], ring[(i + step) % count]) for i in range(count)])
 
 
-def ring_gather(x, count):
-    chunks = [None] * count
-    chunks[0] = x
-    right = left = x
-    for s in range(1, count // 2 + 1):
-        right = ring_hop(right, count, 1)
-        chunks[count - s] = right
-        if s < count // 2:
-            left = ring_hop(left, count, -1)
-            chunks[s] = left
-    return chunks
-
-
-def ring_scatter(part, count):
-    right = part(count - 1, 0).astype(BF)
-    left = part(1, 1).astype(BF)
-    for s in range(1, count):
-        right = ring_hop(right, count, 1)
-        left = ring_hop(left, count, -1)
-        right = right.astype(F32) + part(count - 1 - s, 0).astype(F32)
-        left = left.astype(F32) + part((1 + s) % count, 1).astype(F32)
-        if s < count - 1:
-            right, left = right.astype(BF), left.astype(BF)
-    return right, left
+def tied(*values):
+    return lax.optimization_barrier(values)
+
+
+class RingGather:
+    def __init__(self, own, count):
+        self.count = count
+        self.chunks = [None] * count
+        self.chunks[0] = own
+        self.right = self.left = own
+        self.done = 0
+        self.steps = count // 2
+
+    def step(self):
+        self.done += 1
+        s = self.done
+        if s < self.steps:
+            self.right = ring_hop(self.right, self.count, 1)
+            self.left = ring_hop(self.left, self.count, -1)
+        else:
+            half = self.right.shape[0] // 2
+            self.right = ring_hop(self.right[:half], self.count, 1)
+            self.left = ring_hop(self.left[half:], self.count, -1)
+        self.keep()
+
+    def keep(self):
+        s = self.done
+        if s < self.steps:
+            self.chunks[self.count - s] = self.right
+            self.chunks[s] = self.left
+        else:
+            self.chunks[s] = jnp.concatenate([self.right, self.left], 0)
+
+    def tie(self, value):
+        value, self.right, self.left = tied(value, self.right, self.left)
+        self.keep()
+        return value
+
+
+class RingScatter:
+    def __init__(self, part, count):
+        self.part, self.count = part, count
+        self.right = self.left = None
+        self.done = 0
+        self.steps = count // 2
+
+    def step(self):
+        count, s = self.count, self.done
+        away = self.steps - s
+        if s == 0:
+            far = self.part(away)
+            half = far.shape[0] // 2
+            send_left, send_right = far[:half], far[half:]
+        else:
+            near_left = self.part(count - away).astype(F32)
+            near_right = self.part(away).astype(F32)
+            if s == 1:
+                half = near_left.shape[0] // 2
+                send_left = jnp.concatenate(
+                    [near_left[:half] + self.left.astype(F32), near_left[half:]], 0
+                )
+                send_right = jnp.concatenate(
+                    [near_right[:half], near_right[half:] + self.right.astype(F32)], 0
+                )
+            else:
+                send_left = near_left + self.left.astype(F32)
+                send_right = near_right + self.right.astype(F32)
+        self.left = ring_hop(send_left.astype(BF), count, -1)
+        self.right = ring_hop(send_right.astype(BF), count, 1)
+        self.done += 1
+
+    def tie(self, value):
+        value, self.right, self.left = tied(value, self.right, self.left)
+        return value
+
+    def finish(self):
+        return self.part(0).astype(F32) + self.right.astype(F32) + self.left.astype(F32)
+
+
+MESH_ID = pl.DeviceIdType.MESH
+DEEP = 4
+
+
+class Spot:
+    def __init__(self):
+        e, f = lax.axis_index("expert"), lax.axis_index("fsdp")
+        self.x, self.c = e // 2, lax.rem(e, 2)
+        self.z, self.y = f // 2, lax.rem(f, 2)
+        self.ox, self.oy, self.oc = 1 - self.x, 1 - self.y, 1 - self.c
+
+    def place(self, x=None, y=None, z=None, c=None):
+        x = self.x if x is None else x
+        y = self.y if y is None else y
+        z = self.z if z is None else z
+        c = self.c if c is None else c
+        return {"expert": x * 2 + c, "fsdp": z * 2 + y}
+
+    def block(self, x, y, z, c):
+        return (x * 2 + c) * 8 + z * 2 + y
+
+    def greet(self):
+        barrier = pltpu.get_barrier_semaphore()
+        for target in (self.place(x=self.ox), self.place(y=self.oy), self.place(c=self.oc)):
+            pl.semaphore_signal(barrier, inc=1, device_id=target, device_id_type=MESH_ID)
+        for step in (-1, 1):
+
+            @pl.when(self.inside(self.z + step))
+            def _(step=step):
+                pl.semaphore_signal(
+                    barrier, inc=1, device_id=self.along(step), device_id_type=MESH_ID
+                )
+
+        pl.semaphore_wait(barrier, 4 + self.z * (DEEP - 1 - self.z) // 2)
+
+    def wrap(self, step):
+        return lax.rem(self.z + step + DEEP, DEEP)
+
+    def along(self, step):
+        return self.place(z=self.wrap(step))
+
+    def inside(self, z):
+        return (z >= 0) & (z < DEEP)
+
+
+def dense_gather_kernel(cut, x_ref, out_ref, send_sems, recv_sems, own_sem):
+    me = Spot()
+    rows = x_ref.shape[0]
+    spans = [(0, cut), (cut, rows - cut)]
+    pending = []
+
+    def view(ref, h):
+        return ref.at[pl.ds(*spans[h])]
+
+    def send(src, blk, h, target, cond):
+        copy = pltpu.make_async_remote_copy(
+            src_ref=src,
+            dst_ref=view(out_ref.at[blk], h),
+            send_sem=send_sems.at[len(pending)],
+            recv_sem=recv_sems.at[blk, h],
+            device_id=target,
+            device_id_type=MESH_ID,
+        )
+        pending.append((copy, cond))
+        if cond is None:
+            copy.start()
+        else:
+            pl.when(cond)(copy.start)
+
+    def arrive(blk, h, cond):
+        copy = pltpu.make_async_remote_copy(
+            src_ref=view(out_ref.at[blk], h),
+            dst_ref=view(out_ref.at[blk], h),
+            send_sem=send_sems.at[0],
+            recv_sem=recv_sems.at[blk, h],
+            device_id=me.place(c=me.oc),
+            device_id_type=MESH_ID,
+        )
+        if cond is None:
+            copy.wait_recv()
+        else:
+            pl.when(cond)(copy.wait_recv)
+
+    def both(a, b):
+        return b if a is None else (a if b is None else a & b)
+
+    by_y, by_x = me.place(y=me.oy), me.place(x=me.ox)
+    core = me.place(c=me.oc)
+    me.greet()
+    mine = me.block(me.x, me.y, me.z, me.c)
+    own = pltpu.make_async_copy(x_ref, out_ref.at[mine], own_sem)
+    own.start()
+    for h in range(2):
+        for step in (-1, 1):
+            send(view(x_ref, h), mine, h, me.along(step), me.inside(me.z + step))
+    for h in range(2):
+        for target in (by_y, by_x, core):
+            send(view(x_ref, h), mine, h, target, None)
+
+    def line(dist):
+        if dist == 0:
+            return [(me.z, None, 0)]
+        return [(me.wrap(s * dist), me.inside(me.z + s * dist), s) for s in (-1, 1)]
+
+    def from_line(dist):
+        for zb, cond, sign in line(dist):
+            blk = me.block(me.x, me.y, zb, me.c)
+            for h in range(2):
+                arrive(blk, h, cond)
+                src = view(out_ref.at[blk], h)
+                send(src, blk, h, me.along(-sign), both(cond, me.inside(me.z - sign)))
+                for target in (by_y, by_x, core):
+                    send(src, blk, h, target, cond)
+
+    def from_side(dist):
+        for zb, cond, _ in line(dist):
+            for h in range(2):
+                one = me.block(me.x, me.oy, zb, me.c)
+                two = me.block(me.ox, me.y, zb, me.c)
+                onward, last = ((one, by_x), two) if h == 0 else ((two, by_y), one)
+                arrive(onward[0], h, cond)
+                src = view(out_ref.at[onward[0]], h)
+                send(src, onward[0], h, onward[1], cond)
+                send(src, onward[0], h, core, cond)
+                arrive(last, h, cond)
+                send(view(out_ref.at[last], h), last, h, core, cond)
+
+    def from_corner(dist):
+        for zb, cond, _ in line(dist):
+            blk = me.block(me.ox, me.oy, zb, me.c)
+            for h in range(2):
+                arrive(blk, h, cond)
+                send(view(out_ref.at[blk], h), blk, h, core, cond)
+
+    for dist in range(DEEP):
+        if dist > 0:
+            from_line(dist)
+        from_side(dist)
+        if dist > 0:
+            from_corner(dist - 1)
+    from_corner(DEEP - 1)
+    for x in range(2):
+        for y in range(2):
+            for z in range(DEEP):
+                for h in range(2):
+                    arrive(me.block(x, y, z, me.oc), h, None)
+    own.wait()
+    for copy, cond in pending:
+        if cond is None:
+            copy.wait_send()
+        else:
+            pl.when(cond)(copy.wait_send)
+
+
+def dense_gather(x, count):
+    rows = x.shape[0]
+    if count != 32 or lax.axis_size("fsdp") != 2 * DEEP:
+        return lax.all_gather(x, ("expert", "fsdp"), axis=0, tiled=False)
+    cut = rows // 32 * 16 + 16 * (rows // 16 % 2)
+    return pl.pallas_call(
+        functools.partial(dense_gather_kernel, cut),
+        out_shape=jax.ShapeDtypeStruct((count,) + x.shape, x.dtype),
+        in_specs=[pl.BlockSpec(memory_space=pltpu.VMEM)],
+        out_specs=pl.BlockSpec(memory_space=pl.ANY),
+        scratch_shapes=[
+            pltpu.SemaphoreType.DMA((128,)),
+            pltpu.SemaphoreType.DMA((count, 2)),
+            pltpu.SemaphoreType.DMA,
+        ],
+        compiler_params=pltpu.CompilerParams(collective_id=0, has_side_effects=True),
+        cost_estimate=pl.CostEstimate(
+            flops=0, bytes_accessed=100 * 10**6, transcendentals=0
+        ),
+        name="dense_gather",
+    )(x)
+
+
+def add_into(dst, src):
+    def body(i, _):
+        at = pl.ds(pl.multiple_of(i * 16, 16), 16)
+        dst[at, :] = (dst[at, :].astype(F32) + src[at, :].astype(F32)).astype(BF)
+        return 0
+
+    lax.fori_loop(0, dst.shape[0] // 16, body, 0)
+
+
+def dense_sum_kernel(
+    cut, g_ref, out_ref, acc, cbuf, xbuf, ybuf, zbuf, send_sems, recv_sems, load_sems
+):
+    me = Spot()
+    rows = out_ref.shape[0]
+    top, low = pl.ds(0, cut), pl.ds(cut, rows - cut)
+    pending = []
+
+    def send(src, dst, at, target, cond=None):
+        copy = pltpu.make_async_remote_copy(
+            src_ref=src,
+            dst_ref=dst,
+            send_sem=send_sems.at[len(pending)],
+            recv_sem=recv_sems.at[at],
+            device_id=target,
+            device_id_type=MESH_ID,
+        )
+        pending.append((copy, cond))
+        if cond is None:
+            copy.start()
+        else:
+            pl.when(cond)(copy.start)
+
+    def arrive(dst, at):
+        pltpu.make_async_remote_copy(
+            src_ref=dst,
+            dst_ref=dst,
+            send_sem=send_sems.at[0],
+            recv_sem=recv_sems.at[at],
+            device_id=me.place(c=me.oc),
+            device_id_type=MESH_ID,
+        ).wait_recv()
+
+    by_y, by_x, core = me.place(y=me.oy), me.place(x=me.ox), me.place(c=me.oc)
+    me.greet()
+    offsets = (2, 3, 1, 0)
+    zs = [me.wrap(k) for k in offsets]
+    loads = []
+    for k in range(DEEP):
+        for x in range(2):
+            at = x * DEEP + k
+            theirs = (x * 2 + me.oc) * 8 + zs[k] * 2
+            send(g_ref.at[pl.ds(theirs, 2)], cbuf.at[at], at, core)
+            ours = (x * 2 + me.c) * 8 + zs[k] * 2
+            load = pltpu.make_async_copy(g_ref.at[pl.ds(ours, 2)], acc.at[at], load_sems.at[at])
+            load.start()
+            loads.append(load)
+
+    def first(k):
+        for x in range(2):
+            at = x * DEEP + k
+            loads[k * 2 + x].wait()
+            arrive(cbuf.at[at], at)
+            for y in range(2):
+                add_into(acc.at[at, y], cbuf.at[at, y])
+        base = 8 + k * 6
+        for y in range(2):
+            send(acc.at[me.ox * DEEP + k, y, top], xbuf.at[k, y, top], base + y, by_x)
+        for x in range(2):
+            send(acc.at[x * DEEP + k, me.oy, low], ybuf.at[k, x, low], base + 2 + x, by_y)
+
+    def second(k):
+        base = 8 + k * 6
+        for y in range(2):
+            arrive(xbuf.at[k, y, top], base + y)
+            add_into(acc.at[me.x * DEEP + k, y, top], xbuf.at[k, y, top])
+        for x in range(2):
+            arrive(ybuf.at[k, x, low], base + 2 + x)
+            add_into(acc.at[x * DEEP + k, me.y, low], ybuf.at[k, x, low])
+        send(acc.at[me.x * DEEP + k, me.oy, top], ybuf.at[k, 0, top], base + 4, by_y)
+        send(acc.at[me.ox * DEEP + k, me.y, low], xbuf.at[k, 0, low], base + 5, by_x)
+
+    def third(k):
+        base = 8 + k * 6
+        block = acc.at[me.x * DEEP + k, me.y]
+        arrive(ybuf.at[k, 0, top], base + 4)
+        add_into(block.at[top], ybuf.at[k, 0, top])
+        arrive(xbuf.at[k, 0, low], base + 5)
+        add_into(block.at[low], xbuf.at[k, 0, low])
+
+    for step in range(DEEP + 2):
+        if step < DEEP:
+            first(step)
+        if 0 <= step - 1 < DEEP:
+            second(step - 1)
+        if 0 <= step - 2 < DEEP:
+            third(step - 2)
+
+    for dist in (3, 2, 1):
+        for sign in (-1, 1):
+            side = (sign + 1) // 2
+            term = acc.at[me.x * DEEP + offsets.index(sign * dist % DEEP), me.y]
+            if dist < 3:
+
+                @pl.when(me.inside(me.z + sign * dist) & me.inside(me.z - sign))
+                def _(term=term, dist=dist, side=side):
+                    buf = zbuf.at[dist * 2 + side]
+                    arrive(buf, 34 + dist * 2 + side)
+                    add_into(term, buf)
+
+            send(
+                term,
+                zbuf.at[(dist - 1) * 2 + side],
+                32 + dist * 2 + side,
+                me.along(sign),
+                me.inside(me.z + sign * dist),
+            )
+    block = acc.at[me.x * DEEP + DEEP - 1, me.y]
+    for sign in (-1, 1):
+
+        @pl.when(me.inside(me.z - sign))
+        def _(sign=sign):
+            buf = zbuf.at[(sign + 1) // 2]
+            arrive(buf, 32 + 2 + (sign + 1) // 2)
+            add_into(block, buf)
+
+    def put(i, _):
+        at = pl.ds(pl.multiple_of(i * 16, 16), 16)
+        out_ref[at, :] = block[at, :].astype(F32)
+        return 0
+
+    lax.fori_loop(0, rows // 16, put, 0)
+    for copy, cond in pending:
+        if cond is None:
+            copy.wait_send()
+        else:
+            pl.when(cond)(copy.wait_send)
+
+
+def dense_sum(x):
+    count, rows, width = x.shape
+    if count != 32 or lax.axis_size("fsdp") != 2 * DEEP:
+        flat = x.reshape(count * rows, width)
+        return lax.psum_scatter(
+            flat, ("expert", "fsdp"), scatter_dimension=0, tiled=True
+        ).astype(F32)
+    cut = rows // 32 * 16 + 16 * (rows // 16 % 2)
+    pair = (2 * DEEP, 2, rows, width)
+    return pl.pallas_call(
+        functools.partial(dense_sum_kernel, cut),
+        out_shape=jax.ShapeDtypeStruct((rows, width), F32),
+        in_specs=[pl.BlockSpec(memory_space=pl.ANY)],
+        out_specs=pl.BlockSpec(memory_space=pltpu.VMEM),
+        scratch_shapes=[
+            pltpu.VMEM(pair, BF),
+            pltpu.VMEM(pair, BF),
+            pltpu.VMEM((DEEP, 2, rows, width), BF),
+            pltpu.VMEM((DEEP, 2, rows, width), BF),
+            pltpu.VMEM((6, rows, width), BF),
+            pltpu.SemaphoreType.DMA((48,)),
+            pltpu.SemaphoreType.DMA((48,)),
+            pltpu.SemaphoreType.DMA((8,)),
+        ],
+        compiler_params=pltpu.CompilerParams(
+            collective_id=1, has_side_effects=True, vmem_limit_bytes=40 * 1024 * 1024
+        ),
+        cost_estimate=pl.CostEstimate(
+            flops=0, bytes_accessed=100 * 10**6, transcendentals=0
+        ),
+        name="dense_sum",
+    )(x)
 
 
 def local(
@@ -599,6 +1001,14 @@
         head = x[:prompt_rows].reshape(G_LINE, sh.part, -1).transpose(1, 0, 2)
         return jnp.concatenate([head.reshape(prompt_rows, -1), x[prompt_rows:]], 0)
 
+    weights = RingGather(jnp.concatenate([w_gate[0].T, w_up[0].T, w_down[0]], 0), fsdp_count)
+    spread = [fsdp_count // 8] * 4
+    spread[0] += fsdp_count // 2 - sum(spread)
+
+    def run(ring, count):
+        for _ in range(count):
+            ring.step()
+
     small = jnp.concatenate(
         [attn_gain, moe_gain, w_router.reshape(-1), bias_table, group_map.astype(BF)]
     )
@@ -606,10 +1016,12 @@
     small_rows = -(-small_rows // 16) * 16
     small = jnp.pad(small, (0, small_rows * D - small.shape[0])).reshape(small_rows, D)
     pack = jnp.concatenate([w_qkv[:, i * D : (i + 1) * D] for i in range(3)] + [w_out, small], 0)
-    gathered = lax.all_gather(pack, ("expert", "fsdp"), axis=0, tiled=False)
+    gathered = dense_gather(pack, group_count)
+    run(weights, spread[0])
     qkv_full = jnp.concatenate(
         [gathered[:, i * shard : (i + 1) * shard].reshape(D, D) for i in range(3)], 1
     )
+    qkv_full = weights.tie(qkv_full)
     out_full = gathered[:, 3 * shard : 4 * shard].reshape(D, D)
     tail = gathered[:, 4 * shard]
     marks = [0, shard, 2 * shard, 2 * shard + shard * expert_count]
@@ -624,10 +1036,6 @@
     my_groups = my_groups.astype(jnp.int32)
     bucket = buckets.reshape(SPAN_BLOCKS, HALF)
 
-    gate_chunks = ring_gather(w_gate[0].T, fsdp_count)
-    up_chunks = ring_gather(w_up[0].T, fsdp_count)
-    down_chunks = ring_gather(w_down[0], fsdp_count)
-
     token_input = by_prompt(inputs)
     grad_rows_low = by_prompt(grad_output)
     routes = by_prompt(routes)
@@ -643,8 +1051,12 @@
         .reshape(fsdp_count, tok_count, 3 * sh.width)
     )
     head_qkv = lax.all_to_all(by_heads, "fsdp", split_axis=0, concat_axis=0, tiled=True)
+    run(weights, spread[1])
+    head_qkv = weights.tie(head_qkv)
     head_att, att_turned, att_lse = attend_forward(sh, my_groups, my_table, bucket, head_qkv)
     att_back = lax.all_to_all(head_att, "fsdp", split_axis=0, concat_axis=0, tiled=True)
+    run(weights, spread[2])
+    att_back = weights.tie(att_back)
     attn_low = att_back.transpose(1, 0, 2).reshape(tok_count, D)
 
     middle = input_float + jnp.dot(attn_low, out_full, preferred_element_type=F32)
@@ -670,6 +1082,8 @@
         return rows.reshape(slot_total, D)
 
     expert_rows = swap_experts(outgoing)
+    run(weights, spread[3])
+    expert_rows = weights.tie(expert_rows)
     slot_gate = jnp.sum(
         jnp.where(hot[0], gate_kept[:, 0:1], 0.0) + jnp.where(hot[1], gate_kept[:, 1:2], 0.0),
         axis=0,
@@ -677,9 +1091,10 @@
     slot_grad = lax.dot_general(any_low, grad_rows_low, TN, preferred_element_type=F32)
     grad_result = swap_experts((slot_gate[:, None] * slot_grad).astype(BF))
 
-    gate_whole = jnp.concatenate(gate_chunks, 0)
-    up_whole = jnp.concatenate(up_chunks, 0)
-    down_whole = jnp.concatenate(down_chunks, 0)
+    gate_whole, up_whole, down_whole = (
+        jnp.concatenate([c[i * ff_shard : (i + 1) * ff_shard] for c in weights.chunks], 0)
+        for i in range(3)
+    )
     gate_pre = lax.dot_general(expert_rows, gate_whole, NT, preferred_element_type=F32)
     up_pre = lax.dot_general(expert_rows, up_whole, NT, preferred_element_type=F32)
     hidden = gated_unit(gate_pre, up_pre).astype(BF)
@@ -698,18 +1113,13 @@
     ).astype(BF)
     up_total = lax.dot_general(grad_up_pre, expert_rows, TN, preferred_element_type=F32).astype(BF)
 
-    half_shard = ff_shard // 2
-
-    def shares(total):
-        def part(k, half):
-            start = k * ff_shard + half * half_shard
-            return total[start : start + half_shard]
-
-        return jnp.concatenate(ring_scatter(part, fsdp_count), 0)
-
-    grad_down = shares(down_total)
-    grad_gate = shares(gate_total).T
-    grad_up = shares(up_total).T
+    def part(k):
+        rows = slice(k * ff_shard, (k + 1) * ff_shard)
+        return jnp.concatenate([gate_total[rows], up_total[rows], down_total[rows]], 0)
+
+    sums = RingScatter(part, fsdp_count)
+    run(sums, spread[0])
+    grad_sent = sums.tie(grad_sent)
 
     picked = [
         jnp.dot(h.astype(BF), returned, preferred_element_type=F32) for h in hot
@@ -731,10 +1141,20 @@
         grad_attn.reshape(tok_count, fsdp_count, sh.width).transpose(1, 0, 2)
     )
     head_grad = lax.all_to_all(head_grad, "fsdp", split_axis=0, concat_axis=0, tiled=True)
+    run(sums, spread[1])
+    head_grad = sums.tie(head_grad)
     head_dqkv, head_table = attend_backward(
         sh, my_groups, my_table, bucket, head_qkv, head_grad, att_turned, att_lse
     )
+    run(sums, spread[2])
+    head_dqkv = sums.tie(head_dqkv)
     back_dqkv = lax.all_to_all(head_dqkv, "fsdp", split_axis=0, concat_axis=0, tiled=True)
+    run(sums, spread[3])
+    back_dqkv = sums.tie(back_dqkv)
+    expert_sums = sums.finish()
+    grad_gate = expert_sums[:ff_shard].T
+    grad_up = expert_sums[ff_shard : 2 * ff_shard].T
+    grad_down = expert_sums[2 * ff_shard :]
     grad_qkv = (
         back_dqkv.reshape(fsdp_count, tok_count, 3, sh.width)
         .transpose(1, 2, 0, 3)
@@ -754,27 +1174,21 @@
         flat = jnp.pad(flat, ((0, 0), (0, 16 * D - flat.shape[1])))
         return flat.reshape(group_count, 16, D)
 
-    def sum_shards(parts):
-        whole = jnp.concatenate(parts, 1)
-        count = whole.shape[1]
-        flat = whole.reshape(group_count * count, D)
-        return lax.psum_scatter(
-            flat, ("expert", "fsdp"), scatter_dimension=0, tiled=True
-        ).astype(F32)
-
-    early = sum_shards([rows_of(grad_out_w), small_block([grad_moe_gain, grad_router])])
-    sum_out = early[:shard]
-    sum_moe = early[shard, :shard]
-    sum_router = early[shard, shard : shard + shard * expert_count].reshape(shard, expert_count)
     place_table = (jnp.arange(fsdp_count) == fsdp_place).astype(F32)
     whole_table = place_table[:, None] * head_table[:, 0][None, :]
-    late = sum_shards(
-        [rows_of(grad_qkv_w[:, i * D : (i + 1) * D]) for i in range(3)]
-        + [small_block([grad_attn_gain, whole_table.reshape(-1)])]
-    )
-    sum_qkv = jnp.concatenate([late[i * shard : (i + 1) * shard] for i in range(3)], 1)
-    sum_attn = late[3 * shard, :shard]
-    sum_table = late[3 * shard, shard : shard + bias_table.shape[0]]
+    parts = [rows_of(grad_qkv_w[:, i * D : (i + 1) * D]) for i in range(3)]
+    parts.append(rows_of(grad_out_w))
+    parts.append(
+        small_block([grad_attn_gain, grad_moe_gain, grad_router, whole_table.reshape(-1)])
+    )
+    sums_dense = dense_sum(jnp.concatenate(parts, 1))
+    sum_qkv = jnp.concatenate([sums_dense[i * shard : (i + 1) * shard] for i in range(3)], 1)
+    sum_out = sums_dense[3 * shard : 4 * shard]
+    sum_small = sums_dense[4 * shard]
+    sum_attn = sum_small[marks[0] : marks[1]]
+    sum_moe = sum_small[marks[1] : marks[2]]
+    sum_router = sum_small[marks[2] : marks[3]].reshape(shard, expert_count)
+    sum_table = sum_small[marks[3] : marks[4]]
     return (
         output,
         losses[None, :],

time: 1070 us -> 859 us (0.80)
  waiting for transfers between devices: 504 us -> 213 us
  Pallas kernels: 66.2 us -> 231 us
  starting transfers between devices: 159 us -> 61.6 us
  blocking collectives: 27.5 us -> 50.2 us
  between operations: 17.2 us -> 4.35 us
    ppermute x63 -> x16, waiting for transfers between devices: 324 us -> 141 us  [ring_hop(): lax.ppermute(x, 'fsdp', [(ring[i], ring[(i + step) % count]) for i in ran...]
    pallas_call x0 -> x2, Pallas kernels: none -> 165 us  [the longest x1 83.9 us: dense_gather(): pl.pallas_call(functools.partial(dense_gather_kernel, cut), out_shape=jax...]
    ppermute x63 -> x16, starting transfers between devices: 126 us -> 30.7 us  [ring_hop(): lax.ppermute(x, 'fsdp', [(ring[i], ring[(i + step) % count]) for i in ran...]
    all_gather x1 -> x0, waiting for transfers between devices: 82.8 us -> none  [local(): gathered = lax.all_gather(pack, ('expert', 'fsdp'), axis=0, tiled=False)]
    all_to_all x1, waiting for transfers between devices: 46.4 us -> 0.01 us  [local(): lax.all_to_all(head_dqkv, 'fsdp', split_axis=0, concat_axis=0, tiled=True)]
    all_to_all x1, waiting for transfers between devices: 0.01 us -> 28.7 us  [local(): lax.all_to_all(head_att, 'fsdp', split_axis=0, concat_axis=0, tiled=True)]
    all_to_all x1, blocking collectives: 27.5 us -> 50.2 us  [local(): lax.all_to_all(head_grad, 'fsdp', split_axis=0, concat_axis=0, tiled=True)]
    unnamed x119 -> x234, local copies, waits for them, and re-layouts: 50.7 us -> 31.2 us
  transfers between devices with their start and end apart: 73 -> 23, of which waited for: 42 -> 11; matrix products, arithmetic and copies ran while one was open for 17% -> 16% of each run, Pallas kernels for 2% -> 18%
where the time goes in v2:
time: 859 us; the launch traced here: 843 us
  Pallas kernels  231 us (27%)
  waiting for transfers between devices  213 us (25%)
  matrix products  138 us (16%)
  local copies, waits for them, and re-layouts  104 us (12%)
  starting transfers between devices  61.6 us (7%)
  blocking collectives  50.2 us (6%)
  other arithmetic  41.3 us (5%)
    ppermute x16, waiting for transfers between devices, ring_hop(): lax.ppermute(x, 'fsdp', [(ring[i], ring[(i + step) % count]) for i in ran...  141 us
    pallas_call x1, Pallas kernels, dense_gather(): pl.pallas_call(functools.partial(dense_gather_kernel, cut), out_shape=jax...  83.9 us
    pallas_call x1, Pallas kernels, dense_sum(): pl.pallas_call(functools.partial(dense_sum_kernel, cut), out_shape=jax.Sh...  80.6 us
    all_to_all x1, blocking collectives, local(): lax.all_to_all(head_grad, 'fsdp', split_axis=0, concat_axis=0, tiled=True)  50.2 us
    all_to_all x4, waiting for transfers between devices, swap_experts(): lax.all_to_all(rows, 'expert', split_axis=0, concat_axis=0, tiled=True)  43.3 us
    pallas_call x1, Pallas kernels, attend_backward(): pl.pallas_call(functools.partial(attn_backward_kernel, sh), out_shape=(ja...  43.1 us
    unnamed x234, local copies, waits for them, and re-layouts  31.2 us
    ppermute x16, starting transfers between devices, ring_hop(): lax.ppermute(x, 'fsdp', [(ring[i], ring[(i + step) % count]) for i in ran...  30.7 us
  transfers between devices with their start and end apart: 23, of which 11 were waited for; matrix products, arithmetic and copies ran while one was open for 16% of the time, Pallas kernels for 18%

profile of v2, /device:TPU:0, one launch (start us, length us, event | category | flops | bytes accessed | tf_op | source)
XLA Modules:
  0.0 843.1 jit_solution(9153109856260093897)
XLA Ops:
  0.7 3.2 pad_maximum_fusion.1
  3.9 3.0 collective-permute-start.1
  15.8 83.9 %dense_gather.1 = bf16[32,144,1024]{2,1,0:T(8,128)(2,1)} custom-call(bf16[144,1024]{1,0:T(8,128)(2,1)} %copy-done.41), custom_call_target="tpu_custom_call" | custom-call | bytes 100000000 | tf_op jit(solution)/shard_map/dense_gather/pallas_call | solution.py:776
  101.3 5.2 fusion.74
  108.6 3.1 fusion.19
  115.2 4.3 copy.56
  119.5 5.0 all-to-all-start
  135.8 75.1 %collective-permute-done.2 = bf16[1056,1024]{1,0:T(8,128)(2,1)} collective-permute-done((bf16[1056,1024]{1,0:T(8,128)(2,1)}, bf16[1056,1024]{1,0:T(8,128)(2,1)}, u32[]{:S(2)}, u32[]{:S(2)}) %collective-permute-start.2) | collective-permute-done | bytes 2162720 | tf_op jit(solution)/shard_map/ppermute | solution.py:535
  211.9 14.1 %collective-permute-start.4 = (bf16[1056,1024]{1,0:T(8,128)(2,1)}, bf16[1056,1024]{1,0:T(8,128)(2,1)}, u32[]{:S(2)}, u32[]{:S(2)}) collective-permute-start(bf16[1056,1024]{1,0:T(8,128)(2,1)} %collective-permute-done.2), channel_id=1, source_target_pairs={{0,2},{2,4},{4,6},{6,7},{7,5},{5,3},{3,1},{1,0},{8,10},{10,12},{12... | collective-permute-start | bytes 6488072 | tf_op jit(solution)/shard_map/ppermute | solution.py:535
  226.1 23.1 %attend_forward.1 = (bf16[8,384,128]{2,1,0:T(8,128)(2,1)}, f32[12,128,256]{2,1,0:T(8,128)S(1)}, f32[12,8,256]{2,1,0:T(8,128)S(1)}) custom-call(s32[8]{0:T(128)S(1)} %bitcast_convert_fusion.1.group_ref, f32[2,32]{1,0:T(2,128)S(1)} %bitcast_convert_fusion.table_ref, s32[9,128]{1,0:T(8,128)S(1)} %bitcast.125, bf16[8,384,384]{2,1,0:T(8,128)(2,1)S(1)} %all-to-all-done.x_ref), custom_call_target="tpu_custom_call" | custom-call | flops 10000000000 | bytes 8000000 | tf_op jit(solution)/shard_map/attend_forward/pallas_call | solution.py:474
  250.3 4.4 all-to-all-start.1
  258.1 3.0 slice_dynamic-update-slice_fusion.6
  264.0 28.7 %all-to-all-done.1 = bf16[8,384,128]{2,1,0:T(8,128)(2,1)S(1)} async-done(((bf16[8,384,128]{2,1,0:T(8,128)(2,1)}), bf16[8,384,128]{2,1,0:T(8,128)(2,1)S(1)}, u32[]{:S(2)}, u32[]{:S(2)}) %all-to-all-start.1) | async-done | bytes 786464 | tf_op jit(solution)/shard_map/all_to_all | solution.py:1057
  305.9 3.7 all-to-all-start.2
  314.7 19.2 %all-to-all-done.2 = bf16[4,240,1024]{2,1,0:T(8,128)(2,1)S(1)} async-done(((bf16[4,240,1024]{2,1,0:T(8,128)(2,1)}), bf16[4,240,1024]{2,1,0:T(8,128)(2,1)S(1)}, u32[]{:S(2)}, u32[]{:S(2)}) %all-to-all-start.2) | async-done | bytes 1966112 | tf_op jit(solution)/shard_map/all_to_all | solution.py:1081
  333.9 4.4 all-to-all-start.4
  347.2 3.1 slice_dynamic-update-slice_fusion.1
  351.6 11.0 %all-to-all-done.4 = bf16[4,240,1024]{2,1,0:T(8,128)(2,1)} async-done(((bf16[4,240,1024]{2,1,0:T(8,128)(2,1)}), bf16[4,240,1024]{2,1,0:T(8,128)(2,1)}, u32[]{:S(2)}, u32[]{:S(2)}) %all-to-all-start.4) | async-done | bytes 1966112 | tf_op jit(solution)/shard_map/all_to_all | solution.py:1081
  362.7 11.3 %fusion.82 = f32[960,2816]{1,0:T(8,128)} fusion(bf16[960,1024]{1,0:T(8,128)(2,1)} %bitcast.36, bf16[2816,1024]{1,0:T(8,128)(2,1)} %get-tuple-element.166), kind=kOutput, calls=%fused_computation.223 | convolution fusion | flops 5536481280 | bytes 18546688 | tf_op jit(solution)/shard_map/dot_general | solution.py:1104
  374.0 11.0 %fusion.81 = f32[960,2816]{1,0:T(8,128)} fusion(bf16[960,1024]{1,0:T(8,128)(2,1)S(1)} %bitcast.164, bf16[2816,1024]{1,0:T(8,128)(2,1)} %get-tuple-element.167), kind=kOutput, calls=%fused_computation.222 | convolution fusion | flops 5536481280 | bytes 18546688 | tf_op jit(solution)/shard_map/dot_general | solution.py:1099
  385.0 21.9 %multiply_convert_fusion = (bf16[960,2816]{1,0:T(8,128)(2,1)}, bf16[960,2816]{1,0:T(8,128)(2,1)}, bf16[960,2816]{1,0:T(8,128)(2,1)}) fusion(f32[960,2816]{1,0:T(8,128)} %fusion.82, f32[960,2816]{1,0:T(8,128)} %fusion.81, bf16[960,1024]{1,0:T(8,128)(2,1)S(1)} %bitcast.165, bf16[2816,1024]{1,0:T(8,128)(2,1)} %get-tuple-element.168), kind=kOutput, calls=%fused_computation.9 | convolution fusion | flops 5606768640 | bytes 45580288 | tf_op jit(solution)/shard_map/dot_general | solution.py:1098
  406.9 10.8 %fusion.83 = f32[960,1024]{1,0:T(8,128)} fusion(bf16[960,2816]{1,0:T(8,128)(2,1)} %get-tuple-element.129, bf16[2816,1024]{1,0:T(8,128)(2,1)} %get-tuple-element.168), kind=kOutput, calls=%fused_computation.224 | convolution fusion | flops 5536481280 | bytes 15106048 | tf_op jit(solution)/shard_map/dot_general | solution.py:1106
  417.7 8.3 convolution_convert_fusion.1
  426.0 8.7 %convolution_convert_fusion.7 = bf16[960,1024]{1,0:T(8,128)(2,1)} fusion(bf16[960,2816]{1,0:T(8,128)(2,1)S(1)} %bitcast.187, bf16[2816,1024]{1,0:T(8,128)(2,1)} %get-tuple-element.166), kind=kOutput, calls=%fused_computation.55 | convolution fusion | flops 5537464320 | bytes 13139968 | tf_op jit(solution)/shard_map/dot_general | solution.py:1101
  434.7 9.6 %convolution_convert_fusion.2 = bf16[2816,1024]{1,0:T(8,128)(2,1)} fusion(bf16[960,2816]{1,0:T(8,128)(2,1)S(1)} %bitcast.187, bf16[960,1024]{1,0:T(8,128)(2,1)} %bitcast.36), kind=kOutput, calls=%fused_computation.15 | convolution fusion | flops 5539364864 | bytes 13139968 | tf_op jit(solution)/shard_map/dot_general | solution.py:1110
  444.3 4.4 all-to-all-start.3
  448.8 9.0 %convolution_convert_fusion.3 = bf16[2816,1024]{1,0:T(8,128)(2,1)S(1)} fusion(bf16[960,2816]{1,0:T(8,128)(2,1)} %get-tuple-element.128, bf16[960,1024]{1,0:T(8,128)(2,1)S(1)} %bitcast.167), kind=kOutput, calls=%fused_computation.16 | convolution fusion | flops 5539364864 | bytes 13139968 | tf_op jit(solution)/shard_map/dot_general | solution.py:1114
  457.8 5.2 fusion.76
  471.7 8.8 %add_convert_fusion.4 = bf16[960,1024]{1,0:T(8,128)(2,1)} fusion(f32[960,1024]{1,0:T(8,128)S(1)} %copy-done.100, bf16[960,2816]{1,0:T(8,128)(2,1)S(1)} %bitcast.185, bf16[2816,1024]{1,0:T(8,128)(2,1)} %get-tuple-element.167), kind=kOutput, calls=%fused_computation.27 | convolution fusion | flops 5538447360 | bytes 17072128 | tf_op jit(solution)/shard_map/dot_general | solution.py:1106
  480.5 4.6 all-to-all-start.5
  488.0 3.8 fusion.22
  492.0 4.1 collective-permute-done.9
  496.3 13.1 %all-to-all-done.5 = bf16[4,240,1024]{2,1,0:T(8,128)(2,1)} async-done(((bf16[4,240,1024]{2,1,0:T(8,128)(2,1)}), bf16[4,240,1024]{2,1,0:T(8,128)(2,1)}, u32[]{:S(2)}, u32[]{:S(2)}) %all-to-all-start.5) | async-done | bytes 1966112 | tf_op jit(solution)/shard_map/all_to_all | solution.py:1081
  519.1 3.5 multiply_reduce_fusion
  530.7 50.2 %all_to_all.40.do_ref = bf16[8,384,128]{2,1,0:T(8,128)(2,1)S(1)} all-to-all(bf16[8,384,128]{2,1,0:T(8,128)(2,1)} %bitcast.154), channel_id=1, replica_groups=mesh['expert'=4,'fsdp'=8] {'fsdp'}, dimensions={0} | all-to-all | bytes 1572864 | tf_op jit(solution)/shard_map/all_to_all | solution.py:1143
  581.0 3.4 add_convert_fusion.3
  589.7 43.1 %attend_backward.1 = (bf16[8,384,384]{2,1,0:T(8,128)(2,1)}, f32[64,128]{1,0:T(8,128)S(1)}) custom-call(s32[8]{0:T(128)S(1)} %bitcast_convert_fusion.1.group_ref, f32[2,32]{1,0:T(2,128)S(1)} %bitcast_convert_fusion.table_ref, s32[9,128]{1,0:T(8,128)S(1)} %bitcast.126, bf16[8,384,384]{2,1,0:T(8,128)(2,1)} %copy-done, ...), custom_call_target="tpu_custom_call" | custom-call | flops 20000000000 | bytes 12000000 | tf_op jit(solution)/shard_map/attend_backward/pallas_call | solution.py:499
  632.8 3.2 collective-permute-done.13
  636.0 4.4 all-to-all-start.7
  640.4 4.8 add_convert_fusion.1
  647.1 4.0 add_convert_fusion
  667.4 55.1 %collective-permute-done.14 = bf16[1056,1024]{1,0:T(8,128)(2,1)} collective-permute-done((bf16[1056,1024]{1,0:T(8,128)(2,1)}, bf16[1056,1024]{1,0:T(8,128)(2,1)}, u32[]{:S(2)}, u32[]{:S(2)}) %collective-permute-start.14) | collective-permute-done | bytes 2162720 | tf_op jit(solution)/shard_map/ppermute | solution.py:535
  725.1 4.3 copy.64
  731.4 5.2 fusion.21
  737.1 5.8 convolution_convert_fusion
  743.6 3.6 fusion.75
  749.7 80.6 %dense_sum.1 = f32[144,1024]{1,0:T(8,128)S(1)} custom-call(bf16[32,144,1024]{2,1,0:T(8,128)(2,1)S(1)} %constant_dynamic-update-slice_fusion.8.g_ref), custom_call_target="tpu_custom_call" | custom-call | bytes 100000000 | tf_op jit(solution)/shard_map/dense_sum/pallas_call | solution.py:941
  833.8 4.1 convert_add_fusion
  (385 shorter events, 131.5 us)
Async XLA Ops:
  3.9 103.2 %collective-permute-start.1 = (bf16[1056,1024]{1,0:T(8,128)(2,1)}, bf16[1056,1024]{1,0:T(8,128)(2,1)}, u32[]{:S(2)}, u32[]{:S(2)}) collective-permute-start(bf16[1056,1024]{1,0:T(8,128)(2,1)} %pad_maximum_fusion.1), channel_id=1, source_target_pairs={{0,1},{2,0},{4,2},{6,4},{7,6},{5,7},{3,5},{1,3},{8,9},{10,8},{12,1... | collective-permute-start | bytes 6488072 | tf_op jit(solution)/shard_map/ppermute | solution.py:535
  6.9 100.2 %collective-permute-start = (bf16[1056,1024]{1,0:T(8,128)(2,1)}, bf16[1056,1024]{1,0:T(8,128)(2,1)S(1)}, u32[]{:S(2)}, u32[]{:S(2)}) collective-permute-start(bf16[1056,1024]{1,0:T(8,128)(2,1)} %pad_maximum_fusion.1), channel_id=1, source_target_pairs={{0,2},{2,4},{4,6},{6,7},{7,5},{5,3},{3,1},{1,0},{8,10},{10,12},{12... | collective-permute-start | bytes 6488072 | tf_op jit(solution)/shard_map/ppermute | solution.py:535
  7.0 294.1 %copy-start.15 = (bf16[128,1024]{1,0:T(8,128)(2,1)}, bf16[128,1024]{1,0:T(8,128)(2,1)S(1)}, u32[]{:S(2)}) copy-start(bf16[128,1024]{1,0:T(8,128)(2,1)S(1)} %slice.332) | copy-start | bytes 786436
  11.7 289.4 %copy-start.7 = (bf16[128,2,1024]{2,0,1:T(8,128)(2,1)}, bf16[128,2,1024]{2,0,1:T(8,128)(2,1)S(1)}, u32[]{:S(2)}) copy-start(bf16[128,2,1024]{2,0,1:T(8,128)(2,1)S(1)} %copy.53) | copy-start | bytes 1572868
  119.5 10.8 %slice-start.5 = ((s32[384,2]{0,1:T(2,128)}), s32[256,2]{0,1:T(2,128)S(1)}, s32[]{:S(2)}) async-start(s32[384,2]{0,1:T(2,128)} %param.27), calls=%async_computation.13 | async-start | bytes 4096 | tf_op jit(solution)/shard_map/slice | solution.py:997
  119.5 11.0 %slice-start.4 = ((s32[384,2]{0,1:T(2,128)}), s32[256,2]{0,1:T(2,128)S(1)}, s32[]{:S(2)}) async-start(s32[384,2]{0,1:T(2,128)} %param.26), calls=%async_computation.12 | async-start | bytes 4096 | tf_op jit(solution)/shard_map/slice | solution.py:997
  119.5 92.4 %all-to-all-start = ((bf16[8,384,384]{2,1,0:T(8,128)(2,1)}), bf16[8,384,384]{2,1,0:T(8,128)(2,1)S(1)}, u32[]{:S(2)}, u32[]{:S(2)}) async-start(bf16[8,384,384]{2,1,0:T(8,128)(2,1)} %copy.56), calls=%async_computation | async-start | bytes 4718592 | tf_op jit(solution)/shard_map/all_to_all | solution.py:1053
  124.5 86.5 %collective-permute-start.2 = (bf16[1056,1024]{1,0:T(8,128)(2,1)}, bf16[1056,1024]{1,0:T(8,128)(2,1)}, u32[]{:S(2)}, u32[]{:S(2)}) collective-permute-start(bf16[1056,1024]{1,0:T(8,128)(2,1)} %copy-done.31), channel_id=1, source_target_pairs={{0,2},{2,4},{4,6},{6,7},{7,5},{5,3},{3,1},{1,0},{8,10},{10,12},{12... | collective-permute-start | bytes 6488072 | tf_op jit(solution)/shard_map/ppermute | solution.py:535
  126.5 85.4 %collective-permute-start.3 = (bf16[1056,1024]{1,0:T(8,128)(2,1)}, bf16[1056,1024]{1,0:T(8,128)(2,1)}, u32[]{:S(2)}, u32[]{:S(2)}) collective-permute-start(bf16[1056,1024]{1,0:T(8,128)(2,1)} %collective-permute-done.1), channel_id=1, source_target_pairs={{0,1},{2,0},{4,2},{6,4},{7,6},{5,7},{3,5},{1,3},{8,9},{10,8},{12,1... | collective-permute-start | bytes 6488072 | tf_op jit(solution)/shard_map/ppermute | solution.py:535
  126.5 184.0 %copy-start.76 = (s32[128,2]{0,1:T(2,128)}, s32[128,2]{0,1:T(2,128)S(1)}, u32[]{:S(2)}) copy-start(s32[128,2]{0,1:T(2,128)S(1)} %slice.345) | copy-start | bytes 3076
  128.2 97.8 %copy-start.1 = (s32[1152]{0:T(1024)S(1)}, s32[1152]{0:T(1024)}, u32[]{:S(2)}) copy-start(s32[1152]{0:T(1024)} %param.29) | copy-start | bytes 13828
  130.5 180.1 %copy-start.53 = (s32[2,128,2]{1,2,0:T(2,128)}, s32[2,128,2]{1,2,0:T(2,128)S(1)}, u32[]{:S(2)}) copy-start(s32[2,128,2]{1,2,0:T(2,128)S(1)} %copy.58) | copy-start | bytes 6148
  135.2 168.1 %copy-start.45 = (f32[1024]{0:T(1024)}, f32[1024]{0:T(1024)S(1)}, u32[]{:S(2)}) copy-start(f32[1024]{0:T(1024)S(1)} %reshape.324) | copy-start | bytes 12292
  135.7 166.5 %copy-start.29 = (bf16[1024,4]{1,0:T(8,128)(2,1)}, bf16[1024,4]{1,0:T(8,128)(2,1)S(1)}, u32[]{:S(2)}) copy-start(bf16[1024,4]{1,0:T(8,128)(2,1)S(1)} %reshape.296) | copy-start | bytes 24580
  135.8 174.6 %copy-start.66 = (s32[384]{0:T(512)}, s32[384]{0:T(512)S(1)}, u32[]{:S(2)}) copy-start(s32[384]{0:T(512)S(1)} %get-tuple-element.120) | copy-start | bytes 4612
  135.8 174.6 %copy-start.68 = (s32[384]{0:T(512)}, s32[384]{0:T(512)S(1)}, u32[]{:S(2)}) copy-start(s32[384]{0:T(512)S(1)} %get-tuple-element.121) | copy-start | bytes 4612
  211.9 37.3 %copy-start = (bf16[8,384,384]{2,1,0:T(8,128)(2,1)}, bf16[8,384,384]{2,1,0:T(8,128)(2,1)S(1)}, u32[]{:S(2)}) copy-start(bf16[8,384,384]{2,1,0:T(8,128)(2,1)S(1)} %all-to-all-done.x_ref) | copy-start | bytes 7077892
  211.9 80.8 %collective-permute-start.4 = (bf16[1056,1024]{1,0:T(8,128)(2,1)}, bf16[1056,1024]{1,0:T(8,128)(2,1)}, u32[]{:S(2)}, u32[]{:S(2)}) collective-permute-start(bf16[1056,1024]{1,0:T(8,128)(2,1)} %collective-permute-done.2), channel_id=1, source_target_pairs={{0,2},{2,4},{4,6},{6,7},{7,5},{5,3},{3,1},{1,0},{8,10},{10,12},{12... | collective-permute-start | bytes 6488072 | tf_op jit(solution)/shard_map/ppermute | solution.py:535
  226.1 66.6 %collective-permute-start.5 = (bf16[1056,1024]{1,0:T(8,128)(2,1)}, bf16[1056,1024]{1,0:T(8,128)(2,1)}, u32[]{:S(2)}, u32[]{:S(2)}) collective-permute-start(bf16[1056,1024]{1,0:T(8,128)(2,1)} %collective-permute-done.3), channel_id=1, source_target_pairs={{0,1},{2,0},{4,2},{6,4},{7,6},{5,7},{3,5},{1,3},{8,9},{10,8},{12,1... | collective-permute-start | bytes 6488072 | tf_op jit(solution)/shard_map/ppermute | solution.py:535
  250.3 42.4 %all-to-all-start.1 = ((bf16[8,384,128]{2,1,0:T(8,128)(2,1)}), bf16[8,384,128]{2,1,0:T(8,128)(2,1)S(1)}, u32[]{:S(2)}, u32[]{:S(2)}) async-start(bf16[8,384,128]{2,1,0:T(8,128)(2,1)} %get-tuple-element.45), calls=%async_computation.1 | async-start | bytes 1572864 | tf_op jit(solution)/shard_map/all_to_all | solution.py:1057
  254.7 57.4 %copy-start.84 = (s32[384]{0:T(512)}, s32[384]{0:T(512)S(1)}, u32[]{:S(2)}) copy-start(s32[384]{0:T(512)S(1)} %get-tuple-element.122) | copy-start | bytes 4612
  254.8 57.4 %copy-start.86 = (s32[384]{0:T(512)}, s32[384]{0:T(512)S(1)}, u32[]{:S(2)}) copy-start(s32[384]{0:T(512)S(1)} %get-tuple-element.123) | copy-start | bytes 4612
  298.6 42.7 %collective-permute-start.7 = (bf16[528,1024]{1,0:T(8,128)(2,1)}, bf16[528,1024]{1,0:T(8,128)(2,1)}, u32[]{:S(2)}, u32[]{:S(2)}) collective-permute-start(bf16[528,1024]{1,0:T(8,128)(2,1)} %slice.356), channel_id=1, source_target_pairs={{0,1},{2,0},{4,2},{6,4},{7,6},{5,7},{3,5},{1,3},{8,9},{10,8},{12,1... | collective-permute-start | bytes 3244040 | tf_op jit(solution)/shard_map/ppermute | solution.py:535
  299.0 42.3 %collective-permute-start.6 = (bf16[528,1024]{1,0:T(8,128)(2,1)}, bf16[528,1024]{1,0:T(8,128)(2,1)}, u32[]{:S(2)}, u32[]{:S(2)}) collective-permute-start(bf16[528,1024]{1,0:T(8,128)(2,1)} %slice.355), channel_id=1, source_target_pairs={{0,2},{2,4},{4,6},{6,7},{7,5},{5,3},{3,1},{1,0},{8,10},{10,12},{12... | collective-permute-start | bytes 3244040 | tf_op jit(solution)/shard_map/ppermute | solution.py:535
  305.9 28.0 %all-to-all-start.2 = ((bf16[4,240,1024]{2,1,0:T(8,128)(2,1)}), bf16[4,240,1024]{2,1,0:T(8,128)(2,1)S(1)}, u32[]{:S(2)}, u32[]{:S(2)}) async-start(bf16[4,240,1024]{2,1,0:T(8,128)(2,1)} %bitcast.171), calls=%async_computation.2 | async-start | bytes 3932160 | tf_op jit(solution)/shard_map/all_to_all | solution.py:1081
  333.9 28.8 %all-to-all-start.4 = ((bf16[4,240,1024]{2,1,0:T(8,128)(2,1)}), bf16[4,240,1024]{2,1,0:T(8,128)(2,1)}, u32[]{:S(2)}, u32[]{:S(2)}) async-start(bf16[4,240,1024]{2,1,0:T(8,128)(2,1)} %bitcast.168), calls=%async_computation.4 | async-start | bytes 3932160 | tf_op jit(solution)/shard_map/all_to_all | solution.py:1081
  406.9 10.9 %copy-start.99 = (bf16[960,2816]{1,0:T(8,128)(2,1)S(1)}, bf16[960,2816]{1,0:T(8,128)(2,1)}, u32[]{:S(2)}) copy-start(bf16[960,2816]{1,0:T(8,128)(2,1)} %get-tuple-element.129) | copy-start | bytes 16220164
  406.9 19.1 %slice-start.8 = ((s8[5406720]{0:T(1024)(128)(4,1)}), s8[4194304]{0:T(1024)(128)(4,1)S(1)}, s32[]{:S(2)}) async-start(s8[5406720]{0:T(1024)(128)(4,1)} %bitcast.186), calls=%async_computation.16 | async-start | bytes 8388608
  444.3 36.1 %all-to-all-start.3 = ((bf16[4,240,1024]{2,1,0:T(8,128)(2,1)}), bf16[4,240,1024]{2,1,0:T(8,128)(2,1)}, u32[]{:S(2)}, u32[]{:S(2)}) async-start(bf16[4,240,1024]{2,1,0:T(8,128)(2,1)} %bitcast.170), calls=%async_computation.3 | async-start | bytes 3932160 | tf_op jit(solution)/shard_map/all_to_all | solution.py:1081
  469.4 26.7 %collective-permute-start.9 = (bf16[528,1024]{1,0:T(8,128)(2,1)}, bf16[528,1024]{1,0:T(8,128)(2,1)}, u32[]{:S(2)}, u32[]{:S(2)}) collective-permute-start(bf16[528,1024]{1,0:T(8,128)(2,1)} %get-tuple-element.187), channel_id=1, source_target_pairs={{0,1},{2,0},{4,2},{6,4},{7,6},{5,7},{3,5},{1,3},{8,9},{10,8},{12,1... | collective-permute-start | bytes 3244040 | tf_op jit(solution)/shard_map/ppermute | solution.py:535
  470.1 26.2 %collective-permute-start.8 = (bf16[528,1024]{1,0:T(8,128)(2,1)}, bf16[528,1024]{1,0:T(8,128)(2,1)}, u32[]{:S(2)}, u32[]{:S(2)}) collective-permute-start(bf16[528,1024]{1,0:T(8,128)(2,1)} %get-tuple-element.188), channel_id=1, source_target_pairs={{0,2},{2,4},{4,6},{6,7},{7,5},{5,3},{3,1},{1,0},{8,10},{10,12},{12... | collective-permute-start | bytes 3244040 | tf_op jit(solution)/shard_map/ppermute | solution.py:535
  480.5 28.9 %all-to-all-start.5 = ((bf16[4,240,1024]{2,1,0:T(8,128)(2,1)}), bf16[4,240,1024]{2,1,0:T(8,128)(2,1)}, u32[]{:S(2)}, u32[]{:S(2)}) async-start(bf16[4,240,1024]{2,1,0:T(8,128)(2,1)} %bitcast.169), calls=%async_computation.5 | async-start | bytes 3932160 | tf_op jit(solution)/shard_map/all_to_all | solution.py:1081
  492.0 26.2 %copy-start.48 = (f32[384,4]{0,1:T(4,128)}, f32[384,4]{0,1:T(4,128)S(1)}, u32[]{:S(2)}) copy-start(f32[384,4]{0,1:T(4,128)S(1)} %get-tuple-element.125) | copy-start | bytes 18436
  492.0 26.2 %copy-start.60 = (f32[384]{0:T(512)}, f32[384]{0:T(512)S(1)}, u32[]{:S(2)}) copy-start(f32[384]{0:T(512)S(1)} %negate_add_fusion) | copy-start | bytes 4612
  512.8 68.1 %collective-permute-start.11 = (bf16[1056,1024]{1,0:T(8,128)(2,1)}, bf16[1056,1024]{1,0:T(8,128)(2,1)}, u32[]{:S(2)}, u32[]{:S(2)}) collective-permute-start(bf16[1056,1024]{1,0:T(8,128)(2,1)} %fusion.10), channel_id=1, source_target_pairs={{0,1},{2,0},{4,2},{6,4},{7,6},{5,7},{3,5},{1,3},{8,9},{10,8},{12,1... | collective-permute-start | bytes 6488072 | tf_op jit(solution)/shard_map/ppermute | solution.py:535
  516.6 64.4 %collective-permute-start.10 = (bf16[1056,1024]{1,0:T(8,128)(2,1)}, bf16[1056,1024]{1,0:T(8,128)(2,1)}, u32[]{:S(2)}, u32[]{:S(2)}) collective-permute-start(bf16[1056,1024]{1,0:T(8,128)(2,1)} %fusion.12), channel_id=1, source_target_pairs={{0,2},{2,4},{4,6},{6,7},{7,5},{5,3},{3,1},{1,0},{8,10},{10,12},{12... | collective-permute-start | bytes 6488072 | tf_op jit(solution)/shard_map/ppermute | solution.py:535
  584.4 48.4 %collective-permute-start.12 = (bf16[1056,1024]{1,0:T(8,128)(2,1)S(1)}, bf16[1056,1024]{1,0:T(8,128)(2,1)}, u32[]{:S(2)}, u32[]{:S(2)}) collective-permute-start(bf16[1056,1024]{1,0:T(8,128)(2,1)S(1)} %add_convert_fusion.3), channel_id=1, source_target_pairs={{0,2},{2,4},{4,6},{6,7},{7,5},{5,3},{3,1},{1,0},{8,10},{10,12},{12... | collective-permute-start | bytes 6488072 | tf_op jit(solution)/shard_map/ppermute | solution.py:535
  588.5 47.5 %collective-permute-start.13 = (bf16[1056,1024]{1,0:T(8,128)(2,1)S(1)}, bf16[1056,1024]{1,0:T(8,128)(2,1)}, u32[]{:S(2)}, u32[]{:S(2)}) collective-permute-start(bf16[1056,1024]{1,0:T(8,128)(2,1)S(1)} %add_convert_fusion.2), channel_id=1, source_target_pairs={{0,1},{2,0},{4,2},{6,4},{7,6},{5,7},{3,5},{1,3},{8,9},{10,8},{12,1... | collective-permute-start | bytes 6488072 | tf_op jit(solution)/shard_map/ppermute | solution.py:535
  636.0 89.1 %all-to-all-start.7 = ((bf16[8,384,384]{2,1,0:T(8,128)(2,1)}), bf16[8,384,384]{2,1,0:T(8,128)(2,1)}, u32[]{:S(2)}, u32[]{:S(2)}) async-start(bf16[8,384,384]{2,1,0:T(8,128)(2,1)} %get-tuple-element.63), calls=%async_computation.7 | async-start | bytes 4718592 | tf_op jit(solution)/shard_map/all_to_all | solution.py:1151
  645.2 77.3 %collective-permute-start.14 = (bf16[1056,1024]{1,0:T(8,128)(2,1)}, bf16[1056,1024]{1,0:T(8,128)(2,1)}, u32[]{:S(2)}, u32[]{:S(2)}) collective-permute-start(bf16[1056,1024]{1,0:T(8,128)(2,1)} %add_convert_fusion.1), channel_id=1, source_target_pairs={{0,2},{2,4},{4,6},{6,7},{7,5},{5,3},{3,1},{1,0},{8,10},{10,12},{12... | collective-permute-start | bytes 6488072 | tf_op jit(solution)/shard_map/ppermute | solution.py:535
  647.1 9.8 %copy-start.44 = (f32[384,4]{0,1:T(4,128)S(1)}, f32[384,4]{0,1:T(4,128)}, u32[]{:S(2)}) copy-start(f32[384,4]{0,1:T(4,128)} %copy-done.42) | copy-start | bytes 18436
  647.1 9.7 %copy-start.47 = (f32[1024]{0:T(1024)S(1)}, f32[1024]{0:T(1024)}, u32[]{:S(2)}) copy-start(f32[1024]{0:T(1024)} %copy-done.45) | copy-start | bytes 12292
  647.1 9.7 %copy-start.49 = (f32[384,4]{0,1:T(4,128)S(1)}, f32[384,4]{0,1:T(4,128)}, u32[]{:S(2)}) copy-start(f32[384,4]{0,1:T(4,128)} %copy-done.48) | copy-start | bytes 18436
  647.1 9.7 %copy-start.52 = (f32[384]{0:T(512)S(1)}, f32[384]{0:T(512)}, u32[]{:S(2)}) copy-start(f32[384]{0:T(512)} %copy-done.50) | copy-start | bytes 4612
  647.1 9.7 %copy-start.59 = (f32[384]{0:T(512)S(1)}, f32[384]{0:T(512)}, u32[]{:S(2)}) copy-start(f32[384]{0:T(512)} %copy-done.57) | copy-start | bytes 4612
  647.1 9.7 %copy-start.61 = (f32[384]{0:T(512)S(1)}, f32[384]{0:T(512)}, u32[]{:S(2)}) copy-start(f32[384]{0:T(512)} %copy-done.60) | copy-start | bytes 4612
  651.1 73.9 %collective-permute-start.15 = (bf16[1056,1024]{1,0:T(8,128)(2,1)}, bf16[1056,1024]{1,0:T(8,128)(2,1)}, u32[]{:S(2)}, u32[]{:S(2)}) collective-permute-start(bf16[1056,1024]{1,0:T(8,128)(2,1)} %add_convert_fusion), channel_id=1, source_target_pairs={{0,1},{2,0},{4,2},{6,4},{7,6},{5,7},{3,5},{1,3},{8,9},{10,8},{12,1... | collective-permute-start | bytes 6488072 | tf_op jit(solution)/shard_map/ppermute | solution.py:535
  749.7 82.6 %slice-start.1 = ((f32[384,1024]{1,0:T(8,128)}), f32[256,1024]{1,0:T(8,128)S(1)}, s32[]{:S(2)}) async-start(f32[384,1024]{1,0:T(8,128)} %copy-done.14), calls=%async_computation.9 | async-start | bytes 2097152 | tf_op jit(solution)/shard_map/slice | solution.py:1001
  (86 other events, 365.2 us)

commit v3 on v2

--- a/solution.py
+++ b/solution.py
@@ -6,6 +6,7 @@
 from jax.experimental import pallas as pl
 from jax.experimental.pallas import tpu as pltpu
 from jax.sharding import PartitionSpec as P
+
 
 D = 1024
 HEADS = 16
@@ -34,16 +35,6 @@
 def rms_scale(values, scale_row):
     inverse = lax.rsqrt(jnp.mean(values * values, axis=-1, keepdims=True) + EPSILON)
     return values * inverse * scale_row
-
-
-def gated_unit(gate_pre, up_pre):
-    return jax.nn.gelu(gate_pre, approximate=True) * up_pre
-
-
-def activation_grads(gate_pre, up_pre, grad_hidden):
-    activated, act_pull = jax.vjp(gated_unit, gate_pre, up_pre)
-    grad_gate_pre, grad_up_pre = act_pull(grad_hidden)
-    return (grad_gate_pre.astype(BF), grad_up_pre.astype(BF))
 
 
 def route_local(normed, router, routes):
@@ -102,7 +93,7 @@
             before = now
 
 
-def head_mask(sh, h, rows):
+def head_mask(sh, h):
     if sh.hp == 1:
         return None
     lane = lax.broadcasted_iota(jnp.int32, (1, sh.width), 1)
@@ -110,7 +101,7 @@
 
 
 def only_head(sh, h, x):
-    mask = head_mask(sh, h, x.shape[0])
+    mask = head_mask(sh, h)
     return x if mask is None else jnp.where(mask, x, jnp.zeros_like(x))
 
 
@@ -566,7 +557,7 @@
             self.chunks[self.count - s] = self.right
             self.chunks[s] = self.left
         else:
-            self.chunks[s] = jnp.concatenate([self.right, self.left], 0)
+            self.chunks[s] = (self.right, self.left)
 
     def tie(self, value):
         value, self.right, self.left = tied(value, self.right, self.left)
@@ -585,9 +576,7 @@
         count, s = self.count, self.done
         away = self.steps - s
         if s == 0:
-            far = self.part(away)
-            half = far.shape[0] // 2
-            send_left, send_right = far[:half], far[half:]
+            send_left, send_right = self.part(away)
         else:
             near_left = self.part(count - away).astype(F32)
             near_right = self.part(away).astype(F32)
@@ -772,7 +761,7 @@
     rows = x.shape[0]
     if count != 32 or lax.axis_size("fsdp") != 2 * DEEP:
         return lax.all_gather(x, ("expert", "fsdp"), axis=0, tiled=False)
-    cut = rows // 32 * 16 + 16 * (rows // 16 % 2)
+    cut = rows - 16
     return pl.pallas_call(
         functools.partial(dense_gather_kernel, cut),
         out_shape=jax.ShapeDtypeStruct((count,) + x.shape, x.dtype),
@@ -963,6 +952,245 @@
     )(x)
 
 
+SLICE = 256
+
+
+def gelu_terms(x):
+    root = 0.7978845608028654
+    square = x * x
+    t = jnp.tanh(root * (x + 0.044715 * square * x))
+    half = 0.5 * (1.0 + t)
+    slope = half + 0.5 * x * (1.0 - t * t) * (root * (1.0 + 3 * 0.044715 * square))
+    return x * half, slope
+
+
+def chunk_pieces(index, split, ff_shard):
+    if not split:
+        return [(0, m * ff_shard, m, index * ff_shard, ff_shard) for m in range(3)]
+    half = ff_shard // 2
+    base = index * ff_shard
+    return [
+        (0, 0, 0, base, ff_shard),
+        (0, ff_shard, 1, base, half),
+        (1, 0, 1, base + half, half),
+        (1, half, 2, base, ff_shard),
+    ]
+
+
+def chunk_copies(refs, whole, sems, ff_shard, outward):
+    count = len(refs) - 1
+    far = count // 2
+    out = []
+    for k in range(count):
+        own = refs[k : k + 1] if k < far else (refs[k : k + 2] if k == far else refs[k + 1 : k + 2])
+        pieces = []
+        for n, (src, at, m, row, rows) in enumerate(chunk_pieces(k, k == far, ff_shard)):
+            block = own[src].at[pl.ds(at, rows)]
+            spot = whole.at[m, pl.ds(row, rows)]
+            a, b = (spot, block) if outward else (block, spot)
+            pieces.append(pltpu.make_async_copy(a, b, sems.at[k, n]))
+        out.append(pieces)
+    return out
+
+
+def fetch_weights(refs, whole, sems, ff_shard, t):
+    copies = chunk_copies(refs, whole, sems, ff_shard, False)
+
+    @pl.when(t == 0)
+    def _():
+        for pieces in copies:
+            for c in pieces:
+                c.start()
+
+    for k, pieces in enumerate(copies):
+
+        @pl.when(t == k * ff_shard // SLICE)
+        def _(pieces=pieces):
+            for c in pieces:
+                c.wait()
+
+
+def ffn_forward_kernel(count, ff_shard, rows_ref, *refs):
+    chunks, (out_ref, gate_ref, up_ref, whole, acc, sems) = refs[: count + 1], refs[count + 1 :]
+    t = pl.program_id(0)
+    fetch_weights(chunks, whole, sems, ff_shard, t)
+    at = pl.ds(pl.multiple_of(t * SLICE, SLICE), SLICE)
+    rows = rows_ref[...]
+    gate = lax.dot_general(rows, whole[0, at], NT, preferred_element_type=F32)
+    up = lax.dot_general(rows, whole[1, at], NT, preferred_element_type=F32)
+    gate_ref[0] = gate
+    up_ref[0] = up
+    hidden = (gelu_terms(gate)[0] * up).astype(BF)
+    more = jnp.dot(hidden, whole[2, at], preferred_element_type=F32)
+
+    @pl.when(t == 0)
+    def _():
+        acc[...] = more
+
+    @pl.when(t > 0)
+    def _():
+        acc[...] += more
+
+    @pl.when(t == pl.num_programs(0) - 1)
+    def _():
+        out_ref[...] = acc[...].astype(BF)
+
+
+def ffn_backward_kernel(count, ff_shard, grad_ref, gate_ref, up_ref, *refs):
+    chunks, rest = refs[: count + 1], refs[count + 1 :]
+    out_ref, hid_ref, dgate_ref, dup_ref, whole, acc, sems = rest
+    t = pl.program_id(0)
+    fetch_weights(chunks, whole, sems, ff_shard, t)
+    at = pl.ds(pl.multiple_of(t * SLICE, SLICE), SLICE)
+    dhid = lax.dot_general(grad_ref[...], whole[2, at], NT, preferred_element_type=F32)
+    up = up_ref[0]
+    act, slope = gelu_terms(gate_ref[0])
+    hid_ref[0] = (act * up).astype(BF)
+    dgate = (dhid * up * slope).astype(BF)
+    dup = (dhid * act).astype(BF)
+    dgate_ref[0] = dgate
+    dup_ref[0] = dup
+    more = jnp.dot(dgate, whole[0, at], preferred_element_type=F32) + jnp.dot(
+        dup, whole[1, at], preferred_element_type=F32
+    )
+
+    @pl.when(t == 0)
+    def _():
+        acc[...] = more
+
+    @pl.when(t > 0)
+    def _():
+        acc[...] += more
+
+    @pl.when(t == pl.num_programs(0) - 1)
+    def _():
+        out_ref[...] = acc[...].astype(BF)
+
+
+def ffn_weights_kernel(count, ff_shard, rows_ref, grad_ref, hid_ref, dgate_ref, dup_ref, *refs):
+    chunks, (whole, sems) = refs[: count + 1], refs[count + 1 :]
+    t = pl.program_id(0)
+    at = pl.ds(pl.multiple_of(t * SLICE, SLICE), SLICE)
+    for m, (left, right) in enumerate(
+        ((dgate_ref, rows_ref), (dup_ref, rows_ref), (hid_ref, grad_ref))
+    ):
+        whole[m, at] = lax.dot_general(
+            left[0], right[...], TN, preferred_element_type=F32
+        ).astype(BF)
+    copies = chunk_copies(chunks, whole, sems, ff_shard, True)
+    for k, pieces in enumerate(copies):
+
+        @pl.when(t == ((k + 1) * ff_shard - 1) // SLICE)
+        def _(pieces=pieces):
+            for c in pieces:
+                c.start()
+
+    @pl.when(t == pl.num_programs(0) - 1)
+    def _():
+        for pieces in copies:
+            for c in pieces:
+                c.wait()
+
+
+def fixed(shape):
+    return pl.BlockSpec(shape, lambda t: (0,) * len(shape))
+
+
+def stepped(shape):
+    return pl.BlockSpec(shape, lambda t: (t, 0, 0))
+
+
+ANY_SPEC = pl.BlockSpec(memory_space=pl.ANY)
+
+
+def ffn_cost(slots, hidden):
+    work = 6 * slots * D * hidden
+    return pl.CostEstimate(flops=work, bytes_accessed=40 * 10**6, transcendentals=slots * hidden)
+
+
+def ffn_params():
+    return pltpu.CompilerParams(
+        dimension_semantics=("arbitrary",), vmem_limit_bytes=60 * 1024 * 1024
+    )
+
+
+def ffn_forward(rows, chunks, ff_shard):
+    slots, count = rows.shape[0], len(chunks) - 1
+    hidden = count * ff_shard
+    steps = hidden // SLICE
+    return pl.pallas_call(
+        functools.partial(ffn_forward_kernel, count, ff_shard),
+        grid=(steps,),
+        out_shape=(
+            jax.ShapeDtypeStruct((slots, D), BF),
+            jax.ShapeDtypeStruct((steps, slots, SLICE), F32),
+            jax.ShapeDtypeStruct((steps, slots, SLICE), F32),
+        ),
+        in_specs=[fixed((slots, D))] + [ANY_SPEC] * (count + 1),
+        out_specs=(
+            fixed((slots, D)),
+            stepped((1, slots, SLICE)),
+            stepped((1, slots, SLICE)),
+        ),
+        scratch_shapes=[
+            pltpu.VMEM((3, hidden, D), BF),
+            pltpu.VMEM((slots, D), F32),
+            pltpu.SemaphoreType.DMA((count, 4)),
+        ],
+        compiler_params=ffn_params(),
+        cost_estimate=ffn_cost(slots, hidden),
+        name="ffn_forward",
+    )(rows, *chunks)
+
+
+def ffn_backward(grad, gate, up, chunks, ff_shard):
+    slots, count = grad.shape[0], len(chunks) - 1
+    hidden = count * ff_shard
+    steps = hidden // SLICE
+    tile = jax.ShapeDtypeStruct((steps, slots, SLICE), BF)
+    return pl.pallas_call(
+        functools.partial(ffn_backward_kernel, count, ff_shard),
+        grid=(steps,),
+        out_shape=(jax.ShapeDtypeStruct((slots, D), BF), tile, tile, tile),
+        in_specs=[fixed((slots, D))]
+        + [stepped((1, slots, SLICE))] * 2
+        + [ANY_SPEC] * (count + 1),
+        out_specs=(fixed((slots, D)),) + (stepped((1, slots, SLICE)),) * 3,
+        scratch_shapes=[
+            pltpu.VMEM((3, hidden, D), BF),
+            pltpu.VMEM((slots, D), F32),
+            pltpu.SemaphoreType.DMA((count, 4)),
+        ],
+        compiler_params=ffn_params(),
+        cost_estimate=ffn_cost(slots, hidden),
+        name="ffn_backward",
+    )(grad, gate, up, *chunks)
+
+
+def ffn_weights(rows, grad, hid, dgate, dup, count, ff_shard):
+    slots = rows.shape[0]
+    hidden = count * ff_shard
+    steps = hidden // SLICE
+    full = jax.ShapeDtypeStruct((3 * ff_shard, D), BF)
+    half = jax.ShapeDtypeStruct((3 * ff_shard // 2, D), BF)
+    far = count // 2
+    shapes = [full] * far + [half] * 2 + [full] * (count - far - 1)
+    return pl.pallas_call(
+        functools.partial(ffn_weights_kernel, count, ff_shard),
+        grid=(steps,),
+        out_shape=tuple(shapes),
+        in_specs=[fixed((slots, D))] * 2 + [stepped((1, slots, SLICE))] * 3,
+        out_specs=(ANY_SPEC,) * (count + 1),
+        scratch_shapes=[
+            pltpu.VMEM((3, hidden, D), BF),
+            pltpu.SemaphoreType.DMA((count, 4)),
+        ],
+        compiler_params=ffn_params(),
+        cost_estimate=ffn_cost(slots, hidden),
+        name="ffn_weights",
+    )(rows, grad, hid, dgate, dup)
+
+
 def local(
     inputs,
     w_qkv,
@@ -1091,31 +1319,22 @@
     slot_grad = lax.dot_general(any_low, grad_rows_low, TN, preferred_element_type=F32)
     grad_result = swap_experts((slot_gate[:, None] * slot_grad).astype(BF))
 
-    gate_whole, up_whole, down_whole = (
-        jnp.concatenate([c[i * ff_shard : (i + 1) * ff_shard] for c in weights.chunks], 0)
-        for i in range(3)
-    )
-    gate_pre = lax.dot_general(expert_rows, gate_whole, NT, preferred_element_type=F32)
-    up_pre = lax.dot_general(expert_rows, up_whole, NT, preferred_element_type=F32)
-    hidden = gated_unit(gate_pre, up_pre).astype(BF)
-    result_rows = jnp.dot(hidden, down_whole, preferred_element_type=F32).astype(BF)
+    far = fsdp_count // 2
+    blocks = weights.chunks[:far] + list(weights.chunks[far]) + weights.chunks[far + 1 :]
+    result_rows, gate_pre, up_pre = ffn_forward(expert_rows, blocks, ff_shard)
     returned = swap_experts(result_rows)
-
-    grad_hidden = lax.dot_general(grad_result, down_whole, NT, preferred_element_type=F32)
-    grad_gate_pre, grad_up_pre = activation_grads(gate_pre, up_pre, grad_hidden)
-    grad_rows = jnp.dot(grad_gate_pre, gate_whole, preferred_element_type=F32) + jnp.dot(
-        grad_up_pre, up_whole, preferred_element_type=F32
-    )
-    grad_sent = swap_experts(grad_rows.astype(BF))
-    down_total = lax.dot_general(hidden, grad_result, TN, preferred_element_type=F32).astype(BF)
-    gate_total = lax.dot_general(
-        grad_gate_pre, expert_rows, TN, preferred_element_type=F32
-    ).astype(BF)
-    up_total = lax.dot_general(grad_up_pre, expert_rows, TN, preferred_element_type=F32).astype(BF)
+    grad_rows, hidden, grad_gate_pre, grad_up_pre = ffn_backward(
+        grad_result, gate_pre, up_pre, blocks, ff_shard
+    )
+    grad_sent = swap_experts(grad_rows)
+    totals = ffn_weights(
+        expert_rows, grad_result, hidden, grad_gate_pre, grad_up_pre, fsdp_count, ff_shard
+    )
 
     def part(k):
-        rows = slice(k * ff_shard, (k + 1) * ff_shard)
-        return jnp.concatenate([gate_total[rows], up_total[rows], down_total[rows]], 0)
+        if k == far:
+            return totals[far : far + 2]
+        return totals[k if k < far else k + 1]
 
     sums = RingScatter(part, fsdp_count)
     run(sums, spread[0])
@@ -1214,4 +1433,5 @@
         rows, rows, rows, flat, flat, rows, flat, cols, cols, deep, rows, rows, flat, P(), rows,
     )
     out_specs = (rows, rows, rows, rows, rows, flat, flat, rows, flat, cols, cols, deep)
+
     return jax.shard_map(local, mesh=mesh, in_specs=in_specs, out_specs=out_specs, check_vma=False)

time: 859 us -> 829 us (0.965)
  Pallas kernels: 231 us -> 341 us
  matrix products: 138 us -> 37.6 us
  local copies, waits for them, and re-layouts: 104 us -> 70.3 us
    pallas_call x0 -> x3, Pallas kernels: none -> 103 us  [the longest x1 45.6 us: ffn_backward(): pl.pallas_call(functools.partial(ffn_backward_kernel, count, ff_shard), g...]
    dot_general x9 -> x0, matrix products: 99.4 us -> none  [the longest x1 21.9 us: local(): lax.dot_general(expert_rows, gate_whole, NT, preferred_element_type=F32)]
    unnamed x234 -> x141, local copies, waits for them, and re-layouts: 31.2 us -> 11.6 us
    all_to_all x4, waiting for transfers between devices: 43.3 us -> 24.2 us  [swap_experts(): lax.all_to_all(rows, 'expert', split_axis=0, concat_axis=0, tiled=True)]
    ppermute x16, waiting for transfers between devices: 141 us -> 160 us  [ring_hop(): lax.ppermute(x, 'fsdp', [(ring[i], ring[(i + step) % count]) for i in ran...]
  transfers between devices with their start and end apart: 23 -> 23, of which waited for: 11 -> 10; matrix products, arithmetic and copies ran while one was open for 16% -> 9% of each run, Pallas kernels for 18% -> 32%
where the time goes in v3:
time: 829 us; the launch traced here: 819 us
  Pallas kernels  341 us (41%)
  waiting for transfers between devices  217 us (26%)
  local copies, waits for them, and re-layouts  70.3 us (8%)
  starting transfers between devices  62.5 us (8%)
  blocking collectives  50.7 us (6%)
  matrix products  37.6 us (5%)
  other arithmetic  35.9 us (4%)
    ppermute x16, waiting for transfers between devices, ring_hop(): lax.ppermute(x, 'fsdp', [(ring[i], ring[(i + step) % count]) for i in ran...  160 us
    pallas_call x1, Pallas kernels, dense_gather(): pl.pallas_call(functools.partial(dense_gather_kernel, cut), out_shape=jax...  91.3 us
    pallas_call x1, Pallas kernels, dense_sum(): pl.pallas_call(functools.partial(dense_sum_kernel, cut), out_shape=jax.Sh...  81.1 us
    all_to_all x1, blocking collectives, local(): lax.all_to_all(head_grad, 'fsdp', split_axis=0, concat_axis=0, tiled=True)  50.7 us
    pallas_call x1, Pallas kernels, ffn_backward(): pl.pallas_call(functools.partial(ffn_backward_kernel, count, ff_shard), g...  45.6 us
    pallas_call x1, Pallas kernels, attend_backward(): pl.pallas_call(functools.partial(attn_backward_kernel, sh), out_shape=(ja...  43.2 us
    all_to_all x1, waiting for transfers between devices, local(): lax.all_to_all(head_att, 'fsdp', split_axis=0, concat_axis=0, tiled=True)  33.2 us
    pallas_call x1, Pallas kernels, ffn_forward(): pl.pallas_call(functools.partial(ffn_forward_kernel, count, ff_shard), gr...  31.2 us
  transfers between devices with their start and end apart: 23, of which 10 were waited for; matrix products, arithmetic and copies ran while one was open for 9% of the time, Pallas kernels for 32%

profile of v3, /device:TPU:0, one launch (start us, length us, event | category | flops | bytes accessed | tf_op | source)
XLA Modules:
  0.0 819.3 jit_solution(14844282534738497273)
XLA Ops:
  2.5 3.0 collective-permute-start.1
  14.5 91.3 %dense_gather.1 = bf16[32,144,1024]{2,1,0:T(8,128)(2,1)} custom-call(bf16[144,1024]{1,0:T(8,128)(2,1)} %copy-done.27), custom_call_target="tpu_custom_call" | custom-call | bytes 100000000 | tf_op jit(solution)/shard_map/dense_gather/pallas_call | solution.py:765
  107.4 5.2 fusion.60
  113.2 3.1 fusion.6
  116.9 2.9 copy.55
  119.8 4.3 copy.56
  124.1 5.0 all-to-all-start
  131.5 84.0 %collective-permute-done.2.refs_7_ = bf16[1056,1024]{1,0:T(8,128)(2,1)} collective-permute-done((bf16[1056,1024]{1,0:T(8,128)(2,1)}, bf16[1056,1024]{1,0:T(8,128)(2,1)}, u32[]{:S(2)}, u32[]{:S(2)}) %collective-permute-start.2) | collective-permute-done | bytes 2162720 | tf_op jit(solution)/shard_map/ppermute | solution.py:526
  216.5 14.1 %collective-permute-start.4 = (bf16[1056,1024]{1,0:T(8,128)(2,1)}, bf16[1056,1024]{1,0:T(8,128)(2,1)}, u32[]{:S(2)}, u32[]{:S(2)}) collective-permute-start(bf16[1056,1024]{1,0:T(8,128)(2,1)} %collective-permute-done.2.refs_7_), channel_id=1, source_target_pairs={{0,2},{2,4},{4,6},{6,7},{7,5},{5,3},{3,1},{1,0},{8,10},{10,12},{12... | collective-permute-start | bytes 6488072 | tf_op jit(solution)/shard_map/ppermute | solution.py:526
  230.6 23.1 %attend_forward.1 = (bf16[8,384,128]{2,1,0:T(8,128)(2,1)}, f32[12,128,256]{2,1,0:T(8,128)S(1)}, f32[12,8,256]{2,1,0:T(8,128)S(1)}) custom-call(s32[8]{0:T(128)S(1)} %bitcast_convert_fusion.1.group_ref, f32[2,32]{1,0:T(2,128)S(1)} %bitcast_convert_fusion.table_ref, s32[9,128]{1,0:T(8,128)S(1)} %bitcast.104, bf16[8,384,384]{2,1,0:T(8,128)(2,1)S(1)} %all-to-all-done.x_ref), custom_call_target="tpu_custom_call" | custom-call | flops 10000000000 | bytes 8000000 | tf_op jit(solution)/shard_map/attend_forward/pallas_call | solution.py:465
  254.9 4.4 all-to-all-start.1
  264.0 33.2 %all-to-all-done.1 = bf16[8,384,128]{2,1,0:T(8,128)(2,1)S(1)} async-done(((bf16[8,384,128]{2,1,0:T(8,128)(2,1)}), bf16[8,384,128]{2,1,0:T(8,128)(2,1)S(1)}, u32[]{:S(2)}, u32[]{:S(2)}) %all-to-all-start.1) | async-done | bytes 786464 | tf_op jit(solution)/shard_map/all_to_all | solution.py:1285
  297.6 2.6 slice.208
  300.3 2.3 slice.209
  307.4 2.7 convolution_convert_fusion.3
  310.2 4.6 all-to-all-start.2
  316.7 2.5 multiply_convert_fusion
  319.1 20.0 %all-to-all-done.2 = bf16[4,240,1024]{2,1,0:T(8,128)(2,1)} async-done(((bf16[4,240,1024]{2,1,0:T(8,128)(2,1)}), bf16[4,240,1024]{2,1,0:T(8,128)(2,1)}, u32[]{:S(2)}, u32[]{:S(2)}) %all-to-all-start.2) | async-done | bytes 1966112 | tf_op jit(solution)/shard_map/all_to_all | solution.py:1309
  339.1 4.4 all-to-all-start.4
  343.6 31.2 %ffn_forward.1 = (bf16[960,1024]{1,0:T(8,128)(2,1)}, f32[11,960,256]{2,1,0:T(8,128)}, f32[11,960,256]{2,1,0:T(8,128)}) custom-call(bf16[960,1024]{1,0:T(8,128)(2,1)} %bitcast.23.rows_ref, bf16[1056,1024]{1,0:T(8,128)(2,1)} %copy-done.18, bf16[1056,1024]{1,0:T(8,128)(2,1)} %collective-permute-done.1.refs_1_, ...), custom_call_target="tpu_custom_call" | custom-call | flops 16609443840 | bytes 40000000 | tf_op jit(solution)/shard_map/ffn_forward/pallas_call | solution.py:1121
  374.7 4.7 all-to-all-start.3
  379.4 45.6 %ffn_backward.1 = (bf16[960,1024]{1,0:T(8,128)(2,1)}, bf16[11,960,256]{2,1,0:T(8,128)(2,1)}, bf16[11,960,256]{2,1,0:T(8,128)(2,1)}, bf16[11,960,256]{2,1,0:T(8,128)(2,1)}) custom-call(bf16[960,1024]{1,0:T(8,128)(2,1)} %bitcast.34.grad_ref, f32[11,960,256]{2,1,0:T(8,128)} %get-tuple-element.71.gate_ref, f32[11,960,256]{2,1,0:T(8,128)} %get-tuple-element.72.up_ref, ...), custom_call_target="tpu_custom_call" | custom-call | flops 16609443840 | bytes 40000000 | tf_op jit(solution)/shard_map/ffn_backward/pallas_call | solution.py:1151
  425.0 26.0 %ffn_weights.1 = (bf16[1056,1024]{1,0:T(8,128)(2,1)}, bf16[1056,1024]{1,0:T(8,128)(2,1)}, bf16[1056,1024]{1,0:T(8,128)(2,1)}, bf16[1056,1024]{1,0:T(8,128)(2,1)}...) custom-call(bf16[960,1024]{1,0:T(8,128)(2,1)} %bitcast.23.rows_ref, ...), custom_call_target="tpu_custom_call" | custom-call | flops 16609443840 | bytes 40000000 | tf_op jit(solution)/shard_map/ffn_weights/pallas_call | solution.py:1178
  451.0 2.4 slice.215
  455.6 4.4 all-to-all-start.5
  460.1 2.6 fusion.14
  462.7 3.7 fusion.9
  466.6 13.5 %collective-permute-done.8 = bf16[528,1024]{1,0:T(8,128)(2,1)} collective-permute-done((bf16[528,1024]{1,0:T(8,128)(2,1)}, bf16[528,1024]{1,0:T(8,128)(2,1)}, u32[]{:S(2)}, u32[]{:S(2)}) %collective-permute-start.8) | collective-permute-done | bytes 1081376 | tf_op jit(solution)/shard_map/ppermute | solution.py:526
  480.2 4.2 all-to-all-done.5
  494.6 3.5 multiply_reduce_fusion
  506.3 50.7 %all_to_all.40.do_ref = bf16[8,384,128]{2,1,0:T(8,128)(2,1)S(1)} all-to-all(bf16[8,384,128]{2,1,0:T(8,128)(2,1)} %bitcast.131), channel_id=1, replica_groups=mesh['expert'=4,'fsdp'=8] {'fsdp'}, dimensions={0} | all-to-all | bytes 1572864 | tf_op jit(solution)/shard_map/all_to_all | solution.py:1362
  557.0 3.4 add_convert_fusion.3
  560.5 2.7 add_convert_fusion.2
  563.2 2.5 collective-permute-start.13
  565.7 43.2 %attend_backward.1 = (bf16[8,384,384]{2,1,0:T(8,128)(2,1)}, f32[64,128]{1,0:T(8,128)S(1)}) custom-call(s32[8]{0:T(128)S(1)} %bitcast_convert_fusion.1.group_ref, f32[2,32]{1,0:T(2,128)S(1)} %bitcast_convert_fusion.table_ref, s32[9,128]{1,0:T(8,128)S(1)} %bitcast.105, bf16[8,384,384]{2,1,0:T(8,128)(2,1)} %copy-done, ...), custom_call_target="tpu_custom_call" | custom-call | flops 20000000000 | bytes 12000000 | tf_op jit(solution)/shard_map/attend_backward/pallas_call | solution.py:490
  608.9 2.4 collective-permute-done.13
  611.4 4.4 all-to-all-start.7
  615.8 4.7 add_convert_fusion.1
  622.4 4.0 add_convert_fusion
  634.5 2.4 copy.60
  639.2 2.6 convolution_convert_fusion.2
  642.0 56.5 %collective-permute-done.14 = bf16[1056,1024]{1,0:T(8,128)(2,1)} collective-permute-done((bf16[1056,1024]{1,0:T(8,128)(2,1)}, bf16[1056,1024]{1,0:T(8,128)(2,1)}, u32[]{:S(2)}, u32[]{:S(2)}) %collective-permute-start.14) | collective-permute-done | bytes 2162720 | tf_op jit(solution)/shard_map/ppermute | solution.py:526
  700.6 4.3 copy.64
  706.9 5.2 fusion.8
  712.5 5.8 convolution_convert_fusion
  719.1 3.6 fusion.61
  725.1 81.1 %dense_sum.1 = f32[144,1024]{1,0:T(8,128)S(1)} custom-call(bf16[32,144,1024]{2,1,0:T(8,128)(2,1)S(1)} %constant_dynamic-update-slice_fusion.2.g_ref), custom_call_target="tpu_custom_call" | custom-call | bytes 100000000 | tf_op jit(solution)/shard_map/dense_sum/pallas_call | solution.py:930
  809.7 4.4 convert_add_fusion
  (280 shorter events, 77.0 us)
Async XLA Ops:
  2.5 8.8 %copy-start.18 = (bf16[1056,1024]{1,0:T(8,128)(2,1)}, bf16[1056,1024]{1,0:T(8,128)(2,1)S(1)}, u32[]{:S(2)}) copy-start(bf16[1056,1024]{1,0:T(8,128)(2,1)S(1)} %pad_maximum_fusion.1.refs_0_) | copy-start | bytes 6488068
  2.5 110.7 %collective-permute-start.1 = (bf16[1056,1024]{1,0:T(8,128)(2,1)S(1)}, bf16[1056,1024]{1,0:T(8,128)(2,1)}, u32[]{:S(2)}, u32[]{:S(2)}) collective-permute-start(bf16[1056,1024]{1,0:T(8,128)(2,1)S(1)} %pad_maximum_fusion.1.refs_0_), channel_id=1, source_target_pairs={{0,1},{2,0},{4,2},{6,4},{7,6},{5,7},{3,5},{1,3},{8,9},{10,8},{12,1... | collective-permute-start | bytes 6488072 | tf_op jit(solution)/shard_map/ppermute | solution.py:526
  5.5 107.7 %collective-permute-start = (bf16[1056,1024]{1,0:T(8,128)(2,1)S(1)}, bf16[1056,1024]{1,0:T(8,128)(2,1)}, u32[]{:S(2)}, u32[]{:S(2)}) collective-permute-start(bf16[1056,1024]{1,0:T(8,128)(2,1)S(1)} %pad_maximum_fusion.1.refs_0_), channel_id=1, source_target_pairs={{0,2},{2,4},{4,6},{6,7},{7,5},{5,3},{3,1},{1,0},{8,10},{10,12},{12... | collective-permute-start | bytes 6488072 | tf_op jit(solution)/shard_map/ppermute | solution.py:526
  10.4 294.3 %copy-start.5 = (bf16[128,2,1024]{2,0,1:T(8,128)(2,1)}, bf16[128,2,1024]{2,0,1:T(8,128)(2,1)S(1)}, u32[]{:S(2)}) copy-start(bf16[128,2,1024]{2,0,1:T(8,128)(2,1)S(1)} %copy.53) | copy-start | bytes 1572868
  124.1 106.6 %copy-start.1 = (s32[1152]{0:T(1024)S(1)}, s32[1152]{0:T(1024)}, u32[]{:S(2)}) copy-start(s32[1152]{0:T(1024)} %param.29) | copy-start | bytes 13828
  124.1 92.4 %all-to-all-start = ((bf16[8,384,384]{2,1,0:T(8,128)(2,1)}), bf16[8,384,384]{2,1,0:T(8,128)(2,1)S(1)}, u32[]{:S(2)}, u32[]{:S(2)}) async-start(bf16[8,384,384]{2,1,0:T(8,128)(2,1)} %copy.56), calls=%async_computation | async-start | bytes 4718592 | tf_op jit(solution)/shard_map/all_to_all | solution.py:1281
  129.0 86.5 %collective-permute-start.2 = (bf16[1056,1024]{1,0:T(8,128)(2,1)}, bf16[1056,1024]{1,0:T(8,128)(2,1)}, u32[]{:S(2)}, u32[]{:S(2)}) collective-permute-start(bf16[1056,1024]{1,0:T(8,128)(2,1)} %collective-permute-done.refs_8_), channel_id=1, source_target_pairs={{0,2},{2,4},{4,6},{6,7},{7,5},{5,3},{3,1},{1,0},{8,10},{10,12},{12... | collective-permute-start | bytes 6488072 | tf_op jit(solution)/shard_map/ppermute | solution.py:526
  131.0 85.4 %collective-permute-start.3 = (bf16[1056,1024]{1,0:T(8,128)(2,1)}, bf16[1056,1024]{1,0:T(8,128)(2,1)}, u32[]{:S(2)}, u32[]{:S(2)}) collective-permute-start(bf16[1056,1024]{1,0:T(8,128)(2,1)} %collective-permute-done.1.refs_1_), channel_id=1, source_target_pairs={{0,1},{2,0},{4,2},{6,4},{7,6},{5,7},{3,5},{1,3},{8,9},{10,8},{12,1... | collective-permute-start | bytes 6488072 | tf_op jit(solution)/shard_map/ppermute | solution.py:526
  216.5 37.3 %copy-start = (bf16[8,384,384]{2,1,0:T(8,128)(2,1)}, bf16[8,384,384]{2,1,0:T(8,128)(2,1)S(1)}, u32[]{:S(2)}) copy-start(bf16[8,384,384]{2,1,0:T(8,128)(2,1)S(1)} %all-to-all-done.x_ref) | copy-start | bytes 7077892
  216.5 80.8 %collective-permute-start.4 = (bf16[1056,1024]{1,0:T(8,128)(2,1)}, bf16[1056,1024]{1,0:T(8,128)(2,1)}, u32[]{:S(2)}, u32[]{:S(2)}) collective-permute-start(bf16[1056,1024]{1,0:T(8,128)(2,1)} %collective-permute-done.2.refs_7_), channel_id=1, source_target_pairs={{0,2},{2,4},{4,6},{6,7},{7,5},{5,3},{3,1},{1,0},{8,10},{10,12},{12... | collective-permute-start | bytes 6488072 | tf_op jit(solution)/shard_map/ppermute | solution.py:526
  230.6 66.6 %collective-permute-start.5 = (bf16[1056,1024]{1,0:T(8,128)(2,1)}, bf16[1056,1024]{1,0:T(8,128)(2,1)}, u32[]{:S(2)}, u32[]{:S(2)}) collective-permute-start(bf16[1056,1024]{1,0:T(8,128)(2,1)} %collective-permute-done.3.refs_2_), channel_id=1, source_target_pairs={{0,1},{2,0},{4,2},{6,4},{7,6},{5,7},{3,5},{1,3},{8,9},{10,8},{12,1... | collective-permute-start | bytes 6488072 | tf_op jit(solution)/shard_map/ppermute | solution.py:526
  230.6 28.7 %copy-start.52 = (s32[384,2]{0,1:T(2,128)S(1)}, s32[384,2]{0,1:T(2,128)}, u32[]{:S(2)}) copy-start(s32[384,2]{0,1:T(2,128)} %param.26) | copy-start | bytes 9220
  230.6 28.7 %copy-start.53 = (s32[384,2]{0,1:T(2,128)S(1)}, s32[384,2]{0,1:T(2,128)}, u32[]{:S(2)}) copy-start(s32[384,2]{0,1:T(2,128)} %param.27) | copy-start | bytes 9220
  254.9 6.6 slice-start.2
  254.9 42.3 %all-to-all-start.1 = ((bf16[8,384,128]{2,1,0:T(8,128)(2,1)}), bf16[8,384,128]{2,1,0:T(8,128)(2,1)S(1)}, u32[]{:S(2)}, u32[]{:S(2)}) async-start(bf16[8,384,128]{2,1,0:T(8,128)(2,1)} %get-tuple-element.61), calls=%async_computation.1 | async-start | bytes 1572864 | tf_op jit(solution)/shard_map/all_to_all | solution.py:1285
  262.8 235.4 %copy-start.30 = (f32[1024]{0:T(1024)}, f32[1024]{0:T(1024)S(1)}, u32[]{:S(2)}) copy-start(f32[1024]{0:T(1024)S(1)} %reshape.324) | copy-start | bytes 12292
  264.0 43.4 %copy-start.54 = (s32[384]{0:T(512)}, s32[384]{0:T(512)S(1)}, u32[]{:S(2)}) copy-start(s32[384]{0:T(512)S(1)} %get-tuple-element.154) | copy-start | bytes 4612
  264.0 43.4 %copy-start.56 = (s32[384]{0:T(512)}, s32[384]{0:T(512)S(1)}, u32[]{:S(2)}) copy-start(s32[384]{0:T(512)S(1)} %get-tuple-element.155) | copy-start | bytes 4612
  297.6 7.1 copy-start.9
  297.6 7.1 copy-start.7
  302.5 41.0 %collective-permute-start.7 = (bf16[528,1024]{1,0:T(8,128)(2,1)}, bf16[528,1024]{1,0:T(8,128)(2,1)}, u32[]{:S(2)}, u32[]{:S(2)}) collective-permute-start(bf16[528,1024]{1,0:T(8,128)(2,1)} %slice.209), channel_id=1, source_target_pairs={{0,1},{2,0},{4,2},{6,4},{7,6},{5,7},{3,5},{1,3},{8,9},{10,8},{12,1... | collective-permute-start | bytes 3244040 | tf_op jit(solution)/shard_map/ppermute | solution.py:526
  303.0 40.6 %collective-permute-start.6 = (bf16[528,1024]{1,0:T(8,128)(2,1)}, bf16[528,1024]{1,0:T(8,128)(2,1)}, u32[]{:S(2)}, u32[]{:S(2)}) collective-permute-start(bf16[528,1024]{1,0:T(8,128)(2,1)} %slice.208), channel_id=1, source_target_pairs={{0,2},{2,4},{4,6},{6,7},{7,5},{5,3},{3,1},{1,0},{8,10},{10,12},{12... | collective-permute-start | bytes 3244040 | tf_op jit(solution)/shard_map/ppermute | solution.py:526
  306.4 191.7 %copy-start.36 = (f32[384]{0:T(512)}, f32[384]{0:T(512)S(1)}, u32[]{:S(2)}) copy-start(f32[384]{0:T(512)S(1)} %fusion.52) | copy-start | bytes 4612
  307.4 186.3 %copy-start.28 = (f32[384,4]{0,1:T(4,128)}, f32[384,4]{0,1:T(4,128)S(1)}, u32[]{:S(2)}) copy-start(f32[384,4]{0,1:T(4,128)S(1)} %get-tuple-element.188) | copy-start | bytes 18436
  310.2 28.9 %all-to-all-start.2 = ((bf16[4,240,1024]{2,1,0:T(8,128)(2,1)}), bf16[4,240,1024]{2,1,0:T(8,128)(2,1)}, u32[]{:S(2)}, u32[]{:S(2)}) async-start(bf16[4,240,1024]{2,1,0:T(8,128)(2,1)} %bitcast.140), calls=%async_computation.2 | async-start | bytes 3932160 | tf_op jit(solution)/shard_map/all_to_all | solution.py:1309
  314.8 178.9 %copy-start.34 = (f32[384]{0:T(512)}, f32[384]{0:T(512)S(1)}, u32[]{:S(2)}) copy-start(f32[384]{0:T(512)S(1)} %is-finite_select_fusion) | copy-start | bytes 4612
  339.1 35.6 %all-to-all-start.4 = ((bf16[4,240,1024]{2,1,0:T(8,128)(2,1)}), bf16[4,240,1024]{2,1,0:T(8,128)(2,1)}, u32[]{:S(2)}, u32[]{:S(2)}) async-start(bf16[4,240,1024]{2,1,0:T(8,128)(2,1)} %bitcast.141), calls=%async_computation.4 | async-start | bytes 3932160 | tf_op jit(solution)/shard_map/all_to_all | solution.py:1309
  374.7 80.9 %all-to-all-start.3 = ((bf16[4,240,1024]{2,1,0:T(8,128)(2,1)}), bf16[4,240,1024]{2,1,0:T(8,128)(2,1)}, u32[]{:S(2)}, u32[]{:S(2)}) async-start(bf16[4,240,1024]{2,1,0:T(8,128)(2,1)} %bitcast.139), calls=%async_computation.3 | async-start | bytes 3932160 | tf_op jit(solution)/shard_map/all_to_all | solution.py:1309
  453.5 26.6 %collective-permute-start.8 = (bf16[528,1024]{1,0:T(8,128)(2,1)}, bf16[528,1024]{1,0:T(8,128)(2,1)}, u32[]{:S(2)}, u32[]{:S(2)}) collective-permute-start(bf16[528,1024]{1,0:T(8,128)(2,1)} %get-tuple-element.77), channel_id=1, source_target_pairs={{0,2},{2,4},{4,6},{6,7},{7,5},{5,3},{3,1},{1,0},{8,10},{10,12},{12... | collective-permute-start | bytes 3244040 | tf_op jit(solution)/shard_map/ppermute | solution.py:526
  453.6 26.6 %collective-permute-start.9 = (bf16[528,1024]{1,0:T(8,128)(2,1)}, bf16[528,1024]{1,0:T(8,128)(2,1)}, u32[]{:S(2)}, u32[]{:S(2)}) collective-permute-start(bf16[528,1024]{1,0:T(8,128)(2,1)} %get-tuple-element.78), channel_id=1, source_target_pairs={{0,1},{2,0},{4,2},{6,4},{7,6},{5,7},{3,5},{1,3},{8,9},{10,8},{12,1... | collective-permute-start | bytes 3244040 | tf_op jit(solution)/shard_map/ppermute | solution.py:526
  455.6 28.8 %all-to-all-start.5 = ((bf16[4,240,1024]{2,1,0:T(8,128)(2,1)}), bf16[4,240,1024]{2,1,0:T(8,128)(2,1)}, u32[]{:S(2)}, u32[]{:S(2)}) async-start(bf16[4,240,1024]{2,1,0:T(8,128)(2,1)} %bitcast.138), calls=%async_computation.5 | async-start | bytes 3932160 | tf_op jit(solution)/shard_map/all_to_all | solution.py:1309
  466.6 27.1 %copy-start.32 = (f32[384,4]{0,1:T(4,128)}, f32[384,4]{0,1:T(4,128)S(1)}, u32[]{:S(2)}) copy-start(f32[384,4]{0,1:T(4,128)S(1)} %get-tuple-element.157) | copy-start | bytes 18436
  466.6 27.1 %copy-start.38 = (f32[384]{0:T(512)}, f32[384]{0:T(512)S(1)}, u32[]{:S(2)}) copy-start(f32[384]{0:T(512)S(1)} %negate_add_fusion) | copy-start | bytes 4612
  489.8 67.1 %collective-permute-start.10 = (bf16[1056,1024]{1,0:T(8,128)(2,1)}, bf16[1056,1024]{1,0:T(8,128)(2,1)}, u32[]{:S(2)}, u32[]{:S(2)}) collective-permute-start(bf16[1056,1024]{1,0:T(8,128)(2,1)} %pad_maximum_fusion.2), channel_id=1, source_target_pairs={{0,2},{2,4},{4,6},{6,7},{7,5},{5,3},{3,1},{1,0},{8,10},{10,12},{12... | collective-permute-start | bytes 6488072 | tf_op jit(solution)/shard_map/ppermute | solution.py:526
  491.5 65.4 %collective-permute-start.11 = (bf16[1056,1024]{1,0:T(8,128)(2,1)}, bf16[1056,1024]{1,0:T(8,128)(2,1)}, u32[]{:S(2)}, u32[]{:S(2)}) collective-permute-start(bf16[1056,1024]{1,0:T(8,128)(2,1)} %pad_maximum_fusion.3), channel_id=1, source_target_pairs={{0,1},{2,0},{4,2},{6,4},{7,6},{5,7},{3,5},{1,3},{8,9},{10,8},{12,1... | collective-permute-start | bytes 6488072 | tf_op jit(solution)/shard_map/ppermute | solution.py:526
  560.4 48.6 %collective-permute-start.12 = (bf16[1056,1024]{1,0:T(8,128)(2,1)S(1)}, bf16[1056,1024]{1,0:T(8,128)(2,1)}, u32[]{:S(2)}, u32[]{:S(2)}) collective-permute-start(bf16[1056,1024]{1,0:T(8,128)(2,1)S(1)} %add_convert_fusion.3), channel_id=1, source_target_pairs={{0,2},{2,4},{4,6},{6,7},{7,5},{5,3},{3,1},{1,0},{8,10},{10,12},{12... | collective-permute-start | bytes 6488072 | tf_op jit(solution)/shard_map/ppermute | solution.py:526
  563.2 48.1 %collective-permute-start.13 = (bf16[1056,1024]{1,0:T(8,128)(2,1)S(1)}, bf16[1056,1024]{1,0:T(8,128)(2,1)}, u32[]{:S(2)}, u32[]{:S(2)}) collective-permute-start(bf16[1056,1024]{1,0:T(8,128)(2,1)S(1)} %add_convert_fusion.2), channel_id=1, source_target_pairs={{0,1},{2,0},{4,2},{6,4},{7,6},{5,7},{3,5},{1,3},{8,9},{10,8},{12,1... | collective-permute-start | bytes 6488072 | tf_op jit(solution)/shard_map/ppermute | solution.py:526
  611.4 89.2 %all-to-all-start.7 = ((bf16[8,384,384]{2,1,0:T(8,128)(2,1)}), bf16[8,384,384]{2,1,0:T(8,128)(2,1)}, u32[]{:S(2)}, u32[]{:S(2)}) async-start(bf16[8,384,384]{2,1,0:T(8,128)(2,1)} %get-tuple-element.92), calls=%async_computation.7 | async-start | bytes 4718592 | tf_op jit(solution)/shard_map/all_to_all | solution.py:1370
  615.8 6.6 copy-start.14
  620.5 78.0 %collective-permute-start.14 = (bf16[1056,1024]{1,0:T(8,128)(2,1)}, bf16[1056,1024]{1,0:T(8,128)(2,1)}, u32[]{:S(2)}, u32[]{:S(2)}) collective-permute-start(bf16[1056,1024]{1,0:T(8,128)(2,1)} %add_convert_fusion.1), channel_id=1, source_target_pairs={{0,2},{2,4},{4,6},{6,7},{7,5},{5,3},{3,1},{1,0},{8,10},{10,12},{12... | collective-permute-start | bytes 6488072 | tf_op jit(solution)/shard_map/ppermute | solution.py:526
  622.4 10.4 %copy-start.29 = (f32[384,4]{0,1:T(4,128)S(1)}, f32[384,4]{0,1:T(4,128)}, u32[]{:S(2)}) copy-start(f32[384,4]{0,1:T(4,128)} %copy-done.28) | copy-start | bytes 18436
  622.4 10.4 %copy-start.31 = (f32[1024]{0:T(1024)S(1)}, f32[1024]{0:T(1024)}, u32[]{:S(2)}) copy-start(f32[1024]{0:T(1024)} %copy-done.30) | copy-start | bytes 12292
  622.4 10.4 %copy-start.33 = (f32[384,4]{0,1:T(4,128)S(1)}, f32[384,4]{0,1:T(4,128)}, u32[]{:S(2)}) copy-start(f32[384,4]{0,1:T(4,128)} %copy-done.32) | copy-start | bytes 18436
  622.4 10.4 %copy-start.35 = (f32[384]{0:T(512)S(1)}, f32[384]{0:T(512)}, u32[]{:S(2)}) copy-start(f32[384]{0:T(512)} %copy-done.34) | copy-start | bytes 4612
  622.4 10.4 %copy-start.37 = (f32[384]{0:T(512)S(1)}, f32[384]{0:T(512)}, u32[]{:S(2)}) copy-start(f32[384]{0:T(512)} %copy-done.36) | copy-start | bytes 4612
  622.4 10.4 %copy-start.39 = (f32[384]{0:T(512)S(1)}, f32[384]{0:T(512)}, u32[]{:S(2)}) copy-start(f32[384]{0:T(512)} %copy-done.38) | copy-start | bytes 4612
  626.4 74.1 %collective-permute-start.15 = (bf16[1056,1024]{1,0:T(8,128)(2,1)}, bf16[1056,1024]{1,0:T(8,128)(2,1)}, u32[]{:S(2)}, u32[]{:S(2)}) collective-permute-start(bf16[1056,1024]{1,0:T(8,128)(2,1)} %add_convert_fusion), channel_id=1, source_target_pairs={{0,1},{2,0},{4,2},{6,4},{7,6},{5,7},{3,5},{1,3},{8,9},{10,8},{12,1... | collective-permute-start | bytes 6488072 | tf_op jit(solution)/shard_map/ppermute | solution.py:526
  725.1 83.0 %slice-start.1 = ((f32[384,1024]{1,0:T(8,128)}), f32[256,1024]{1,0:T(8,128)S(1)}, s32[]{:S(2)}) async-start(f32[384,1024]{1,0:T(8,128)} %copy-done.12), calls=%async_computation.9 | async-start | bytes 2097152 | tf_op jit(solution)/shard_map/slice | solution.py:1229
  (44 other events, 179.2 us)

commit v4 on v3

--- a/solution.py
+++ b/solution.py
@@ -572,7 +572,7 @@
         self.done = 0
         self.steps = count // 2
 
-    def step(self):
+    def step(self, after=None):
         count, s = self.count, self.done
         away = self.steps - s
         if s == 0:
@@ -591,9 +591,13 @@
             else:
                 send_left = near_left + self.left.astype(F32)
                 send_right = near_right + self.right.astype(F32)
-        self.left = ring_hop(send_left.astype(BF), count, -1)
-        self.right = ring_hop(send_right.astype(BF), count, 1)
+        send_left, send_right = send_left.astype(BF), send_right.astype(BF)
+        if after is not None:
+            after, send_left, send_right = tied(after, send_left, send_right)
+        self.left = ring_hop(send_left, count, -1)
+        self.right = ring_hop(send_right, count, 1)
         self.done += 1
+        return after
 
     def tie(self, value):
         value, self.right, self.left = tied(value, self.right, self.left)
@@ -761,7 +765,7 @@
     rows = x.shape[0]
     if count != 32 or lax.axis_size("fsdp") != 2 * DEEP:
         return lax.all_gather(x, ("expert", "fsdp"), axis=0, tiled=False)
-    cut = rows - 16
+    cut = rows // 32 * 16 + 16 * (rows // 16 % 2)
     return pl.pallas_call(
         functools.partial(dense_gather_kernel, cut),
         out_shape=jax.ShapeDtypeStruct((count,) + x.shape, x.dtype),
@@ -1011,16 +1015,19 @@
 
 
 def ffn_forward_kernel(count, ff_shard, rows_ref, *refs):
-    chunks, (out_ref, gate_ref, up_ref, whole, acc, sems) = refs[: count + 1], refs[count + 1 :]
+    chunks, rest = refs[: count + 1], refs[count + 1 :]
+    out_ref, act_ref, turn_ref, hid_ref, whole, acc, sems = rest
     t = pl.program_id(0)
     fetch_weights(chunks, whole, sems, ff_shard, t)
     at = pl.ds(pl.multiple_of(t * SLICE, SLICE), SLICE)
     rows = rows_ref[...]
     gate = lax.dot_general(rows, whole[0, at], NT, preferred_element_type=F32)
     up = lax.dot_general(rows, whole[1, at], NT, preferred_element_type=F32)
-    gate_ref[0] = gate
-    up_ref[0] = up
-    hidden = (gelu_terms(gate)[0] * up).astype(BF)
+    act, slope = gelu_terms(gate)
+    hidden = (act * up).astype(BF)
+    act_ref[0] = act
+    turn_ref[0] = up * slope
+    hid_ref[0] = hidden
     more = jnp.dot(hidden, whole[2, at], preferred_element_type=F32)
 
     @pl.when(t == 0)
@@ -1036,18 +1043,15 @@
         out_ref[...] = acc[...].astype(BF)
 
 
-def ffn_backward_kernel(count, ff_shard, grad_ref, gate_ref, up_ref, *refs):
+def ffn_backward_kernel(count, ff_shard, grad_ref, act_ref, turn_ref, *refs):
     chunks, rest = refs[: count + 1], refs[count + 1 :]
-    out_ref, hid_ref, dgate_ref, dup_ref, whole, acc, sems = rest
+    out_ref, dgate_ref, dup_ref, whole, acc, sems = rest
     t = pl.program_id(0)
     fetch_weights(chunks, whole, sems, ff_shard, t)
     at = pl.ds(pl.multiple_of(t * SLICE, SLICE), SLICE)
     dhid = lax.dot_general(grad_ref[...], whole[2, at], NT, preferred_element_type=F32)
-    up = up_ref[0]
-    act, slope = gelu_terms(gate_ref[0])
-    hid_ref[0] = (act * up).astype(BF)
-    dgate = (dhid * up * slope).astype(BF)
-    dup = (dhid * act).astype(BF)
+    dgate = (dhid * turn_ref[0]).astype(BF)
+    dup = (dhid * act_ref[0]).astype(BF)
     dgate_ref[0] = dgate
     dup_ref[0] = dup
     more = jnp.dot(dgate, whole[0, at], preferred_element_type=F32) + jnp.dot(
@@ -1125,10 +1129,12 @@
             jax.ShapeDtypeStruct((slots, D), BF),
             jax.ShapeDtypeStruct((steps, slots, SLICE), F32),
             jax.ShapeDtypeStruct((steps, slots, SLICE), F32),
+            jax.ShapeDtypeStruct((steps, slots, SLICE), BF),
         ),
         in_specs=[fixed((slots, D))] + [ANY_SPEC] * (count + 1),
         out_specs=(
             fixed((slots, D)),
+            stepped((1, slots, SLICE)),
             stepped((1, slots, SLICE)),
             stepped((1, slots, SLICE)),
         ),
@@ -1143,7 +1149,7 @@
     )(rows, *chunks)
 
 
-def ffn_backward(grad, gate, up, chunks, ff_shard):
+def ffn_backward(grad, act, turn, chunks, ff_shard):
     slots, count = grad.shape[0], len(chunks) - 1
     hidden = count * ff_shard
     steps = hidden // SLICE
@@ -1151,11 +1157,11 @@
     return pl.pallas_call(
         functools.partial(ffn_backward_kernel, count, ff_shard),
         grid=(steps,),
-        out_shape=(jax.ShapeDtypeStruct((slots, D), BF), tile, tile, tile),
+        out_shape=(jax.ShapeDtypeStruct((slots, D), BF), tile, tile),
         in_specs=[fixed((slots, D))]
         + [stepped((1, slots, SLICE))] * 2
         + [ANY_SPEC] * (count + 1),
-        out_specs=(fixed((slots, D)),) + (stepped((1, slots, SLICE)),) * 3,
+        out_specs=(fixed((slots, D)),) + (stepped((1, slots, SLICE)),) * 2,
         scratch_shapes=[
             pltpu.VMEM((3, hidden, D), BF),
             pltpu.VMEM((slots, D), F32),
@@ -1164,7 +1170,7 @@
         compiler_params=ffn_params(),
         cost_estimate=ffn_cost(slots, hidden),
         name="ffn_backward",
-    )(grad, gate, up, *chunks)
+    )(grad, act, turn, *chunks)
 
 
 def ffn_weights(rows, grad, hid, dgate, dup, count, ff_shard):
@@ -1229,7 +1235,7 @@
         head = x[:prompt_rows].reshape(G_LINE, sh.part, -1).transpose(1, 0, 2)
         return jnp.concatenate([head.reshape(prompt_rows, -1), x[prompt_rows:]], 0)
 
-    weights = RingGather(jnp.concatenate([w_gate[0].T, w_up[0].T, w_down[0]], 0), fsdp_count)
+    own_weights = jnp.concatenate([w_gate[0].T, w_up[0].T, w_down[0]], 0)
     spread = [fsdp_count // 8] * 4
     spread[0] += fsdp_count // 2 - sum(spread)
 
@@ -1245,13 +1251,13 @@
     small = jnp.pad(small, (0, small_rows * D - small.shape[0])).reshape(small_rows, D)
     pack = jnp.concatenate([w_qkv[:, i * D : (i + 1) * D] for i in range(3)] + [w_out, small], 0)
     gathered = dense_gather(pack, group_count)
+    own_weights, tail = tied(own_weights, gathered[:, 4 * shard])
+    weights = RingGather(own_weights, fsdp_count)
     run(weights, spread[0])
     qkv_full = jnp.concatenate(
         [gathered[:, i * shard : (i + 1) * shard].reshape(D, D) for i in range(3)], 1
     )
-    qkv_full = weights.tie(qkv_full)
     out_full = gathered[:, 3 * shard : 4 * shard].reshape(D, D)
-    tail = gathered[:, 4 * shard]
     marks = [0, shard, 2 * shard, 2 * shard + shard * expert_count]
     marks += [marks[-1] + bias_table.shape[0]]
     attn_scale = tail[:, marks[0] : marks[1]].reshape(D).astype(F32)
@@ -1279,12 +1285,13 @@
         .reshape(fsdp_count, tok_count, 3 * sh.width)
     )
     head_qkv = lax.all_to_all(by_heads, "fsdp", split_axis=0, concat_axis=0, tiled=True)
+    head_qkv = weights.tie(head_qkv)
     run(weights, spread[1])
-    head_qkv = weights.tie(head_qkv)
     head_att, att_turned, att_lse = attend_forward(sh, my_groups, my_table, bucket, head_qkv)
     att_back = lax.all_to_all(head_att, "fsdp", split_axis=0, concat_axis=0, tiled=True)
+    att_back = weights.tie(att_back)
     run(weights, spread[2])
-    att_back = weights.tie(att_back)
+    run(weights, spread[3])
     attn_low = att_back.transpose(1, 0, 2).reshape(tok_count, D)
 
     middle = input_float + jnp.dot(attn_low, out_full, preferred_element_type=F32)
@@ -1310,8 +1317,6 @@
         return rows.reshape(slot_total, D)
 
     expert_rows = swap_experts(outgoing)
-    run(weights, spread[3])
-    expert_rows = weights.tie(expert_rows)
     slot_gate = jnp.sum(
         jnp.where(hot[0], gate_kept[:, 0:1], 0.0) + jnp.where(hot[1], gate_kept[:, 1:2], 0.0),
         axis=0,
@@ -1321,10 +1326,10 @@
 
     far = fsdp_count // 2
     blocks = weights.chunks[:far] + list(weights.chunks[far]) + weights.chunks[far + 1 :]
-    result_rows, gate_pre, up_pre = ffn_forward(expert_rows, blocks, ff_shard)
+    result_rows, act, turn, hidden = ffn_forward(expert_rows, blocks, ff_shard)
     returned = swap_experts(result_rows)
-    grad_rows, hidden, grad_gate_pre, grad_up_pre = ffn_backward(
-        grad_result, gate_pre, up_pre, blocks, ff_shard
+    grad_rows, grad_gate_pre, grad_up_pre = ffn_backward(
+        grad_result, act, turn, blocks, ff_shard
     )
     grad_sent = swap_experts(grad_rows)
     totals = ffn_weights(
@@ -1368,8 +1373,8 @@
     run(sums, spread[2])
     head_dqkv = sums.tie(head_dqkv)
     back_dqkv = lax.all_to_all(head_dqkv, "fsdp", split_axis=0, concat_axis=0, tiled=True)
-    run(sums, spread[3])
-    back_dqkv = sums.tie(back_dqkv)
+    back_dqkv = sums.step(back_dqkv)
+    run(sums, spread[3] - 1)
     expert_sums = sums.finish()
     grad_gate = expert_sums[:ff_shard].T
     grad_up = expert_sums[ff_shard : 2 * ff_shard].T

time: 829 us -> 805 us (0.971)
  blocking collectives: 50.7 us -> 96.2 us
  waiting for transfers between devices: 217 us -> 177 us
  Pallas kernels: 341 us -> 305 us
  local copies, waits for them, and re-layouts: 70.3 us -> 79.6 us
    all_to_all x0 -> x1, blocking collectives: none -> 44.2 us  [local(): lax.all_to_all(head_att, 'fsdp', split_axis=0, concat_axis=0, tiled=True)]
    pallas_call x1, Pallas kernels: 91.3 us -> 51.4 us  [dense_gather(): pl.pallas_call(functools.partial(dense_gather_kernel, cut), out_shape=jax...]
    all_to_all x1 -> x0, waiting for transfers between devices: 33.2 us -> none  [local(): lax.all_to_all(head_att, 'fsdp', split_axis=0, concat_axis=0, tiled=True)]
    all_to_all x1, waiting for transfers between devices: 0.01 us -> 28.8 us  [local(): lax.all_to_all(head_dqkv, 'fsdp', split_axis=0, concat_axis=0, tiled=True)]
    all_to_all x4, waiting for transfers between devices: 24.2 us -> 2.89 us  [swap_experts(): lax.all_to_all(rows, 'expert', split_axis=0, concat_axis=0, tiled=True)]
    ppermute x16, waiting for transfers between devices: 160 us -> 146 us  [ring_hop(): lax.ppermute(x, 'fsdp', [(ring[i], ring[(i + step) % count]) for i in ran...]
    unnamed x141 -> x147, local copies, waits for them, and re-layouts: 11.6 us -> 16.7 us
  transfers between devices with their start and end apart: 23 -> 22, of which waited for: 10 -> 9; matrix products, arithmetic and copies ran while one was open for 9% -> 11% of each run, Pallas kernels for 32% -> 32%
where the time goes in v4:
time: 805 us; the launch traced here: 796 us
  Pallas kernels  305 us (38%)
  waiting for transfers between devices  177 us (22%)
  blocking collectives  96.2 us (12%)
  local copies, waits for them, and re-layouts  79.6 us (10%)
  starting transfers between devices  57.2 us (7%)
  matrix products  41.4 us (5%)
  other arithmetic  35.4 us (4%)
    ppermute x16, waiting for transfers between devices, ring_hop(): lax.ppermute(x, 'fsdp', [(ring[i], ring[(i + step) % count]) for i in ran...  146 us
    pallas_call x1, Pallas kernels, dense_sum(): pl.pallas_call(functools.partial(dense_sum_kernel, cut), out_shape=jax.Sh...  87.8 us
    all_to_all x1, blocking collectives, local(): lax.all_to_all(head_grad, 'fsdp', split_axis=0, concat_axis=0, tiled=True)  52 us
    pallas_call x1, Pallas kernels, dense_gather(): pl.pallas_call(functools.partial(dense_gather_kernel, cut), out_shape=jax...  51.4 us
    all_to_all x1, blocking collectives, local(): lax.all_to_all(head_att, 'fsdp', split_axis=0, concat_axis=0, tiled=True)  44.2 us
    pallas_call x1, Pallas kernels, attend_backward(): pl.pallas_call(functools.partial(attn_backward_kernel, sh), out_shape=(ja...  43.2 us
    pallas_call x1, Pallas kernels, ffn_backward(): pl.pallas_call(functools.partial(ffn_backward_kernel, count, ff_shard), g...  40 us
    pallas_call x1, Pallas kernels, ffn_forward(): pl.pallas_call(functools.partial(ffn_forward_kernel, count, ff_shard), gr...  34.8 us
  transfers between devices with their start and end apart: 22, of which 9 were waited for; matrix products, arithmetic and copies ran while one was open for 11% of the time, Pallas kernels for 32%

profile of v4, /device:TPU:0, one launch (start us, length us, event | category | flops | bytes accessed | tf_op | source)
XLA Modules:
  0.0 796.4 jit_solution(9189640962903514907)
XLA Ops:
  8.6 51.4 %dense_gather.1 = bf16[32,144,1024]{2,1,0:T(8,128)(2,1)} custom-call(bf16[144,1024]{1,0:T(8,128)(2,1)} %copy-done.33), custom_call_target="tpu_custom_call" | custom-call | bytes 100000000 | tf_op jit(solution)/shard_map/dense_gather/pallas_call | solution.py:769
  61.2 6.2 fusion.63
  69.1 2.8 pad_maximum_fusion.3.refs_0_
  72.1 4.9 fusion.7
  77.6 2.9 copy.55
  80.5 4.3 copy.56
  84.8 4.9 all-to-all-start
  92.2 84.9 %collective-permute-done.1.refs_1_ = bf16[1056,1024]{1,0:T(8,128)(2,1)} collective-permute-done((bf16[1056,1024]{1,0:T(8,128)(2,1)}, bf16[1056,1024]{1,0:T(8,128)(2,1)}, u32[]{:S(2)}, u32[]{:S(2)}) %collective-permute-start.1) | collective-permute-done | bytes 2162720 | tf_op jit(solution)/shard_map/ppermute | solution.py:526
  177.2 14.2 %collective-permute-start.2 = (bf16[1056,1024]{1,0:T(8,128)(2,1)}, bf16[1056,1024]{1,0:T(8,128)(2,1)}, u32[]{:S(2)}, u32[]{:S(2)}) collective-permute-start(bf16[1056,1024]{1,0:T(8,128)(2,1)} %collective-permute-done.refs_8_), channel_id=1, source_target_pairs={{0,2},{2,4},{4,6},{6,7},{7,5},{5,3},{3,1},{1,0},{8,10},{10,12},{12... | collective-permute-start | bytes 6488072 | tf_op jit(solution)/shard_map/ppermute | solution.py:526
  191.4 22.3 %attend_forward.1 = (bf16[8,384,128]{2,1,0:T(8,128)(2,1)S(1)}, f32[12,128,256]{2,1,0:T(8,128)S(1)}, f32[12,8,256]{2,1,0:T(8,128)S(1)}) custom-call(s32[8]{0:T(128)S(1)} %bitcast_convert_fusion.1.group_ref, f32[2,32]{1,0:T(2,128)S(1)} %bitcast_convert_fusion.table_ref, s32[9,128]{1,0:T(8,128)S(1)} %bitcast.102, bf16[8,384,384]{2,1,0:T(8,128)(2,1)S(1)} %all-to-all-done.x_ref), custom_call_target="tpu_custom_call" | custom-call | flops 10000000000 | bytes 8000000 | tf_op jit(solution)/shard_map/attend_forward/pallas_call | solution.py:465
  213.7 44.2 %all_to_all.40 = bf16[8,384,128]{2,1,0:T(8,128)(2,1)S(1)} all-to-all(bf16[8,384,128]{2,1,0:T(8,128)(2,1)S(1)} %get-tuple-element.56), channel_id=1, replica_groups=mesh['expert'=4,'fsdp'=8] {'fsdp'}, dimensions={0} | all-to-all | bytes 1572864 | tf_op jit(solution)/shard_map/all_to_all | solution.py:1291
  264.2 3.0 multiply_reduce_fusion.2
  267.3 2.6 convolution_convert_fusion.3
  269.9 4.4 all-to-all-start.2
  276.0 29.8 %collective-permute-done.4.refs_3_ = bf16[1056,1024]{1,0:T(8,128)(2,1)} collective-permute-done((bf16[1056,1024]{1,0:T(8,128)(2,1)}, bf16[1056,1024]{1,0:T(8,128)(2,1)}, u32[]{:S(2)}, u32[]{:S(2)}) %collective-permute-start.4) | collective-permute-done | bytes 2162720 | tf_op jit(solution)/shard_map/ppermute | solution.py:526
  305.8 2.3 slice.249
  308.9 2.3 slice.248
  313.6 2.5 multiply_convert_fusion
  316.1 4.4 all-to-all-start.4
  320.6 11.4 %collective-permute-done.7.refs_5_ = bf16[528,1024]{1,0:T(8,128)(2,1)} collective-permute-done((bf16[528,1024]{1,0:T(8,128)(2,1)}, bf16[528,1024]{1,0:T(8,128)(2,1)}, u32[]{:S(2)}, u32[]{:S(2)}) %collective-permute-start.7) | collective-permute-done | bytes 1081376 | tf_op jit(solution)/shard_map/ppermute | solution.py:526
  331.9 2.4 collective-permute-done.6.refs_4_
  334.4 34.8 %ffn_forward.1 = (bf16[960,1024]{1,0:T(8,128)(2,1)}, f32[11,960,256]{2,1,0:T(8,128)}, f32[11,960,256]{2,1,0:T(8,128)}, bf16[11,960,256]{2,1,0:T(8,128)(2,1)}) custom-call(bf16[960,1024]{1,0:T(8,128)(2,1)} %bitcast.23.rows_ref, bf16[1056,1024]{1,0:T(8,128)(2,1)} %pad_maximum_fusion.3.refs_0_, bf16[1056,1024]{1,0:T(8,128)(2,1)} %collective-permute-done.1.refs_1_, ...), custom_call_target="tpu_custom_call" | custom-call | flops 16609443840 | bytes 40000000 | tf_op jit(solution)/shard_map/ffn_forward/pallas_call | solution.py:1125
  369.1 4.7 all-to-all-start.3
  373.8 40.0 %ffn_backward.1 = (bf16[960,1024]{1,0:T(8,128)(2,1)}, bf16[11,960,256]{2,1,0:T(8,128)(2,1)}, bf16[11,960,256]{2,1,0:T(8,128)(2,1)}) custom-call(bf16[960,1024]{1,0:T(8,128)(2,1)} %bitcast.34.grad_ref, f32[11,960,256]{2,1,0:T(8,128)} %get-tuple-element.63.act_ref, f32[11,960,256]{2,1,0:T(8,128)} %get-tuple-element.64.turn_ref, ...), custom_call_target="tpu_custom_call" | custom-call | flops 16609443840 | bytes 40000000 | tf_op jit(solution)/shard_map/ffn_backward/pallas_call | solution.py:1157
  413.8 26.0 %ffn_weights.1 = (bf16[1056,1024]{1,0:T(8,128)(2,1)}, bf16[1056,1024]{1,0:T(8,128)(2,1)}, bf16[1056,1024]{1,0:T(8,128)(2,1)}, bf16[1056,1024]{1,0:T(8,128)(2,1)}...) custom-call(bf16[960,1024]{1,0:T(8,128)(2,1)} %bitcast.23.rows_ref, ...), custom_call_target="tpu_custom_call" | custom-call | flops 16609443840 | bytes 40000000 | tf_op jit(solution)/shard_map/ffn_weights/pallas_call | solution.py:1184
  439.8 2.4 slice.215
  444.4 4.4 all-to-all-start.5
  448.9 2.6 fusion.15
  451.6 3.7 fusion.10
  455.4 13.5 %collective-permute-done.8 = bf16[528,1024]{1,0:T(8,128)(2,1)} collective-permute-done((bf16[528,1024]{1,0:T(8,128)(2,1)}, bf16[528,1024]{1,0:T(8,128)(2,1)}, u32[]{:S(2)}, u32[]{:S(2)}) %collective-permute-start.8) | collective-permute-done | bytes 1081376 | tf_op jit(solution)/shard_map/ppermute | solution.py:526
  470.3 2.9 all-to-all-done.5
  483.4 3.5 multiply_reduce_fusion
  495.1 52.0 %all_to_all.41.do_ref = bf16[8,384,128]{2,1,0:T(8,128)(2,1)S(1)} all-to-all(bf16[8,384,128]{2,1,0:T(8,128)(2,1)} %bitcast.126), channel_id=1, replica_groups=mesh['expert'=4,'fsdp'=8] {'fsdp'}, dimensions={0} | all-to-all | bytes 1572864 | tf_op jit(solution)/shard_map/all_to_all | solution.py:1367
  547.1 3.4 add_convert_fusion.3
  550.6 2.7 add_convert_fusion.2
  553.4 2.5 collective-permute-start.13
  555.9 43.2 %attend_backward.1 = (bf16[8,384,384]{2,1,0:T(8,128)(2,1)}, f32[64,128]{1,0:T(8,128)S(1)}) custom-call(s32[8]{0:T(128)S(1)} %bitcast_convert_fusion.1.group_ref, f32[2,32]{1,0:T(2,128)S(1)} %bitcast_convert_fusion.table_ref, s32[9,128]{1,0:T(8,128)S(1)} %bitcast.103, bf16[8,384,384]{2,1,0:T(8,128)(2,1)} %copy-done, ...), custom_call_target="tpu_custom_call" | custom-call | flops 20000000000 | bytes 12000000 | tf_op jit(solution)/shard_map/attend_backward/pallas_call | solution.py:490
  601.4 4.7 all-to-all-start.7
  613.9 2.4 copy.60
  618.5 2.6 convolution_convert_fusion.2
  621.4 7.8 add_convert_fusion
  629.2 28.8 %all-to-all-done.7 = bf16[8,384,384]{2,1,0:T(8,128)(2,1)} async-done(((bf16[8,384,384]{2,1,0:T(8,128)(2,1)}), bf16[8,384,384]{2,1,0:T(8,128)(2,1)}, u32[]{:S(2)}, u32[]{:S(2)}) %all-to-all-start.7) | async-done | bytes 2359328 | tf_op jit(solution)/shard_map/all_to_all | solution.py:1375
  658.0 4.3 copy.64
  665.4 5.3 fusion.9
  670.6 5.8 convolution_convert_fusion
  678.8 5.9 fusion.64
  698.1 87.8 %dense_sum.1 = f32[144,1024]{1,0:T(8,128)S(1)} custom-call(bf16[32,144,1024]{2,1,0:T(8,128)(2,1)S(1)} %constant_dynamic-update-slice_fusion.2.g_ref), custom_call_target="tpu_custom_call" | custom-call | bytes 100000000 | tf_op jit(solution)/shard_map/dense_sum/pallas_call | solution.py:934
  790.7 3.3 convert_add_fusion
  (283 shorter events, 83.4 us)
Async XLA Ops:
  67.7 196.5 %copy-start.8 = (bf16[128,2,1024]{2,0,1:T(8,128)(2,1)}, bf16[128,2,1024]{2,0,1:T(8,128)(2,1)S(1)}, u32[]{:S(2)}) copy-start(bf16[128,2,1024]{2,0,1:T(8,128)(2,1)S(1)} %copy.53) | copy-start | bytes 1572868
  84.8 106.5 %copy-start.1 = (s32[1152]{0:T(1024)S(1)}, s32[1152]{0:T(1024)}, u32[]{:S(2)}) copy-start(s32[1152]{0:T(1024)} %param.29) | copy-start | bytes 13828
  84.8 92.3 %all-to-all-start = ((bf16[8,384,384]{2,1,0:T(8,128)(2,1)}), bf16[8,384,384]{2,1,0:T(8,128)(2,1)S(1)}, u32[]{:S(2)}, u32[]{:S(2)}) async-start(bf16[8,384,384]{2,1,0:T(8,128)(2,1)} %copy.56), calls=%async_computation | async-start | bytes 4718592 | tf_op jit(solution)/shard_map/all_to_all | solution.py:1287
  89.7 87.4 %collective-permute-start.1 = (bf16[1056,1024]{1,0:T(8,128)(2,1)}, bf16[1056,1024]{1,0:T(8,128)(2,1)}, u32[]{:S(2)}, u32[]{:S(2)}) collective-permute-start(bf16[1056,1024]{1,0:T(8,128)(2,1)} %pad_maximum_fusion.3.refs_0_), channel_id=1, source_target_pairs={{0,1},{2,0},{4,2},{6,4},{7,6},{5,7},{3,5},{1,3},{8,9},{10,8},{12,1... | collective-permute-start | bytes 6488072 | tf_op jit(solution)/shard_map/ppermute | solution.py:526
  91.7 85.4 %collective-permute-start = (bf16[1056,1024]{1,0:T(8,128)(2,1)}, bf16[1056,1024]{1,0:T(8,128)(2,1)}, u32[]{:S(2)}, u32[]{:S(2)}) collective-permute-start(bf16[1056,1024]{1,0:T(8,128)(2,1)} %pad_maximum_fusion.3.refs_0_), channel_id=1, source_target_pairs={{0,2},{2,4},{4,6},{6,7},{7,5},{5,3},{3,1},{1,0},{8,10},{10,12},{12... | collective-permute-start | bytes 6488072 | tf_op jit(solution)/shard_map/ppermute | solution.py:526
  177.1 36.5 %copy-start = (bf16[8,384,384]{2,1,0:T(8,128)(2,1)}, bf16[8,384,384]{2,1,0:T(8,128)(2,1)S(1)}, u32[]{:S(2)}) copy-start(bf16[8,384,384]{2,1,0:T(8,128)(2,1)S(1)} %all-to-all-done.x_ref) | copy-start | bytes 7077892
  177.2 80.7 %collective-permute-start.2 = (bf16[1056,1024]{1,0:T(8,128)(2,1)}, bf16[1056,1024]{1,0:T(8,128)(2,1)}, u32[]{:S(2)}, u32[]{:S(2)}) collective-permute-start(bf16[1056,1024]{1,0:T(8,128)(2,1)} %collective-permute-done.refs_8_), channel_id=1, source_target_pairs={{0,2},{2,4},{4,6},{6,7},{7,5},{5,3},{3,1},{1,0},{8,10},{10,12},{12... | collective-permute-start | bytes 6488072 | tf_op jit(solution)/shard_map/ppermute | solution.py:526
  191.3 66.5 %collective-permute-start.3 = (bf16[1056,1024]{1,0:T(8,128)(2,1)}, bf16[1056,1024]{1,0:T(8,128)(2,1)}, u32[]{:S(2)}, u32[]{:S(2)}) collective-permute-start(bf16[1056,1024]{1,0:T(8,128)(2,1)} %collective-permute-done.1.refs_1_), channel_id=1, source_target_pairs={{0,1},{2,0},{4,2},{6,4},{7,6},{5,7},{3,5},{1,3},{8,9},{10,8},{12,1... | collective-permute-start | bytes 6488072 | tf_op jit(solution)/shard_map/ppermute | solution.py:526
  191.4 68.8 %copy-start.59 = (s32[384,2]{0,1:T(2,128)S(1)}, s32[384,2]{0,1:T(2,128)}, u32[]{:S(2)}) copy-start(s32[384,2]{0,1:T(2,128)} %param.26) | copy-start | bytes 9220
  191.4 68.8 %copy-start.60 = (s32[384,2]{0,1:T(2,128)S(1)}, s32[384,2]{0,1:T(2,128)}, u32[]{:S(2)}) copy-start(s32[384,2]{0,1:T(2,128)} %param.27) | copy-start | bytes 9220
  191.4 68.8 %copy-start.19 = (bf16[384,1024]{1,0:T(8,128)(2,1)S(1)}, bf16[384,1024]{1,0:T(8,128)(2,1)}, u32[]{:S(2)}) copy-start(bf16[384,1024]{1,0:T(8,128)(2,1)} %param.30) | copy-start | bytes 2359300
  213.6 44.2 %copy-start.2 = (f32[12,128,256]{2,1,0:T(8,128)}, f32[12,128,256]{2,1,0:T(8,128)S(1)}, u32[]{:S(2)}) copy-start(f32[12,128,256]{2,1,0:T(8,128)S(1)} %get-tuple-element.77.ot_ref) | copy-start | bytes 4718596
  213.7 47.3 %slice-start.4 = ((s32[384,2]{0,1:T(2,128)}), s32[256,2]{0,1:T(2,128)S(1)}, s32[]{:S(2)}) async-start(s32[384,2]{0,1:T(2,128)} %param.27), calls=%async_computation.12 | async-start | bytes 4096 | tf_op jit(solution)/shard_map/slice | solution.py:1231
  213.7 47.5 %slice-start.3 = ((s32[384,2]{0,1:T(2,128)}), s32[256,2]{0,1:T(2,128)S(1)}, s32[]{:S(2)}) async-start(s32[384,2]{0,1:T(2,128)} %param.26), calls=%async_computation.11 | async-start | bytes 4096 | tf_op jit(solution)/shard_map/slice | solution.py:1231
  213.7 47.7 %slice-start.2 = ((bf16[384,1024]{1,0:T(8,128)(2,1)}), bf16[256,1024]{1,0:T(8,128)(2,1)S(1)}, s32[]{:S(2)}) async-start(bf16[384,1024]{1,0:T(8,128)(2,1)} %param.30), calls=%async_computation.10 | async-start | bytes 1048576 | tf_op jit(solution)/shard_map/slice | solution.py:1231
  257.9 47.9 %collective-permute-start.4 = (bf16[1056,1024]{1,0:T(8,128)(2,1)}, bf16[1056,1024]{1,0:T(8,128)(2,1)}, u32[]{:S(2)}, u32[]{:S(2)}) collective-permute-start(bf16[1056,1024]{1,0:T(8,128)(2,1)} %collective-permute-done.3.refs_2_), channel_id=1, source_target_pairs={{0,1},{2,0},{4,2},{6,4},{7,6},{5,7},{3,5},{1,3},{8,9},{10,8},{12,1... | collective-permute-start | bytes 6488072 | tf_op jit(solution)/shard_map/ppermute | solution.py:526
  259.0 49.8 %collective-permute-start.5 = (bf16[1056,1024]{1,0:T(8,128)(2,1)}, bf16[1056,1024]{1,0:T(8,128)(2,1)}, u32[]{:S(2)}, u32[]{:S(2)}) collective-permute-start(bf16[1056,1024]{1,0:T(8,128)(2,1)} %collective-permute-done.2.refs_7_), channel_id=1, source_target_pairs={{0,2},{2,4},{4,6},{6,7},{7,5},{5,3},{3,1},{1,0},{8,10},{10,12},{12... | collective-permute-start | bytes 6488072 | tf_op jit(solution)/shard_map/ppermute | solution.py:526
  262.6 224.4 %copy-start.37 = (f32[1024]{0:T(1024)}, f32[1024]{0:T(1024)S(1)}, u32[]{:S(2)}) copy-start(f32[1024]{0:T(1024)S(1)} %reshape.324) | copy-start | bytes 12292
  267.2 219.8 %copy-start.43 = (f32[384]{0:T(512)}, f32[384]{0:T(512)S(1)}, u32[]{:S(2)}) copy-start(f32[384]{0:T(512)S(1)} %fusion.53) | copy-start | bytes 4612
  269.9 46.2 %all-to-all-start.2 = ((bf16[4,240,1024]{2,1,0:T(8,128)(2,1)}), bf16[4,240,1024]{2,1,0:T(8,128)(2,1)}, u32[]{:S(2)}, u32[]{:S(2)}) async-start(bf16[4,240,1024]{2,1,0:T(8,128)(2,1)} %bitcast.140), calls=%async_computation.2 | async-start | bytes 3932160 | tf_op jit(solution)/shard_map/all_to_all | solution.py:1316
  275.3 207.2 %copy-start.34 = (f32[384,4]{0,1:T(4,128)}, f32[384,4]{0,1:T(4,128)S(1)}, u32[]{:S(2)}) copy-start(f32[384,4]{0,1:T(4,128)S(1)} %get-tuple-element.180) | copy-start | bytes 18436
  275.3 207.2 %copy-start.41 = (f32[384]{0:T(512)}, f32[384]{0:T(512)S(1)}, u32[]{:S(2)}) copy-start(f32[384]{0:T(512)S(1)} %is-finite_select_fusion) | copy-start | bytes 4612
  276.0 36.4 %copy-start.51 = (s32[384]{0:T(512)S(1)}, s32[384]{0:T(512)}, u32[]{:S(2)}) copy-start(s32[384]{0:T(512)} %get-tuple-element.144) | copy-start | bytes 4612
  276.0 36.4 %copy-start.52 = (s32[384]{0:T(512)S(1)}, s32[384]{0:T(512)}, u32[]{:S(2)}) copy-start(s32[384]{0:T(512)} %get-tuple-element.145) | copy-start | bytes 4612
  276.0 36.6 %copy-start.54 = (s32[128,2]{0,1:T(2,128)S(1)}, s32[128,2]{0,1:T(2,128)}, u32[]{:S(2)}) copy-start(s32[128,2]{0,1:T(2,128)} %copy-done.53) | copy-start | bytes 3076
  276.0 36.7 %copy-start.62 = (s32[384]{0:T(512)S(1)}, s32[384]{0:T(512)}, u32[]{:S(2)}) copy-start(s32[384]{0:T(512)} %copy-done.61) | copy-start | bytes 4612
  276.0 36.7 %copy-start.64 = (s32[384]{0:T(512)S(1)}, s32[384]{0:T(512)}, u32[]{:S(2)}) copy-start(s32[384]{0:T(512)} %copy-done.63) | copy-start | bytes 4612
  276.0 37.6 %copy-start.20 = (bf16[128,2,1024]{2,0,1:T(8,128)(2,1)S(1)}, bf16[128,2,1024]{2,0,1:T(8,128)(2,1)}, u32[]{:S(2)}) copy-start(bf16[128,2,1024]{2,0,1:T(8,128)(2,1)} %copy.61) | copy-start | bytes 1572868
  276.0 37.6 %copy-start.28 = (bf16[128,1024]{1,0:T(8,128)(2,1)S(1)}, bf16[128,1024]{1,0:T(8,128)(2,1)}, u32[]{:S(2)}) copy-start(bf16[128,1024]{1,0:T(8,128)(2,1)} %slice.214) | copy-start | bytes 786436
  308.1 23.8 %collective-permute-start.7 = (bf16[528,1024]{1,0:T(8,128)(2,1)}, bf16[528,1024]{1,0:T(8,128)(2,1)}, u32[]{:S(2)}, u32[]{:S(2)}) collective-permute-start(bf16[528,1024]{1,0:T(8,128)(2,1)} %slice.249), channel_id=1, source_target_pairs={{0,1},{2,0},{4,2},{6,4},{7,6},{5,7},{3,5},{1,3},{8,9},{10,8},{12,1... | collective-permute-start | bytes 3244040 | tf_op jit(solution)/shard_map/ppermute | solution.py:526
  311.1 23.2 %collective-permute-start.6 = (bf16[528,1024]{1,0:T(8,128)(2,1)}, bf16[528,1024]{1,0:T(8,128)(2,1)}, u32[]{:S(2)}, u32[]{:S(2)}) collective-permute-start(bf16[528,1024]{1,0:T(8,128)(2,1)} %slice.248), channel_id=1, source_target_pairs={{0,2},{2,4},{4,6},{6,7},{7,5},{5,3},{3,1},{1,0},{8,10},{10,12},{12... | collective-permute-start | bytes 3244040 | tf_op jit(solution)/shard_map/ppermute | solution.py:526
  316.1 53.0 %all-to-all-start.4 = ((bf16[4,240,1024]{2,1,0:T(8,128)(2,1)}), bf16[4,240,1024]{2,1,0:T(8,128)(2,1)}, u32[]{:S(2)}, u32[]{:S(2)}) async-start(bf16[4,240,1024]{2,1,0:T(8,128)(2,1)} %bitcast.142), calls=%async_computation.4 | async-start | bytes 3932160 | tf_op jit(solution)/shard_map/all_to_all | solution.py:1316
  369.1 75.3 %all-to-all-start.3 = ((bf16[4,240,1024]{2,1,0:T(8,128)(2,1)}), bf16[4,240,1024]{2,1,0:T(8,128)(2,1)}, u32[]{:S(2)}, u32[]{:S(2)}) async-start(bf16[4,240,1024]{2,1,0:T(8,128)(2,1)} %bitcast.141), calls=%async_computation.3 | async-start | bytes 3932160 | tf_op jit(solution)/shard_map/all_to_all | solution.py:1316
  442.4 26.6 %collective-permute-start.8 = (bf16[528,1024]{1,0:T(8,128)(2,1)}, bf16[528,1024]{1,0:T(8,128)(2,1)}, u32[]{:S(2)}, u32[]{:S(2)}) collective-permute-start(bf16[528,1024]{1,0:T(8,128)(2,1)} %get-tuple-element.69), channel_id=1, source_target_pairs={{0,2},{2,4},{4,6},{6,7},{7,5},{5,3},{3,1},{1,0},{8,10},{10,12},{12... | collective-permute-start | bytes 3244040 | tf_op jit(solution)/shard_map/ppermute | solution.py:526
  444.0 26.3 %collective-permute-start.9 = (bf16[528,1024]{1,0:T(8,128)(2,1)}, bf16[528,1024]{1,0:T(8,128)(2,1)}, u32[]{:S(2)}, u32[]{:S(2)}) collective-permute-start(bf16[528,1024]{1,0:T(8,128)(2,1)} %get-tuple-element.70), channel_id=1, source_target_pairs={{0,1},{2,0},{4,2},{6,4},{7,6},{5,7},{3,5},{1,3},{8,9},{10,8},{12,1... | collective-permute-start | bytes 3244040 | tf_op jit(solution)/shard_map/ppermute | solution.py:526
  444.4 28.8 %all-to-all-start.5 = ((bf16[4,240,1024]{2,1,0:T(8,128)(2,1)}), bf16[4,240,1024]{2,1,0:T(8,128)(2,1)}, u32[]{:S(2)}, u32[]{:S(2)}) async-start(bf16[4,240,1024]{2,1,0:T(8,128)(2,1)} %bitcast.139), calls=%async_computation.5 | async-start | bytes 3932160 | tf_op jit(solution)/shard_map/all_to_all | solution.py:1316
  455.4 27.1 %copy-start.39 = (f32[384,4]{0,1:T(4,128)}, f32[384,4]{0,1:T(4,128)S(1)}, u32[]{:S(2)}) copy-start(f32[384,4]{0,1:T(4,128)S(1)} %get-tuple-element.149) | copy-start | bytes 18436
  455.4 27.1 %copy-start.45 = (f32[384]{0:T(512)}, f32[384]{0:T(512)S(1)}, u32[]{:S(2)}) copy-start(f32[384]{0:T(512)S(1)} %negate_add_fusion) | copy-start | bytes 4612
  478.6 68.5 %collective-permute-start.10 = (bf16[1056,1024]{1,0:T(8,128)(2,1)}, bf16[1056,1024]{1,0:T(8,128)(2,1)}, u32[]{:S(2)}, u32[]{:S(2)}) collective-permute-start(bf16[1056,1024]{1,0:T(8,128)(2,1)} %pad_maximum_fusion.4), channel_id=1, source_target_pairs={{0,2},{2,4},{4,6},{6,7},{7,5},{5,3},{3,1},{1,0},{8,10},{10,12},{12... | collective-permute-start | bytes 6488072 | tf_op jit(solution)/shard_map/ppermute | solution.py:526
  481.9 65.2 %collective-permute-start.11 = (bf16[1056,1024]{1,0:T(8,128)(2,1)}, bf16[1056,1024]{1,0:T(8,128)(2,1)}, u32[]{:S(2)}, u32[]{:S(2)}) collective-permute-start(bf16[1056,1024]{1,0:T(8,128)(2,1)} %pad_maximum_fusion.5), channel_id=1, source_target_pairs={{0,1},{2,0},{4,2},{6,4},{7,6},{5,7},{3,5},{1,3},{8,9},{10,8},{12,1... | collective-permute-start | bytes 6488072 | tf_op jit(solution)/shard_map/ppermute | solution.py:526
  550.5 48.6 %collective-permute-start.12 = (bf16[1056,1024]{1,0:T(8,128)(2,1)S(1)}, bf16[1056,1024]{1,0:T(8,128)(2,1)}, u32[]{:S(2)}, u32[]{:S(2)}) collective-permute-start(bf16[1056,1024]{1,0:T(8,128)(2,1)S(1)} %add_convert_fusion.3), channel_id=1, source_target_pairs={{0,2},{2,4},{4,6},{6,7},{7,5},{5,3},{3,1},{1,0},{8,10},{10,12},{12... | collective-permute-start | bytes 6488072 | tf_op jit(solution)/shard_map/ppermute | solution.py:526
  553.4 48.0 %collective-permute-start.13 = (bf16[1056,1024]{1,0:T(8,128)(2,1)S(1)}, bf16[1056,1024]{1,0:T(8,128)(2,1)}, u32[]{:S(2)}, u32[]{:S(2)}) collective-permute-start(bf16[1056,1024]{1,0:T(8,128)(2,1)S(1)} %add_convert_fusion.2), channel_id=1, source_target_pairs={{0,1},{2,0},{4,2},{6,4},{7,6},{5,7},{3,5},{1,3},{8,9},{10,8},{12,1... | collective-permute-start | bytes 6488072 | tf_op jit(solution)/shard_map/ppermute | solution.py:526
  601.4 10.8 %copy-start.44 = (f32[384]{0:T(512)S(1)}, f32[384]{0:T(512)}, u32[]{:S(2)}) copy-start(f32[384]{0:T(512)} %copy-done.43) | copy-start | bytes 4612
  601.4 10.8 %copy-start.46 = (f32[384]{0:T(512)S(1)}, f32[384]{0:T(512)}, u32[]{:S(2)}) copy-start(f32[384]{0:T(512)} %copy-done.45) | copy-start | bytes 4612
  601.4 56.6 %all-to-all-start.7 = ((bf16[8,384,384]{2,1,0:T(8,128)(2,1)}), bf16[8,384,384]{2,1,0:T(8,128)(2,1)}, u32[]{:S(2)}, u32[]{:S(2)}) async-start(bf16[8,384,384]{2,1,0:T(8,128)(2,1)} %get-tuple-element.84), calls=%async_computation.7 | async-start | bytes 4718592 | tf_op jit(solution)/shard_map/all_to_all | solution.py:1375
  676.6 114.1 %collective-permute-start.14 = (bf16[1056,1024]{1,0:T(8,128)(2,1)}, bf16[1056,1024]{1,0:T(8,128)(2,1)}, u32[]{:S(2)}, u32[]{:S(2)}) collective-permute-start(bf16[1056,1024]{1,0:T(8,128)(2,1)} %get-tuple-element.92), channel_id=1, source_target_pairs={{0,2},{2,4},{4,6},{6,7},{7,5},{5,3},{3,1},{1,0},{8,10},{10,12},{12... | collective-permute-start | bytes 6488072 | tf_op jit(solution)/shard_map/ppermute | solution.py:526
  676.6 114.1 %collective-permute-start.15 = (bf16[1056,1024]{1,0:T(8,128)(2,1)}, bf16[1056,1024]{1,0:T(8,128)(2,1)}, u32[]{:S(2)}, u32[]{:S(2)}) collective-permute-start(bf16[1056,1024]{1,0:T(8,128)(2,1)} %get-tuple-element.93), channel_id=1, source_target_pairs={{0,1},{2,0},{4,2},{6,4},{7,6},{5,7},{3,5},{1,3},{8,9},{10,8},{12,1... | collective-permute-start | bytes 6488072 | tf_op jit(solution)/shard_map/ppermute | solution.py:526
  698.1 88.7 %slice-start = ((f32[384,1024]{1,0:T(8,128)}), f32[128,1024]{1,0:T(8,128)S(1)}, s32[]{:S(2)}) async-start(f32[384,1024]{1,0:T(8,128)} %copy-done.13), calls=%async_computation.8 | async-start | bytes 1048576 | tf_op jit(solution)/shard_map/slice | solution.py:1236
  (46 other events, 188.3 us)

commit v5 on v4

--- a/solution.py
+++ b/solution.py
@@ -828,8 +828,7 @@
 
     by_y, by_x, core = me.place(y=me.oy), me.place(x=me.ox), me.place(c=me.oc)
     me.greet()
-    offsets = (2, 3, 1, 0)
-    zs = [me.wrap(k) for k in offsets]
+    zs = (0, 3, 2, 1)
     loads = []
     for k in range(DEEP):
         for x in range(2):
@@ -873,41 +872,41 @@
         arrive(xbuf.at[k, 0, low], base + 5)
         add_into(block.at[low], xbuf.at[k, 0, low])
 
-    for step in range(DEEP + 2):
+    def along(k, sign, behind):
+        zo = zs[k]
+        here = behind if sign > 0 else DEEP - 1 - behind
+        term = acc.at[me.x * DEEP + k, me.y]
+        base = 32 + k * 4 + (sign + 1)
+        side = k * 4 + (sign + 1)
+        is_here = me.z == here
+        for h, at in ((0, top), (1, low)):
+            if behind > 0:
+
+                @pl.when(is_here)
+                def _(h=h, at=at):
+                    arrive(zbuf.at[side + h, at], base + h)
+                    add_into(term.at[at], zbuf.at[side + h, at])
+
+            if here != zo:
+                send(
+                    term.at[at], zbuf.at[side + h, at], base + h, me.along(sign), is_here
+                )
+
+    for step in range(DEEP + 6):
         if step < DEEP:
             first(step)
         if 0 <= step - 1 < DEEP:
             second(step - 1)
         if 0 <= step - 2 < DEEP:
             third(step - 2)
-
-    for dist in (3, 2, 1):
-        for sign in (-1, 1):
-            side = (sign + 1) // 2
-            term = acc.at[me.x * DEEP + offsets.index(sign * dist % DEEP), me.y]
-            if dist < 3:
-
-                @pl.when(me.inside(me.z + sign * dist) & me.inside(me.z - sign))
-                def _(term=term, dist=dist, side=side):
-                    buf = zbuf.at[dist * 2 + side]
-                    arrive(buf, 34 + dist * 2 + side)
-                    add_into(term, buf)
-
-            send(
-                term,
-                zbuf.at[(dist - 1) * 2 + side],
-                32 + dist * 2 + side,
-                me.along(sign),
-                me.inside(me.z + sign * dist),
-            )
-    block = acc.at[me.x * DEEP + DEEP - 1, me.y]
-    for sign in (-1, 1):
-
-        @pl.when(me.inside(me.z - sign))
-        def _(sign=sign):
-            buf = zbuf.at[(sign + 1) // 2]
-            arrive(buf, 32 + 2 + (sign + 1) // 2)
-            add_into(block, buf)
+        for k in range(DEEP):
+            behind = step - 2 - k
+            if behind >= 0:
+                if behind <= zs[k]:
+                    along(k, 1, behind)
+                if behind <= DEEP - 1 - zs[k]:
+                    along(k, -1, behind)
+    block = acc.at[me.x * DEEP + lax.rem(DEEP - me.z, DEEP), me.y]
 
     def put(i, _):
         at = pl.ds(pl.multiple_of(i * 16, 16), 16)
@@ -941,8 +940,8 @@
             pltpu.VMEM(pair, BF),
             pltpu.VMEM((DEEP, 2, rows, width), BF),
             pltpu.VMEM((DEEP, 2, rows, width), BF),
-            pltpu.VMEM((6, rows, width), BF),
-            pltpu.SemaphoreType.DMA((48,)),
+            pltpu.VMEM((4 * DEEP, rows, width), BF),
+            pltpu.SemaphoreType.DMA((72,)),
             pltpu.SemaphoreType.DMA((48,)),
             pltpu.SemaphoreType.DMA((8,)),
         ],
@@ -1054,8 +1053,10 @@
     dup = (dhid * act_ref[0]).astype(BF)
     dgate_ref[0] = dgate
     dup_ref[0] = dup
-    more = jnp.dot(dgate, whole[0, at], preferred_element_type=F32) + jnp.dot(
-        dup, whole[1, at], preferred_element_type=F32
+    more = jnp.dot(
+        jnp.concatenate([dgate, dup], axis=1),
+        jnp.concatenate([whole[0, at], whole[1, at]], axis=0),
+        preferred_element_type=F32,
     )
 
     @pl.when(t == 0)
@@ -1343,7 +1344,6 @@
 
     sums = RingScatter(part, fsdp_count)
     run(sums, spread[0])
-    grad_sent = sums.tie(grad_sent)
 
     picked = [
         jnp.dot(h.astype(BF), returned, preferred_element_type=F32) for h in hot
@@ -1364,6 +1364,7 @@
     head_grad = (
         grad_attn.reshape(tok_count, fsdp_count, sh.width).transpose(1, 0, 2)
     )
+    head_grad = sums.tie(head_grad)
     head_grad = lax.all_to_all(head_grad, "fsdp", split_axis=0, concat_axis=0, tiled=True)
     run(sums, spread[1])
     head_grad = sums.tie(head_grad)

time: 805 us -> 791 us (0.983)
  waiting for transfers between devices: 177 us -> 160 us
  blocking collectives: 96.2 us -> 109 us
  Pallas kernels: 305 us -> 296 us
    all_to_all x1, blocking collectives: 52 us -> 64.8 us  [local(): lax.all_to_all(head_grad, 'fsdp', split_axis=0, concat_axis=0, tiled=True)]
    ppermute x16, waiting for transfers between devices: 146 us -> 134 us  [ring_hop(): lax.ppermute(x, 'fsdp', [(ring[i], ring[(i + step) % count]) for i in ran...]
    pallas_call x1, Pallas kernels: 87.8 us -> 78.3 us  [dense_sum(): pl.pallas_call(functools.partial(dense_sum_kernel, cut), out_shape=jax.Sh...]
    unnamed x147 -> x145, local copies, waits for them, and re-layouts: 16.7 us -> 17.9 us
  transfers between devices with their start and end apart: 22 -> 22, of which waited for: 9 -> 10; matrix products, arithmetic and copies ran while one was open for 11% -> 11% of each run, Pallas kernels for 32% -> 32%
where the time goes in v5:
time: 791 us; the launch traced here: 775 us
  Pallas kernels  296 us (37%)
  waiting for transfers between devices  160 us (20%)
  blocking collectives  109 us (14%)
  local copies, waits for them, and re-layouts  78.3 us (10%)
  starting transfers between devices  57.1 us (7%)
  matrix products  40.7 us (5%)
  other arithmetic  29.6 us (4%)
    ppermute x16, waiting for transfers between devices, ring_hop(): lax.ppermute(x, 'fsdp', [(ring[i], ring[(i + step) % count]) for i in ran...  134 us
    pallas_call x1, Pallas kernels, dense_sum(): pl.pallas_call(functools.partial(dense_sum_kernel, cut), out_shape=jax.Sh...  78.3 us
    all_to_all x1, blocking collectives, local(): lax.all_to_all(head_grad, 'fsdp', split_axis=0, concat_axis=0, tiled=True)  64.8 us
    pallas_call x1, Pallas kernels, dense_gather(): pl.pallas_call(functools.partial(dense_gather_kernel, cut), out_shape=jax...  51.4 us
    all_to_all x1, blocking collectives, local(): lax.all_to_all(head_att, 'fsdp', split_axis=0, concat_axis=0, tiled=True)  44.3 us
    pallas_call x1, Pallas kernels, attend_backward(): pl.pallas_call(functools.partial(attn_backward_kernel, sh), out_shape=(ja...  43.2 us
    pallas_call x1, Pallas kernels, ffn_backward(): pl.pallas_call(functools.partial(ffn_backward_kernel, count, ff_shard), g...  39.9 us
    pallas_call x1, Pallas kernels, ffn_forward(): pl.pallas_call(functools.partial(ffn_forward_kernel, count, ff_shard), gr...  34.7 us
  transfers between devices with their start and end apart: 22, of which 10 were waited for; matrix products, arithmetic and copies ran while one was open for 11% of the time, Pallas kernels for 32%

profile of v5, /device:TPU:0, one launch (start us, length us, event | category | flops | bytes accessed | tf_op | source)
XLA Modules:
  0.0 775.1 jit_solution(8562300137502848612)
XLA Ops:
  4.7 2.1 concatenate.49
  8.4 51.4 %dense_gather.1 = bf16[32,144,1024]{2,1,0:T(8,128)(2,1)} custom-call(bf16[144,1024]{1,0:T(8,128)(2,1)} %copy-done.33), custom_call_target="tpu_custom_call" | custom-call | bytes 100000000 | tf_op jit(solution)/shard_map/dense_gather/pallas_call | solution.py:769
  61.0 6.3 fusion.63
  70.9 5.6 fusion.7
  77.1 2.9 copy.55
  80.0 4.3 copy.56
  84.3 4.9 all-to-all-start
  91.7 84.0 %collective-permute-done.refs_8_ = bf16[1056,1024]{1,0:T(8,128)(2,1)} collective-permute-done((bf16[1056,1024]{1,0:T(8,128)(2,1)}, bf16[1056,1024]{1,0:T(8,128)(2,1)}, u32[]{:S(2)}, u32[]{:S(2)}) %collective-permute-start) | collective-permute-done | bytes 2162720 | tf_op jit(solution)/shard_map/ppermute | solution.py:526
  176.6 14.1 %collective-permute-start.2 = (bf16[1056,1024]{1,0:T(8,128)(2,1)}, bf16[1056,1024]{1,0:T(8,128)(2,1)}, u32[]{:S(2)}, u32[]{:S(2)}) collective-permute-start(bf16[1056,1024]{1,0:T(8,128)(2,1)} %collective-permute-done.refs_8_), channel_id=1, source_target_pairs={{0,2},{2,4},{4,6},{6,7},{7,5},{5,3},{3,1},{1,0},{8,10},{10,12},{12... | collective-permute-start | bytes 6488072 | tf_op jit(solution)/shard_map/ppermute | solution.py:526
  190.8 22.2 %attend_forward.1 = (bf16[8,384,128]{2,1,0:T(8,128)(2,1)S(1)}, f32[12,128,256]{2,1,0:T(8,128)S(1)}, f32[12,8,256]{2,1,0:T(8,128)S(1)}) custom-call(s32[8]{0:T(128)S(1)} %bitcast_convert_fusion.1.group_ref, f32[2,32]{1,0:T(2,128)S(1)} %bitcast_convert_fusion.table_ref, s32[9,128]{1,0:T(8,128)S(1)} %bitcast.102, bf16[8,384,384]{2,1,0:T(8,128)(2,1)S(1)} %all-to-all-done.x_ref), custom_call_target="tpu_custom_call" | custom-call | flops 10000000000 | bytes 8000000 | tf_op jit(solution)/shard_map/attend_forward/pallas_call | solution.py:465
  213.1 44.3 %all_to_all.40 = bf16[8,384,128]{2,1,0:T(8,128)(2,1)S(1)} all-to-all(bf16[8,384,128]{2,1,0:T(8,128)(2,1)S(1)} %get-tuple-element.56), channel_id=1, replica_groups=mesh['expert'=4,'fsdp'=8] {'fsdp'}, dimensions={0} | all-to-all | bytes 1572864 | tf_op jit(solution)/shard_map/all_to_all | solution.py:1292
  257.5 2.2 collective-permute-start.4
  263.8 3.0 multiply_reduce_fusion.2
  266.8 2.6 convolution_convert_fusion.3
  269.4 4.4 all-to-all-start.2
  275.6 29.8 %collective-permute-done.5.refs_6_ = bf16[1056,1024]{1,0:T(8,128)(2,1)} collective-permute-done((bf16[1056,1024]{1,0:T(8,128)(2,1)}, bf16[1056,1024]{1,0:T(8,128)(2,1)}, u32[]{:S(2)}, u32[]{:S(2)}) %collective-permute-start.5) | collective-permute-done | bytes 2162720 | tf_op jit(solution)/shard_map/ppermute | solution.py:526
  305.4 2.3 slice.248
  307.9 2.3 slice.249
  313.2 2.5 multiply_convert_fusion
  315.7 4.5 all-to-all-start.4
  320.1 11.3 %collective-permute-done.6.refs_4_ = bf16[528,1024]{1,0:T(8,128)(2,1)} collective-permute-done((bf16[528,1024]{1,0:T(8,128)(2,1)}, bf16[528,1024]{1,0:T(8,128)(2,1)}, u32[]{:S(2)}, u32[]{:S(2)}) %collective-permute-start.6) | collective-permute-done | bytes 1081376 | tf_op jit(solution)/shard_map/ppermute | solution.py:526
  331.5 2.6 collective-permute-done.7.refs_5_
  334.1 34.7 %ffn_forward.1 = (bf16[960,1024]{1,0:T(8,128)(2,1)}, f32[11,960,256]{2,1,0:T(8,128)}, f32[11,960,256]{2,1,0:T(8,128)}, bf16[11,960,256]{2,1,0:T(8,128)(2,1)}) custom-call(bf16[960,1024]{1,0:T(8,128)(2,1)} %bitcast.23.rows_ref, bf16[1056,1024]{1,0:T(8,128)(2,1)} %pad_maximum_fusion.3.refs_0_, bf16[1056,1024]{1,0:T(8,128)(2,1)} %collective-permute-done.1.refs_1_, ...), custom_call_target="tpu_custom_call" | custom-call | flops 16609443840 | bytes 40000000 | tf_op jit(solution)/shard_map/ffn_forward/pallas_call | solution.py:1126
  368.8 4.9 all-to-all-start.3
  373.7 39.9 %ffn_backward.1 = (bf16[960,1024]{1,0:T(8,128)(2,1)}, bf16[11,960,256]{2,1,0:T(8,128)(2,1)}, bf16[11,960,256]{2,1,0:T(8,128)(2,1)}) custom-call(bf16[960,1024]{1,0:T(8,128)(2,1)} %bitcast.34.grad_ref, f32[11,960,256]{2,1,0:T(8,128)} %get-tuple-element.63.act_ref, f32[11,960,256]{2,1,0:T(8,128)} %get-tuple-element.64.turn_ref, ...), custom_call_target="tpu_custom_call" | custom-call | flops 16609443840 | bytes 40000000 | tf_op jit(solution)/shard_map/ffn_backward/pallas_call | solution.py:1158
  413.7 4.4 all-to-all-start.5
  418.1 25.9 %ffn_weights.1 = (bf16[1056,1024]{1,0:T(8,128)(2,1)}, bf16[1056,1024]{1,0:T(8,128)(2,1)}, bf16[1056,1024]{1,0:T(8,128)(2,1)}, bf16[1056,1024]{1,0:T(8,128)(2,1)}...) custom-call(bf16[960,1024]{1,0:T(8,128)(2,1)} %bitcast.23.rows_ref, ...), custom_call_target="tpu_custom_call" | custom-call | flops 16609443840 | bytes 40000000 | tf_op jit(solution)/shard_map/ffn_weights/pallas_call | solution.py:1185
  446.1 2.3 slice.215
  449.5 2.6 fusion.15
  452.1 3.7 fusion.10
  455.8 2.6 fusion.25
  464.0 2.3 copy.62
  466.3 2.3 copy.63
  477.8 64.8 %all_to_all.41.do_ref = bf16[8,384,128]{2,1,0:T(8,128)(2,1)S(1)} all-to-all(bf16[8,384,128]{2,1,0:T(8,128)(2,1)S(1)} %bitcast.125), channel_id=1, replica_groups=mesh['expert'=4,'fsdp'=8] {'fsdp'}, dimensions={0} | all-to-all | bytes 1572864 | tf_op jit(solution)/shard_map/all_to_all | solution.py:1368
  546.9 43.2 %attend_backward.1 = (bf16[8,384,384]{2,1,0:T(8,128)(2,1)}, f32[64,128]{1,0:T(8,128)S(1)}) custom-call(s32[8]{0:T(128)S(1)} %bitcast_convert_fusion.1.group_ref, f32[2,32]{1,0:T(2,128)S(1)} %bitcast_convert_fusion.table_ref, s32[9,128]{1,0:T(8,128)S(1)} %bitcast.103, bf16[8,384,384]{2,1,0:T(8,128)(2,1)} %copy-done, ...), custom_call_target="tpu_custom_call" | custom-call | flops 20000000000 | bytes 12000000 | tf_op jit(solution)/shard_map/attend_backward/pallas_call | solution.py:490
  592.9 4.6 all-to-all-start.7
  612.1 2.6 convolution_convert_fusion.2
  615.0 7.9 %add_convert_fusion = (bf16[1056,1024]{1,0:T(8,128)(2,1)}, bf16[1056,1024]{1,0:T(8,128)(2,1)}) fusion(bf16[1056,1024]{1,0:T(8,128)(2,1)} %collective-permute-done.12, bf16[1056,1024]{1,0:T(8,128)(2,1)} %get-tuple-element.87, bf16[1056,1024]{1,0:T(8,128)(2,1)} %collective-permute-done.13, bf16[1056,1024]{1,0:T(8,128)(2,1)} %get-tuple-element.85), kind=kLoop, calls=%fused_computation.3 | loop fusion | flops 8650752 | bytes 12976128 | tf_op jit(solution)/shard_map/convert_element_type | solution.py:594
  622.8 26.6 %all-to-all-done.7 = bf16[8,384,384]{2,1,0:T(8,128)(2,1)} async-done(((bf16[8,384,384]{2,1,0:T(8,128)(2,1)}), bf16[8,384,384]{2,1,0:T(8,128)(2,1)}, u32[]{:S(2)}, u32[]{:S(2)}) %all-to-all-start.7) | async-done | bytes 2359328 | tf_op jit(solution)/shard_map/all_to_all | solution.py:1376
  649.4 4.3 copy.64
  653.7 2.2 copy.65
  656.8 5.3 fusion.9
  662.1 4.0 convolution_convert_fusion
  666.2 2.8 fusion.64
  677.1 2.1 reshape.313
  686.1 78.3 %dense_sum.1 = f32[144,1024]{1,0:T(8,128)S(1)} custom-call(bf16[32,144,1024]{2,1,0:T(8,128)(2,1)S(1)} %constant_dynamic-update-slice_fusion.2.g_ref), custom_call_target="tpu_custom_call" | custom-call | bytes 100000000 | tf_op jit(solution)/shard_map/dense_sum/pallas_call | solution.py:933
  769.2 3.3 convert_add_fusion
  772.4 2.2 slice_bitcast_fusion
  (281 shorter events, 81.6 us)
Async XLA Ops:
  70.6 193.2 %copy-start.8 = (bf16[128,2,1024]{2,0,1:T(8,128)(2,1)}, bf16[128,2,1024]{2,0,1:T(8,128)(2,1)S(1)}, u32[]{:S(2)}) copy-start(bf16[128,2,1024]{2,0,1:T(8,128)(2,1)S(1)} %copy.53) | copy-start | bytes 1572868
  84.3 106.5 %copy-start.1 = (s32[1152]{0:T(1024)S(1)}, s32[1152]{0:T(1024)}, u32[]{:S(2)}) copy-start(s32[1152]{0:T(1024)} %param.29) | copy-start | bytes 13828
  84.3 92.3 %all-to-all-start = ((bf16[8,384,384]{2,1,0:T(8,128)(2,1)}), bf16[8,384,384]{2,1,0:T(8,128)(2,1)S(1)}, u32[]{:S(2)}, u32[]{:S(2)}) async-start(bf16[8,384,384]{2,1,0:T(8,128)(2,1)} %copy.56), calls=%async_computation | async-start | bytes 4718592 | tf_op jit(solution)/shard_map/all_to_all | solution.py:1288
  89.2 86.5 %collective-permute-start = (bf16[1056,1024]{1,0:T(8,128)(2,1)}, bf16[1056,1024]{1,0:T(8,128)(2,1)}, u32[]{:S(2)}, u32[]{:S(2)}) collective-permute-start(bf16[1056,1024]{1,0:T(8,128)(2,1)} %pad_maximum_fusion.3.refs_0_), channel_id=1, source_target_pairs={{0,2},{2,4},{4,6},{6,7},{7,5},{5,3},{3,1},{1,0},{8,10},{10,12},{12... | collective-permute-start | bytes 6488072 | tf_op jit(solution)/shard_map/ppermute | solution.py:526
  91.2 85.4 %collective-permute-start.1 = (bf16[1056,1024]{1,0:T(8,128)(2,1)}, bf16[1056,1024]{1,0:T(8,128)(2,1)}, u32[]{:S(2)}, u32[]{:S(2)}) collective-permute-start(bf16[1056,1024]{1,0:T(8,128)(2,1)} %pad_maximum_fusion.3.refs_0_), channel_id=1, source_target_pairs={{0,1},{2,0},{4,2},{6,4},{7,6},{5,7},{3,5},{1,3},{8,9},{10,8},{12,1... | collective-permute-start | bytes 6488072 | tf_op jit(solution)/shard_map/ppermute | solution.py:526
  176.6 36.4 %copy-start = (bf16[8,384,384]{2,1,0:T(8,128)(2,1)}, bf16[8,384,384]{2,1,0:T(8,128)(2,1)S(1)}, u32[]{:S(2)}) copy-start(bf16[8,384,384]{2,1,0:T(8,128)(2,1)S(1)} %all-to-all-done.x_ref) | copy-start | bytes 7077892
  176.6 80.8 %collective-permute-start.2 = (bf16[1056,1024]{1,0:T(8,128)(2,1)}, bf16[1056,1024]{1,0:T(8,128)(2,1)}, u32[]{:S(2)}, u32[]{:S(2)}) collective-permute-start(bf16[1056,1024]{1,0:T(8,128)(2,1)} %collective-permute-done.refs_8_), channel_id=1, source_target_pairs={{0,2},{2,4},{4,6},{6,7},{7,5},{5,3},{3,1},{1,0},{8,10},{10,12},{12... | collective-permute-start | bytes 6488072 | tf_op jit(solution)/shard_map/ppermute | solution.py:526
  190.8 66.7 %collective-permute-start.3 = (bf16[1056,1024]{1,0:T(8,128)(2,1)}, bf16[1056,1024]{1,0:T(8,128)(2,1)}, u32[]{:S(2)}, u32[]{:S(2)}) collective-permute-start(bf16[1056,1024]{1,0:T(8,128)(2,1)} %collective-permute-done.1.refs_1_), channel_id=1, source_target_pairs={{0,1},{2,0},{4,2},{6,4},{7,6},{5,7},{3,5},{1,3},{8,9},{10,8},{12,1... | collective-permute-start | bytes 6488072 | tf_op jit(solution)/shard_map/ppermute | solution.py:526
  190.8 68.9 %copy-start.23 = (bf16[384,1024]{1,0:T(8,128)(2,1)S(1)}, bf16[384,1024]{1,0:T(8,128)(2,1)}, u32[]{:S(2)}) copy-start(bf16[384,1024]{1,0:T(8,128)(2,1)} %param.30) | copy-start | bytes 2359300
  213.0 44.4 %copy-start.2 = (f32[12,128,256]{2,1,0:T(8,128)}, f32[12,128,256]{2,1,0:T(8,128)S(1)}, u32[]{:S(2)}) copy-start(f32[12,128,256]{2,1,0:T(8,128)S(1)} %get-tuple-element.77.ot_ref) | copy-start | bytes 4718596
  213.1 47.4 %copy-start.60 = (s32[384,2]{0,1:T(2,128)S(1)}, s32[384,2]{0,1:T(2,128)}, u32[]{:S(2)}) copy-start(s32[384,2]{0,1:T(2,128)} %param.26) | copy-start | bytes 9220
  213.1 47.4 %copy-start.59 = (s32[384,2]{0,1:T(2,128)S(1)}, s32[384,2]{0,1:T(2,128)}, u32[]{:S(2)}) copy-start(s32[384,2]{0,1:T(2,128)} %param.27) | copy-start | bytes 9220
  213.1 47.4 %slice-start.2 = ((bf16[384,1024]{1,0:T(8,128)(2,1)}), bf16[256,1024]{1,0:T(8,128)(2,1)S(1)}, s32[]{:S(2)}) async-start(bf16[384,1024]{1,0:T(8,128)(2,1)} %param.30), calls=%async_computation.10 | async-start | bytes 1048576 | tf_op jit(solution)/shard_map/slice | solution.py:1232
  257.4 47.9 %collective-permute-start.5 = (bf16[1056,1024]{1,0:T(8,128)(2,1)}, bf16[1056,1024]{1,0:T(8,128)(2,1)}, u32[]{:S(2)}, u32[]{:S(2)}) collective-permute-start(bf16[1056,1024]{1,0:T(8,128)(2,1)} %collective-permute-done.2.refs_7_), channel_id=1, source_target_pairs={{0,2},{2,4},{4,6},{6,7},{7,5},{5,3},{3,1},{1,0},{8,10},{10,12},{12... | collective-permute-start | bytes 6488072 | tf_op jit(solution)/shard_map/ppermute | solution.py:526
  257.5 50.4 %collective-permute-start.4 = (bf16[1056,1024]{1,0:T(8,128)(2,1)}, bf16[1056,1024]{1,0:T(8,128)(2,1)}, u32[]{:S(2)}, u32[]{:S(2)}) collective-permute-start(bf16[1056,1024]{1,0:T(8,128)(2,1)} %collective-permute-done.3.refs_2_), channel_id=1, source_target_pairs={{0,1},{2,0},{4,2},{6,4},{7,6},{5,7},{3,5},{1,3},{8,9},{10,8},{12,1... | collective-permute-start | bytes 6488072 | tf_op jit(solution)/shard_map/ppermute | solution.py:526
  261.7 198.7 %copy-start.36 = (f32[1024]{0:T(1024)}, f32[1024]{0:T(1024)S(1)}, u32[]{:S(2)}) copy-start(f32[1024]{0:T(1024)S(1)} %reshape.324) | copy-start | bytes 12292
  263.4 48.6 %copy-start.50 = (s32[384]{0:T(512)}, s32[384]{0:T(512)S(1)}, u32[]{:S(2)}) copy-start(s32[384]{0:T(512)S(1)} %get-tuple-element.144) | copy-start | bytes 4612
  266.8 193.7 %copy-start.40 = (f32[384]{0:T(512)}, f32[384]{0:T(512)S(1)}, u32[]{:S(2)}) copy-start(f32[384]{0:T(512)S(1)} %fusion.54) | copy-start | bytes 4612
  269.4 46.2 %all-to-all-start.2 = ((bf16[4,240,1024]{2,1,0:T(8,128)(2,1)}), bf16[4,240,1024]{2,1,0:T(8,128)(2,1)}, u32[]{:S(2)}, u32[]{:S(2)}) async-start(bf16[4,240,1024]{2,1,0:T(8,128)(2,1)} %bitcast.139), calls=%async_computation.2 | async-start | bytes 3932160 | tf_op jit(solution)/shard_map/all_to_all | solution.py:1317
  274.9 183.7 %copy-start.34 = (f32[384,4]{0,1:T(4,128)}, f32[384,4]{0,1:T(4,128)S(1)}, u32[]{:S(2)}) copy-start(f32[384,4]{0,1:T(4,128)S(1)} %get-tuple-element.180) | copy-start | bytes 18436
  274.9 183.7 %copy-start.42 = (f32[384]{0:T(512)}, f32[384]{0:T(512)S(1)}, u32[]{:S(2)}) copy-start(f32[384]{0:T(512)S(1)} %is-finite_select_fusion) | copy-start | bytes 4612
  275.6 36.4 %copy-start.52 = (s32[384]{0:T(512)S(1)}, s32[384]{0:T(512)}, u32[]{:S(2)}) copy-start(s32[384]{0:T(512)} %get-tuple-element.145) | copy-start | bytes 4612
  275.6 36.6 %copy-start.54 = (s32[128,2]{0,1:T(2,128)S(1)}, s32[128,2]{0,1:T(2,128)}, u32[]{:S(2)}) copy-start(s32[128,2]{0,1:T(2,128)} %copy-done.53) | copy-start | bytes 3076
  275.6 36.6 %copy-start.62 = (s32[384]{0:T(512)S(1)}, s32[384]{0:T(512)}, u32[]{:S(2)}) copy-start(s32[384]{0:T(512)} %copy-done.61) | copy-start | bytes 4612
  275.6 36.6 %copy-start.64 = (s32[384]{0:T(512)S(1)}, s32[384]{0:T(512)}, u32[]{:S(2)}) copy-start(s32[384]{0:T(512)} %copy-done.63) | copy-start | bytes 4612
  275.6 37.6 %copy-start.24 = (bf16[128,2,1024]{2,0,1:T(8,128)(2,1)S(1)}, bf16[128,2,1024]{2,0,1:T(8,128)(2,1)}, u32[]{:S(2)}) copy-start(bf16[128,2,1024]{2,0,1:T(8,128)(2,1)} %copy.61) | copy-start | bytes 1572868
  275.6 37.6 %copy-start.28 = (bf16[128,1024]{1,0:T(8,128)(2,1)S(1)}, bf16[128,1024]{1,0:T(8,128)(2,1)}, u32[]{:S(2)}) copy-start(bf16[128,1024]{1,0:T(8,128)(2,1)} %slice.214) | copy-start | bytes 786436
  307.6 23.8 %collective-permute-start.6 = (bf16[528,1024]{1,0:T(8,128)(2,1)}, bf16[528,1024]{1,0:T(8,128)(2,1)}, u32[]{:S(2)}, u32[]{:S(2)}) collective-permute-start(bf16[528,1024]{1,0:T(8,128)(2,1)} %slice.248), channel_id=1, source_target_pairs={{0,2},{2,4},{4,6},{6,7},{7,5},{5,3},{3,1},{1,0},{8,10},{10,12},{12... | collective-permute-start | bytes 3244040 | tf_op jit(solution)/shard_map/ppermute | solution.py:526
  310.2 23.8 %collective-permute-start.7 = (bf16[528,1024]{1,0:T(8,128)(2,1)}, bf16[528,1024]{1,0:T(8,128)(2,1)}, u32[]{:S(2)}, u32[]{:S(2)}) collective-permute-start(bf16[528,1024]{1,0:T(8,128)(2,1)} %slice.249), channel_id=1, source_target_pairs={{0,1},{2,0},{4,2},{6,4},{7,6},{5,7},{3,5},{1,3},{8,9},{10,8},{12,1... | collective-permute-start | bytes 3244040 | tf_op jit(solution)/shard_map/ppermute | solution.py:526
  315.7 53.2 %all-to-all-start.4 = ((bf16[4,240,1024]{2,1,0:T(8,128)(2,1)}), bf16[4,240,1024]{2,1,0:T(8,128)(2,1)}, u32[]{:S(2)}, u32[]{:S(2)}) async-start(bf16[4,240,1024]{2,1,0:T(8,128)(2,1)} %bitcast.142), calls=%async_computation.4 | async-start | bytes 3932160 | tf_op jit(solution)/shard_map/all_to_all | solution.py:1317
  368.8 44.8 %all-to-all-start.3 = ((bf16[4,240,1024]{2,1,0:T(8,128)(2,1)}), bf16[4,240,1024]{2,1,0:T(8,128)(2,1)}, u32[]{:S(2)}, u32[]{:S(2)}) async-start(bf16[4,240,1024]{2,1,0:T(8,128)(2,1)} %bitcast.141), calls=%async_computation.3 | async-start | bytes 3932160 | tf_op jit(solution)/shard_map/all_to_all | solution.py:1317
  413.7 42.1 %all-to-all-start.5 = ((bf16[4,240,1024]{2,1,0:T(8,128)(2,1)}), bf16[4,240,1024]{2,1,0:T(8,128)(2,1)}, u32[]{:S(2)}, u32[]{:S(2)}) async-start(bf16[4,240,1024]{2,1,0:T(8,128)(2,1)} %bitcast.140), calls=%async_computation.5 | async-start | bytes 3932160 | tf_op jit(solution)/shard_map/all_to_all | solution.py:1317
  444.1 26.6 %collective-permute-start.8 = (bf16[528,1024]{1,0:T(8,128)(2,1)}, bf16[528,1024]{1,0:T(8,128)(2,1)}, u32[]{:S(2)}, u32[]{:S(2)}) collective-permute-start(bf16[528,1024]{1,0:T(8,128)(2,1)} %get-tuple-element.69), channel_id=1, source_target_pairs={{0,2},{2,4},{4,6},{6,7},{7,5},{5,3},{3,1},{1,0},{8,10},{10,12},{12... | collective-permute-start | bytes 3244040 | tf_op jit(solution)/shard_map/ppermute | solution.py:526
  444.7 26.3 %collective-permute-start.9 = (bf16[528,1024]{1,0:T(8,128)(2,1)}, bf16[528,1024]{1,0:T(8,128)(2,1)}, u32[]{:S(2)}, u32[]{:S(2)}) collective-permute-start(bf16[528,1024]{1,0:T(8,128)(2,1)} %get-tuple-element.70), channel_id=1, source_target_pairs={{0,1},{2,0},{4,2},{6,4},{7,6},{5,7},{3,5},{1,3},{8,9},{10,8},{12,1... | collective-permute-start | bytes 3244040 | tf_op jit(solution)/shard_map/ppermute | solution.py:526
  473.1 69.5 %collective-permute-start.10 = (bf16[1056,1024]{1,0:T(8,128)(2,1)S(1)}, bf16[1056,1024]{1,0:T(8,128)(2,1)S(1)}, u32[]{:S(2)}, u32[]{:S(2)}) collective-permute-start(bf16[1056,1024]{1,0:T(8,128)(2,1)S(1)} %pad_maximum_fusion.4), channel_id=1, source_target_pairs={{0,2},{2,4},{4,6},{6,7},{7,5},{5,3},{3,1},{1,0},{8,10},{10,12},{12... | collective-permute-start | bytes 6488072 | tf_op jit(solution)/shard_map/ppermute | solution.py:526
  476.7 66.0 %copy-start.18 = (bf16[1056,1024]{1,0:T(8,128)(2,1)S(1)}, bf16[1056,1024]{1,0:T(8,128)(2,1)}, u32[]{:S(2)}) copy-start(bf16[1056,1024]{1,0:T(8,128)(2,1)} %get-tuple-element.80) | copy-start | bytes 6488068
  476.9 65.8 %collective-permute-start.11 = (bf16[1056,1024]{1,0:T(8,128)(2,1)S(1)}, bf16[1056,1024]{1,0:T(8,128)(2,1)S(1)}, u32[]{:S(2)}, u32[]{:S(2)}) collective-permute-start(bf16[1056,1024]{1,0:T(8,128)(2,1)S(1)} %pad_maximum_fusion.5), channel_id=1, source_target_pairs={{0,1},{2,0},{4,2},{6,4},{7,6},{5,7},{3,5},{1,3},{8,9},{10,8},{12,1... | collective-permute-start | bytes 6488072 | tf_op jit(solution)/shard_map/ppermute | solution.py:526
  543.7 47.6 %collective-permute-start.12 = (bf16[1056,1024]{1,0:T(8,128)(2,1)S(1)}, bf16[1056,1024]{1,0:T(8,128)(2,1)}, u32[]{:S(2)}, u32[]{:S(2)}) collective-permute-start(bf16[1056,1024]{1,0:T(8,128)(2,1)S(1)} %add_convert_fusion.3), channel_id=1, source_target_pairs={{0,2},{2,4},{4,6},{6,7},{7,5},{5,3},{3,1},{1,0},{8,10},{10,12},{12... | collective-permute-start | bytes 6488072 | tf_op jit(solution)/shard_map/ppermute | solution.py:526
  545.3 47.6 %collective-permute-start.13 = (bf16[1056,1024]{1,0:T(8,128)(2,1)S(1)}, bf16[1056,1024]{1,0:T(8,128)(2,1)}, u32[]{:S(2)}, u32[]{:S(2)}) collective-permute-start(bf16[1056,1024]{1,0:T(8,128)(2,1)S(1)} %add_convert_fusion.2), channel_id=1, source_target_pairs={{0,1},{2,0},{4,2},{6,4},{7,6},{5,7},{3,5},{1,3},{8,9},{10,8},{12,1... | collective-permute-start | bytes 6488072 | tf_op jit(solution)/shard_map/ppermute | solution.py:526
  592.9 56.5 %all-to-all-start.7 = ((bf16[8,384,384]{2,1,0:T(8,128)(2,1)}), bf16[8,384,384]{2,1,0:T(8,128)(2,1)}, u32[]{:S(2)}, u32[]{:S(2)}) async-start(bf16[8,384,384]{2,1,0:T(8,128)(2,1)} %get-tuple-element.84), calls=%async_computation.7 | async-start | bytes 4718592 | tf_op jit(solution)/shard_map/all_to_all | solution.py:1376
  597.5 8.7 %copy-start.35 = (f32[384,4]{0,1:T(4,128)S(1)}, f32[384,4]{0,1:T(4,128)}, u32[]{:S(2)}) copy-start(f32[384,4]{0,1:T(4,128)} %copy-done.34) | copy-start | bytes 18436
  597.5 8.7 %copy-start.37 = (f32[1024]{0:T(1024)S(1)}, f32[1024]{0:T(1024)}, u32[]{:S(2)}) copy-start(f32[1024]{0:T(1024)} %copy-done.36) | copy-start | bytes 12292
  597.5 8.7 %copy-start.39 = (f32[384,4]{0,1:T(4,128)S(1)}, f32[384,4]{0,1:T(4,128)}, u32[]{:S(2)}) copy-start(f32[384,4]{0,1:T(4,128)} %copy-done.38) | copy-start | bytes 18436
  597.5 8.7 %copy-start.41 = (f32[384]{0:T(512)S(1)}, f32[384]{0:T(512)}, u32[]{:S(2)}) copy-start(f32[384]{0:T(512)} %copy-done.40) | copy-start | bytes 4612
  597.5 8.7 %copy-start.43 = (f32[384]{0:T(512)S(1)}, f32[384]{0:T(512)}, u32[]{:S(2)}) copy-start(f32[384]{0:T(512)} %copy-done.42) | copy-start | bytes 4612
  669.1 100.1 %collective-permute-start.15 = (bf16[1056,1024]{1,0:T(8,128)(2,1)}, bf16[1056,1024]{1,0:T(8,128)(2,1)}, u32[]{:S(2)}, u32[]{:S(2)}) collective-permute-start(bf16[1056,1024]{1,0:T(8,128)(2,1)} %get-tuple-element.93), channel_id=1, source_target_pairs={{0,1},{2,0},{4,2},{6,4},{7,6},{5,7},{3,5},{1,3},{8,9},{10,8},{12,1... | collective-permute-start | bytes 6488072 | tf_op jit(solution)/shard_map/ppermute | solution.py:526
  670.5 98.7 %collective-permute-start.14 = (bf16[1056,1024]{1,0:T(8,128)(2,1)}, bf16[1056,1024]{1,0:T(8,128)(2,1)}, u32[]{:S(2)}, u32[]{:S(2)}) collective-permute-start(bf16[1056,1024]{1,0:T(8,128)(2,1)} %get-tuple-element.92), channel_id=1, source_target_pairs={{0,2},{2,4},{4,6},{6,7},{7,5},{5,3},{3,1},{1,0},{8,10},{10,12},{12... | collective-permute-start | bytes 6488072 | tf_op jit(solution)/shard_map/ppermute | solution.py:526
  686.1 79.2 %slice-start = ((f32[384,1024]{1,0:T(8,128)}), f32[128,1024]{1,0:T(8,128)S(1)}, s32[]{:S(2)}) async-start(f32[384,1024]{1,0:T(8,128)} %copy-done.13), calls=%async_computation.8 | async-start | bytes 1048576 | tf_op jit(solution)/shard_map/slice | solution.py:1237
  (45 other events, 146.9 us)
